TPU v7x, 32 devices: a whole 2x2x4 slice. The times are simulated.
32 devices in a mesh: dp: 8 (over z, y), upd: 4 (over x, core).
Axes of the slice: x: 2, y: 2, z: 4, core: 2. Of those that a mesh axis runs over, the one named last changes fastest.
Arguments:
- inputs: bfloat16 [256, 128, 768], P(('dp', 'upd')), may hold values from -6 to 6
- memory: bfloat16 [256, 256, 768], P(('dp', 'upd')), may hold values from -6 to 6
- cotangent: bfloat16 [256, 128, 768], P(('dp', 'upd')), may hold values from -6 to 6
- lengths: int32 [256], P(('dp', 'upd')), may hold values from 1 to 128, as said below
- memory_len: int32 [256], P(('dp', 'upd')), may hold values from 64 to 225, as said below
- square_master: float32 [8, 768, 768], P(None, ('dp', 'upd')), may hold values from -0.21875 to 0.21875
- tall_master: float32 [2, 3072, 768], P(None, ('dp', 'upd'))
- square_momentum: float32 [8, 768, 768], P(None, ('dp', 'upd'))
- tall_momentum: float32 [2, 3072, 768], P(None, ('dp', 'upd'))
- vectors: bfloat16 [17, 768], replicated, may hold values from -1.5 to 1.5
- feed_vectors: bfloat16 [3, 3072], replicated, may hold values from -1.5 to 1.5
- head_scale: bfloat16 [12], replicated, may hold values from 0.25 to 1.75
- relative: bfloat16 [12, 128], replicated, may hold values from -4 to 4
Outputs:
- output: bfloat16 [256, 128, 768], P(('dp', 'upd'))
- input_gradient: bfloat16 [256, 128, 768], P(('dp', 'upd'))
- memory_gradient: bfloat16 [256, 256, 768], P(('dp', 'upd'))
- square_state: float32 [8, 768, 768], P(None, ('dp', 'upd'))
- tall_state: float32 [2, 3072, 768], P(None, ('dp', 'upd'))
- square_weight: float32 [8, 768, 768], P(None, ('dp', 'upd'))
- tall_weight: float32 [2, 3072, 768], P(None, ('dp', 'upd'))
- vector_gradient: float32 [17, 768], P(None, ('dp', 'upd'))
- feed_gradient: float32 [3, 3072], P(None, ('dp', 'upd'))
- scale_gradient: float32 [12], replicated
- bias_gradient: float32 [12, 128], replicated
Inputs may be any that keep to these rules, and one draw needn't show every extreme that they name: `lengths`: positions at or past an item's count are padding; some item has exactly 128. `memory_len`: each item has 64 or 225 real memory rows, the first ones; both occur.
All inputs are finite; a program needn't handle non-finite values.
Results may differ from a plain program's by a relative error of at most 0.02.
Values may be sent and summed in bfloat16 or wider, within the bound.
A program may use at most 384 MiB of HBM per device.

v0:
```python
import jax
import jax.numpy as jnp
from jax import lax
from jax.sharding import PartitionSpec as P

D = 768
FF = 3072
ITERS = 5


NORM_EPSILON = 1e-05
FLOOR_EPSILON = 1e-07
FIRST_TERM = 3.4445
SECOND_TERM = -4.775
THIRD_TERM = 2.0315
MOMENTUM_DECAY = 0.95
LEARN_RATE = 0.8
WEIGHT_DECAY = 0.01
NEGATIVE_LARGE = -1e30


def plain_round(values):
    return lax.optimization_barrier(values.astype(jnp.bfloat16)).astype(jnp.float32)


def same_value(values):
    return values


def value_keep(values):
    return (plain_round(values), None)


def value_pass(kept, slope):
    return (slope,)


def gradient_keep(values):
    return (values, None)


def gradient_round(kept, slope):
    return (plain_round(slope),)


def round_value(values):
    wrapped = jax.custom_vjp(plain_round)
    wrapped.defvjp(value_keep, value_pass)
    return wrapped(values)


def round_gradient(values):
    wrapped = jax.custom_vjp(same_value)
    wrapped.defvjp(gradient_keep, gradient_round)
    return wrapped(values)


def norm_rows(values, gain, shift):
    center = values - jnp.mean(values, axis=-1, keepdims=True)
    spread = jnp.mean(center * center, axis=-1, keepdims=True)
    return center * lax.rsqrt(spread + NORM_EPSILON) * gain + shift


def attend(query, keys, values, allowed, bias):
    scores = jnp.einsum("bqhe,bkhe->bhqk", query, keys) + bias
    scores = jnp.where(allowed, round_gradient(scores), NEGATIVE_LARGE)
    weights = jnp.exp(scores - jnp.max(scores, axis=-1, keepdims=True))
    weights = round_value(weights / jnp.sum(weights, axis=-1, keepdims=True))
    return round_gradient(jnp.einsum("bhqk,bkhe->bqhe", weights, values))


def split_heads(values, head_count):
    return values.reshape(
        values.shape[0], values.shape[1], head_count, values.shape[2] // head_count
    )


def layer_block(
    inputs, memory, memory_len, square, tall, vectors, feed_vectors, head_scale, relative
):
    item_count, query_count, model_width = inputs.shape
    head_count = head_scale.shape[0]
    memory_slots = memory.shape[1]
    normed = round_value(norm_rows(inputs, vectors[0], vectors[1]))
    query = round_gradient(round_value((jnp.matmul(normed, square[0]) + vectors[2]) * 0.125))
    keys = round_gradient(round_value(jnp.matmul(normed, square[1])))
    values = round_gradient(round_value(jnp.matmul(normed, square[2]) + vectors[3]))
    query_index = jnp.arange(query_count)[:, None]
    key_index = jnp.arange(query_count)[None, :]
    distance = jnp.clip(query_index - key_index, 0, query_count - 1)
    position_table = (distance[:, :, None] == jnp.arange(query_count)[None, None, :]).astype(
        jnp.float32
    )
    bias = jnp.einsum("hd,qkd->hqk", relative, position_table)[None]
    mixed = attend(
        split_heads(query, head_count),
        split_heads(keys, head_count),
        split_heads(values, head_count),
        (query_index >= key_index)[None, None],
        bias,
    )
    mixed = (mixed * head_scale[None, None, :, None]).reshape(item_count, query_count, model_width)
    mixed = round_value(norm_rows(mixed, vectors[5], vectors[6]))
    hidden = inputs + round_gradient(jnp.matmul(mixed, square[3]) + vectors[4])
    normed = round_value(norm_rows(hidden, vectors[7], vectors[8]))
    query = round_gradient(round_value((jnp.matmul(normed, square[4]) + vectors[9]) * 0.125))
    keys = round_gradient(round_value(jnp.matmul(memory, square[5])))
    values = round_gradient(round_value(jnp.matmul(memory, square[6]) + vectors[10]))
    allowed = (jnp.arange(memory_slots)[None, :] < memory_len[:, None])[:, None, None, :]
    mixed = attend(
        split_heads(query, head_count),
        split_heads(keys, head_count),
        split_heads(values, head_count),
        allowed,
        0.0,
    )
    mixed = round_value(
        norm_rows(mixed.reshape(item_count, query_count, model_width), vectors[12], vectors[13])
    )
    hidden = hidden + round_gradient(jnp.matmul(mixed, square[7]) + vectors[11])
    normed = round_value(norm_rows(hidden, vectors[14], vectors[15]))
    inner = round_gradient(jnp.matmul(normed, tall[0].T) + feed_vectors[0])
    active = round_value(
        norm_rows(jax.nn.gelu(inner, approximate=False), feed_vectors[1], feed_vectors[2])
    )
    return hidden + round_gradient(jnp.matmul(active, tall[1]) + vectors[16])


def gram_of(block):
    return jnp.einsum("wrd,wre->wde", block, block, precision=lax.Precision.HIGHEST)


def advance(current, gram):
    mixed = jnp.einsum("wrd,wde->wre", current, gram, precision=lax.Precision.HIGHEST)
    second = jnp.einsum("wrd,wde->wre", mixed, gram, precision=lax.Precision.HIGHEST)
    return FIRST_TERM * current + SECOND_TERM * mixed + THIRD_TERM * second


def both_grams(square, tall):
    joined = jnp.concatenate([gram_of(square), gram_of(tall)], axis=0)
    summed = lax.all_gather(
        lax.psum_scatter(joined, ("dp", "upd"), scatter_dimension=1, tiled=True).astype(
            jnp.bfloat16
        ),
        ("dp", "upd"),
        axis=1,
        tiled=True,
    ).astype(jnp.float32)
    return (summed[:8], summed[8:])


def shared_rows(square_state, tall_state):
    square_squares, tall_squares = lax.psum(
        (
            jnp.sum(square_state * square_state, axis=(1, 2)),
            jnp.sum(tall_state * tall_state, axis=(1, 2)),
        ),
        ("dp", "upd"),
    )
    square = square_state * (1.0 / (jnp.sqrt(square_squares) + FLOOR_EPSILON))[:, None, None]
    tall = tall_state * (1.0 / (jnp.sqrt(tall_squares) + FLOOR_EPSILON))[:, None, None]
    first_sweep = 0
    for sweep in range(first_sweep, ITERS):
        square_gram, tall_gram = both_grams(square, tall)
        square = advance(square, square_gram)
        tall = advance(tall, tall_gram)
    return (square, tall)


def local(
    inputs,
    memory,
    cotangent,
    lengths,
    memory_len,
    square_master,
    tall_master,
    square_momentum,
    tall_momentum,
    vectors,
    feed_vectors,
    head_scale,
    relative,
):
    square_copy, tall_copy = (
        lax.all_gather(square_master.astype(jnp.bfloat16), ("dp", "upd"), axis=1, tiled=True),
        lax.all_gather(tall_master.astype(jnp.bfloat16), ("dp", "upd"), axis=1, tiled=True),
    )
    params = (
        square_copy.astype(jnp.float32),
        tall_copy.astype(jnp.float32),
        vectors.astype(jnp.float32),
        feed_vectors.astype(jnp.float32),
        head_scale.astype(jnp.float32),
        relative.astype(jnp.float32),
    )

    def forward(params, inputs_full, memory_full):
        return layer_block(inputs_full, memory_full, memory_len, *params)

    output, pullback = jax.vjp(
        forward, params, inputs.astype(jnp.float32), memory.astype(jnp.float32)
    )
    valid = (jnp.arange(inputs.shape[1])[None, :] < lengths[:, None]).astype(jnp.float32)
    param_slopes, input_slope, memory_slope = pullback(
        cotangent.astype(jnp.float32) * valid[:, :, None]
    )
    square_slope, tall_slope, vector_slope, feed_slope, scale_slope, bias_slope = param_slopes
    total, scale_sum, bias_sum = lax.psum(
        (jnp.sum(lengths).astype(jnp.float32), scale_slope, bias_slope), ("dp", "upd")
    )
    square_sum, tall_sum, vector_sum, feed_sum = (
        lax.psum_scatter(square_slope, ("dp", "upd"), scatter_dimension=1, tiled=True),
        lax.psum_scatter(tall_slope, ("dp", "upd"), scatter_dimension=1, tiled=True),
        lax.psum_scatter(vector_slope, ("dp", "upd"), scatter_dimension=1, tiled=True),
        lax.psum_scatter(feed_slope, ("dp", "upd"), scatter_dimension=1, tiled=True),
    )
    factor = inputs.shape[0] * lax.axis_size("dp") * lax.axis_size("upd") / total
    square_state = MOMENTUM_DECAY * square_momentum + factor * square_sum
    tall_state = MOMENTUM_DECAY * tall_momentum + factor * tall_sum
    square, tall = shared_rows(square_state, tall_state)
    square_weight = square_master * (1.0 - LEARN_RATE * WEIGHT_DECAY) - LEARN_RATE * square
    tall_weight = (
        tall_master * (1.0 - LEARN_RATE * WEIGHT_DECAY)
        - LEARN_RATE * max(1.0, FF / D) ** 0.5 * tall
    )
    return (
        output.astype(jnp.bfloat16),
        input_slope.astype(jnp.bfloat16),
        memory_slope.astype(jnp.bfloat16),
        square_state,
        tall_state,
        square_weight,
        tall_weight,
        factor * vector_sum,
        factor * feed_sum,
        factor * scale_sum,
        factor * bias_sum,
    )


def solution(mesh):
    placed = (
        P(("dp", "upd"), None, None),
        P(("dp", "upd"), None, None),
        P(("dp", "upd"), None, None),
        P(("dp", "upd")),
        P(("dp", "upd")),
        P(None, ("dp", "upd"), None),
        P(None, ("dp", "upd"), None),
        P(None, ("dp", "upd"), None),
        P(None, ("dp", "upd"), None),
        P(),
        P(),
        P(),
        P(),
    )
    return jax.shard_map(
        local,
        mesh=mesh,
        in_specs=placed,
        out_specs=(
            P(("dp", "upd"), None, None),
            P(("dp", "upd"), None, None),
            P(("dp", "upd"), None, None),
            P(None, ("dp", "upd"), None),
            P(None, ("dp", "upd"), None),
            P(None, ("dp", "upd"), None),
            P(None, ("dp", "upd"), None),
            P(None, ("dp", "upd")),
            P(None, ("dp", "upd")),
            P(),
            P(),
        ),
        check_vma=False,
    )
```

profile of v0, /device:TPU:0, one launch (start us, length us, event | category | flops | bytes accessed | tf_op | source)
XLA Modules:
  0.0 2761.8 jit_solution(14452595280854810627)
XLA Ops:
  28.9 67.6 %all-gather.8.cloned.1.call-done = bf16[8,768,768]{2,1,0:T(8,128)(2,1)} async-done(((bf16[8,24,768]{2,1,0:T(8,128)(2,1)}), bf16[8,768,768]{2,1,0:T(8,128)(2,1)}) %all-gather.8.cloned.1.call-update) | async-done | bytes 9437200 | tf_op jit(solution)/shard_map/all_gather | solution.py:186
  212.7 13.1 fusion.59
  225.8 35.1 %fusion.208 = (f32[8,128]{1,0:T(8,128)S(1)}, f32[8,128,3072]{2,1,0:T(8,128)S(1)}, f32[8,128,3072]{2,1,0:T(8,128)}) fusion(f32[8,128,3072]{2,1,0:T(8,128)} %get-tuple-element.100, f32[3072]{0:T(1024)S(1)} %bitcast.312, u8[128,3072]{1,0:T(8,128)(4,1)S(1)} %get-tuple-element.14, u8[128,3072]{1,0:T(8,128)(4,1)S(1)} %get-tuple-element.13), kind=kLoop, calls=%fused_computation.340 | loop fusion | flops 223345664 | bytes 38551552 | tf_op jit(solution)/shard_map/jvp()/reduce_sum | solution.py:59
  260.9 12.0 multiply_reduce_fusion.2
  281.2 19.7 add_convert_fusion
  300.8 8.5 convolution_bitcast_fusion
  309.4 8.7 multiply_reduce_fusion.8
  351.3 12.2 multiply_reduce_fusion.1
  363.5 11.4 convert_reduce_fusion.1
  375.0 10.1 select_convert_fusion
  473.3 42.2 %psum.35 = f32[]{:T(128)} all-reduce(f32[]{:T(128)S(6)} %convert_element_type.296), channel_id=1, replica_groups=mesh['dp'=8,'upd'=4] {'dp','upd'}, use_global_device_ids=true, to_apply=%region_35.36 | all-reduce | flops 1 | bytes 8 | tf_op jit(solution)/shard_map/psum | solution.py:209
  549.2 200.3 %reduce-scatter.12.cloned.1.call-done = f32[8,24,768]{2,1,0:T(8,128)} async-done(((f32[8,768,768]{2,1,0:T(8,128)}), f32[8,24,768]{2,1,0:T(8,128)}) %reduce-scatter.12.cloned.1.call-update) | async-done | bytes 589840 | tf_op jit(solution)/shard_map/reduce_scatter | solution.py:213
  750.7 40.5 %all-reduce.31 = (f32[2]{0:T(128)S(1)}, f32[8]{0:T(128)S(1)}, f32[17,768]{1,0:T(8,128)}, f32[12]{0:T(128)}, f32[12,128]{1,0:T(8,128)}) all-reduce(f32[2]{0:T(128)S(1)} %get-tuple-element.61, f32[8]{0:T(128)S(1)} %get-tuple-element.59, f32[17,768]{1,0:T(8,128)S(1)} %pad_add_fusion.2, ...), channel_id=1, replica_groups=mesh['dp'=8,'upd'=4] {'dp','upd'}, use_global_device_ids=true, to_apply=%region_41.42 | all-reduce | flops 14614 | bytes 116912 | tf_op jit(solution)/shard_map/psum | solution.py:153
  791.2 15.9 fusion.177
  811.3 8.2 pad_maximum_fusion
  819.6 231.2 %reduce-scatter.16.cloned.1.call-done = f32[10,24,768]{2,1,0:T(8,128)} async-done(((f32[10,768,768]{2,1,0:T(8,128)}), f32[10,24,768]{2,1,0:T(8,128)}) %reduce-scatter.16.cloned.1.call-update) | async-done | bytes 737296 | tf_op jit(solution)/shard_map/reduce_scatter | solution.py:142
  1052.7 93.8 %all-gather.12.cloned.1.call-done = bf16[10,768,768]{2,1,0:T(8,128)(2,1)} async-done(((bf16[10,24,768]{2,1,0:T(8,128)(2,1)}), bf16[10,768,768]{2,1,0:T(8,128)(2,1)}) %all-gather.12.cloned.1.call-update) | async-done | bytes 11796496 | tf_op jit(solution)/shard_map/all_gather | solution.py:141
  1159.6 15.6 fusion.214
  1185.2 8.2 pad_maximum_fusion.1
  1193.5 229.9 %reduce-scatter.18.cloned.1.call-done = f32[10,24,768]{2,1,0:T(8,128)} async-done(((f32[10,768,768]{2,1,0:T(8,128)}), f32[10,24,768]{2,1,0:T(8,128)}) %reduce-scatter.18.cloned.1.call-update) | async-done | bytes 737296 | tf_op jit(solution)/shard_map/reduce_scatter | solution.py:142
  1425.3 93.5 %all-gather.14.cloned.1.call-done = bf16[10,768,768]{2,1,0:T(8,128)(2,1)} async-done(((bf16[10,24,768]{2,1,0:T(8,128)(2,1)}), bf16[10,768,768]{2,1,0:T(8,128)(2,1)}) %all-gather.14.cloned.1.call-update) | async-done | bytes 11796496 | tf_op jit(solution)/shard_map/all_gather | solution.py:141
  1531.8 15.6 fusion.216
  1557.2 8.2 pad_maximum_fusion.2
  1565.5 229.9 %reduce-scatter.20.cloned.1.call-done = f32[10,24,768]{2,1,0:T(8,128)} async-done(((f32[10,768,768]{2,1,0:T(8,128)}), f32[10,24,768]{2,1,0:T(8,128)}) %reduce-scatter.20.cloned.1.call-update) | async-done | bytes 737296 | tf_op jit(solution)/shard_map/reduce_scatter | solution.py:142
  1797.4 93.8 %all-gather.16.cloned.1.call-done = bf16[10,768,768]{2,1,0:T(8,128)(2,1)} async-done(((bf16[10,24,768]{2,1,0:T(8,128)(2,1)}), bf16[10,768,768]{2,1,0:T(8,128)(2,1)}) %all-gather.16.cloned.1.call-update) | async-done | bytes 11796496 | tf_op jit(solution)/shard_map/all_gather | solution.py:141
  1904.2 15.6 fusion.218
  1937.9 229.9 %reduce-scatter.22.cloned.1.call-done = f32[10,24,768]{2,1,0:T(8,128)} async-done(((f32[10,768,768]{2,1,0:T(8,128)}), f32[10,24,768]{2,1,0:T(8,128)}) %reduce-scatter.22.cloned.1.call-update) | async-done | bytes 737296 | tf_op jit(solution)/shard_map/reduce_scatter | solution.py:142
  2169.8 93.4 %all-gather.18.cloned.1.call-done = bf16[10,768,768]{2,1,0:T(8,128)(2,1)} async-done(((bf16[10,24,768]{2,1,0:T(8,128)(2,1)}), bf16[10,768,768]{2,1,0:T(8,128)(2,1)}) %all-gather.18.cloned.1.call-update) | async-done | bytes 11796496 | tf_op jit(solution)/shard_map/all_gather | solution.py:141
  2276.2 15.6 fusion.220
  2315.5 224.5 %reduce-scatter.24.cloned.1.call-done = f32[10,24,768]{2,1,0:T(8,128)} async-done(((f32[10,768,768]{2,1,0:T(8,128)}), f32[10,24,768]{2,1,0:T(8,128)}) %reduce-scatter.24.cloned.1.call-update) | async-done | bytes 737296 | tf_op jit(solution)/shard_map/reduce_scatter | solution.py:142
  2562.8 79.6 %reduce-scatter.26.cloned.1.call-done = f32[96,3]{1,0:T(8,128)} async-done(((f32[3072,3]{1,0:T(8,128)}), f32[96,3]{1,0:T(8,128)}) %reduce-scatter.26.cloned.1.call-update) | async-done | bytes 1168
  2646.3 90.7 %all-gather.20.cloned.1.call-done = bf16[10,768,768]{2,1,0:T(8,128)(2,1)} async-done(((bf16[10,24,768]{2,1,0:T(8,128)(2,1)}), bf16[10,768,768]{2,1,0:T(8,128)(2,1)}) %all-gather.20.cloned.1.call-update) | async-done | bytes 11796496 | tf_op jit(solution)/shard_map/all_gather | solution.py:141
  (512 shorter events, 469.7 us)
Async XLA Ops:
  7.2 147.8 %copy-start = (bf16[8,256,768]{2,1,0:T(8,128)(2,1)S(1)}, bf16[8,256,768]{2,1,0:T(8,128)(2,1)}, u32[]{:S(2)}) copy-start(bf16[8,256,768]{2,1,0:T(8,128)(2,1)} %param.14) | copy-start | bytes 9437188
  7.2 89.2 %all-gather.8.cloned.1.call-start = ((), (), s32[]{:S(2)}) async-start(), calls=%async_computation.8 | async-start | bytes 9732096 | tf_op jit(solution)/shard_map/all_gather | solution.py:186
  9.2 203.5 %all-gather.10.cloned.1.call-start = ((), (), s32[]{:S(2)}) async-start(), calls=%async_computation.9 | async-start | bytes 9732096 | tf_op jit(solution)/shard_map/all_gather | solution.py:187
  11.1 536.8 %reduce-scatter.14.cloned.1.call-start = ((), (), s32[]{:S(2)}) async-start(), calls=%async_computation.11 | async-start | bytes 19464192 | tf_op jit(solution)/shard_map/reduce_scatter | solution.py:214
  12.7 128.4 %copy-start.98 = (f32[768]{0:T(1024)}, f32[768]{0:T(1024)S(1)}, u32[]{:S(2)}) copy-start(f32[768]{0:T(1024)S(1)} %get-tuple-element.49) | copy-start | bytes 9220
  12.7 133.3 %copy-start.100 = (f32[768]{0:T(1024)}, f32[768]{0:T(1024)S(1)}, u32[]{:S(2)}) copy-start(f32[768]{0:T(1024)S(1)} %get-tuple-element.45) | copy-start | bytes 9220
  25.7 102.8 %copy-start.119 = (f32[12]{0:T(128)}, f32[12]{0:T(128)S(1)}, u32[]{:S(2)}) copy-start(f32[12]{0:T(128)S(1)} %convert_element_type.248) | copy-start | bytes 148
  333.8 415.6 %reduce-scatter.12.cloned.1.call-start = ((), (), s32[]{:S(2)}) async-start(), calls=%async_computation.10 | async-start | bytes 19464192 | tf_op jit(solution)/shard_map/reduce_scatter | solution.py:213
  471.4 579.4 %reduce-scatter.16.cloned.1.call-start = ((), (), s32[]{:S(2)}) async-start(), calls=%async_computation.12 | async-start | bytes 24330240 | tf_op jit(solution)/shard_map/reduce_scatter | solution.py:142
  540.6 208.9 %copy-start.77 = (f32[8,24,768]{2,1,0:T(8,128)S(1)}, f32[8,24,768]{2,1,0:T(8,128)}, u32[]{:S(2)}) copy-start(f32[8,24,768]{2,1,0:T(8,128)} %param.20) | copy-start | bytes 1769476
  541.9 208.8 %copy-start.121 = (f32[12]{0:T(128)S(1)}, f32[12]{0:T(128)}, u32[]{:S(2)}) copy-start(f32[12]{0:T(128)} %get-tuple-element.82) | copy-start | bytes 148
  549.2 629.0 %copy-start.42 = (f32[2,96,768]{2,1,0:T(8,128)}, f32[2,96,768]{2,1,0:T(8,128)S(1)}, u32[]{:S(2)}) copy-start(f32[2,96,768]{2,1,0:T(8,128)S(1)} %get-tuple-element.62) | copy-start | bytes 1769476
  750.7 402.2 %copy-start.41 = (f32[8,24,768]{2,1,0:T(8,128)}, f32[8,24,768]{2,1,0:T(8,128)S(1)}, u32[]{:S(2)}) copy-start(f32[8,24,768]{2,1,0:T(8,128)S(1)} %get-tuple-element.60) | copy-start | bytes 1769476
  819.6 327.0 %all-gather.12.cloned.1.call-start = ((), (), s32[]{:S(2)}) async-start(), calls=%async_computation.13 | async-start | bytes 12165120 | tf_op jit(solution)/shard_map/all_gather | solution.py:141
  1052.7 370.6 %reduce-scatter.18.cloned.1.call-start = ((), (), s32[]{:S(2)}) async-start(), calls=%async_computation.14 | async-start | bytes 24330240 | tf_op jit(solution)/shard_map/reduce_scatter | solution.py:142
  1193.4 325.4 %all-gather.14.cloned.1.call-start = ((), (), s32[]{:S(2)}) async-start(), calls=%async_computation.15 | async-start | bytes 12165120 | tf_op jit(solution)/shard_map/all_gather | solution.py:141
  1425.2 370.2 %reduce-scatter.20.cloned.1.call-start = ((), (), s32[]{:S(2)}) async-start(), calls=%async_computation.16 | async-start | bytes 24330240 | tf_op jit(solution)/shard_map/reduce_scatter | solution.py:142
  1565.5 325.7 %all-gather.16.cloned.1.call-start = ((), (), s32[]{:S(2)}) async-start(), calls=%async_computation.17 | async-start | bytes 12165120 | tf_op jit(solution)/shard_map/all_gather | solution.py:141
  1797.4 370.5 %reduce-scatter.22.cloned.1.call-start = ((), (), s32[]{:S(2)}) async-start(), calls=%async_computation.18 | async-start | bytes 24330240 | tf_op jit(solution)/shard_map/reduce_scatter | solution.py:142
  1937.9 325.3 %all-gather.18.cloned.1.call-start = ((), (), s32[]{:S(2)}) async-start(), calls=%async_computation.19 | async-start | bytes 12165120 | tf_op jit(solution)/shard_map/all_gather | solution.py:141
  2169.7 370.2 %reduce-scatter.24.cloned.1.call-start = ((), (), s32[]{:S(2)}) async-start(), calls=%async_computation.20 | async-start | bytes 24330240 | tf_op jit(solution)/shard_map/reduce_scatter | solution.py:142
  2309.9 332.4 %reduce-scatter.26.cloned.1.call-start = ((), (), s32[]{:S(2)}) async-start(), calls=%async_computation.22 | async-start | bytes 1622016
  2313.6 228.2 %copy-start.113 = (f32[8,128]{1,0:T(8,128)S(1)}, f32[8,128]{1,0:T(8,128)}, u32[]{:S(2)}) copy-start(f32[8,128]{1,0:T(8,128)} %get-tuple-element.27) | copy-start | bytes 12292
  2313.7 228.2 %copy-start.7 = (bf16[8,128,768]{2,1,0:T(8,128)(2,1)S(1)}, bf16[8,128,768]{2,1,0:T(8,128)(2,1)}, u32[]{:S(2)}) copy-start(bf16[8,128,768]{2,1,0:T(8,128)(2,1)} %param.13) | copy-start | bytes 4718596
  2313.7 228.2 %copy-start.81 = (f32[8,128]{1,0:T(8,128)S(1)}, f32[8,128]{1,0:T(8,128)}, u32[]{:S(2)}) copy-start(f32[8,128]{1,0:T(8,128)} %copy-done.79) | copy-start | bytes 12292
  2313.7 228.2 %copy-start.88 = (f32[768]{0:T(1024)S(1)}, f32[768]{0:T(1024)}, u32[]{:S(2)}) copy-start(f32[768]{0:T(1024)} %copy-done.86) | copy-start | bytes 9220
  2313.7 228.2 %copy-start.91 = (f32[8,128]{1,0:T(8,128)S(1)}, f32[8,128]{1,0:T(8,128)}, u32[]{:S(2)}) copy-start(f32[8,128]{1,0:T(8,128)} %copy-done.89) | copy-start | bytes 12292
  2313.7 228.2 %copy-start.106 = (f32[8,128]{1,0:T(8,128)S(1)}, f32[8,128]{1,0:T(8,128)}, u32[]{:S(2)}) copy-start(f32[8,128]{1,0:T(8,128)} %copy-done.105) | copy-start | bytes 12292
  2315.5 421.6 %all-gather.20.cloned.1.call-start = ((), (), s32[]{:S(2)}) async-start(), calls=%async_computation.21 | async-start | bytes 12165120 | tf_op jit(solution)/shard_map/all_gather | solution.py:141
  2556.5 88.7 %copy-start.127 = (f32[12]{0:T(128)S(1)}, f32[12]{0:T(128)}, u32[]{:S(2)}) copy-start(f32[12]{0:T(128)} %get-tuple-element.57) | copy-start | bytes 148
  2556.6 89.2 %copy-start.115 = (f32[12,128]{1,0:T(8,128)S(1)}, f32[12,128]{1,0:T(8,128)}, u32[]{:S(2)}) copy-start(f32[12,128]{1,0:T(8,128)} %get-tuple-element.58) | copy-start | bytes 18436
  2562.8 177.5 %copy-start.29 = (f32[8,24,768]{2,1,0:T(8,128)S(1)}, f32[8,24,768]{2,1,0:T(8,128)}, u32[]{:S(2)}) copy-start(f32[8,24,768]{2,1,0:T(8,128)} %copy-done.28) | copy-start | bytes 1769476
  (123 other events, 774.0 us)
Sparse Core Ops, SparseCore 0:
  11.5 84.8 all-gather.7
  99.9 80.6 all-gather.9
  333.9 205.2 reduce-scatter.13
  545.5 203.8 reduce-scatter.11
  819.7 231.0 reduce-scatter.15
  1054.6 91.9 all-gather.11
  1193.5 229.7 reduce-scatter.17
  1426.8 91.9 all-gather.13
  1565.6 229.7 reduce-scatter.19
  1799.2 91.9 all-gather.15
  1938.0 229.7 reduce-scatter.21
  2171.2 91.9 all-gather.17
  2310.0 229.9 reduce-scatter.23
  2545.9 96.3 reduce-scatter.25
  2645.6 91.4 all-gather.19
where the time goes:
time: 2770 us; the launch traced here: 2760 us
  waiting for transfers between devices  1960 us (71%)
  matrix products  401 us (14%)
  other arithmetic  235 us (8%)
  blocking collectives  82.7 us (3%)
  local copies, waits for them, and re-layouts  65.6 us (2%)
    reduce_scatter x5, waiting for transfers between devices, both_grams(): lax.psum_scatter(joined, ('dp', 'upd'), scatter_dimension=1, tiled=True)  1150 us
    all_gather x5, waiting for transfers between devices, both_grams(): lax.all_gather(lax.psum_scatter(joined, ('dp', 'upd'), scatter_dimension=...  465 us
    reduce_scatter x1, waiting for transfers between devices, local(): lax.psum_scatter(square_slope, ('dp', 'upd'), scatter_dimension=1, tiled=...  200 us
    dot_general x10, matrix products, gram_of(): jnp.einsum('wrd,wre->wde', block, block, precision=lax.Precision.HIGHEST)  98.5 us
    unnamed x16, waiting for transfers between devices  79.8 us
    all_gather x1, waiting for transfers between devices, local(): lax.all_gather(square_master.astype(jnp.bfloat16), ('dp', 'upd'), axis=1,...  67.6 us
  transfers between devices with their start and end apart: 15, of which 13 were waited for; matrix products, arithmetic and copies ran while one was open for 12% of the time, Pallas kernels for 0%

commit v1 on v0

--- a/solution.py
+++ b/solution.py
@@ -1,7 +1,7 @@
 import jax
 import jax.numpy as jnp
 from jax import lax
-from jax.sharding import PartitionSpec as P
+from jax.sharding import Mesh, PartitionSpec as P
 
 D = 768
 FF = 3072
@@ -126,45 +126,72 @@
     return hidden + round_gradient(jnp.matmul(active, tall[1]) + vectors[16])
 
 
-def gram_of(block):
-    return jnp.einsum("wrd,wre->wde", block, block, precision=lax.Precision.HIGHEST)
-
-
-def advance(current, gram):
-    mixed = jnp.einsum("wrd,wde->wre", current, gram, precision=lax.Precision.HIGHEST)
-    second = jnp.einsum("wrd,wde->wre", mixed, gram, precision=lax.Precision.HIGHEST)
-    return FIRST_TERM * current + SECOND_TERM * mixed + THIRD_TERM * second
-
-
-def both_grams(square, tall):
-    joined = jnp.concatenate([gram_of(square), gram_of(tall)], axis=0)
-    summed = lax.all_gather(
-        lax.psum_scatter(joined, ("dp", "upd"), scatter_dimension=1, tiled=True).astype(
-            jnp.bfloat16
-        ),
-        ("dp", "upd"),
-        axis=1,
-        tiled=True,
-    ).astype(jnp.float32)
-    return (summed[:8], summed[8:])
-
-
-def shared_rows(square_state, tall_state):
-    square_squares, tall_squares = lax.psum(
-        (
-            jnp.sum(square_state * square_state, axis=(1, 2)),
-            jnp.sum(tall_state * tall_state, axis=(1, 2)),
-        ),
-        ("dp", "upd"),
-    )
-    square = square_state * (1.0 / (jnp.sqrt(square_squares) + FLOOR_EPSILON))[:, None, None]
-    tall = tall_state * (1.0 / (jnp.sqrt(tall_squares) + FLOOR_EPSILON))[:, None, None]
-    first_sweep = 0
-    for sweep in range(first_sweep, ITERS):
-        square_gram, tall_gram = both_grams(square, tall)
-        square = advance(square, square_gram)
-        tall = advance(tall, tall_gram)
-    return (square, tall)
+AXES = ("tall", "square", "row")
+
+
+def matmul3(left, right):
+    return jnp.matmul(left, right, precision=lax.Precision.HIGH)
+
+
+def to_owner_rows(square_state, tall_state, count):
+    rows = square_state.shape[1]
+    group = count // 16
+    if rows % group == 0:
+        piece = rows // group
+        pieces = jnp.concatenate(
+            [
+                square_state.reshape(8 * group, piece, D),
+                tall_state.reshape(8 * group, piece, D),
+            ],
+            axis=0,
+        ).astype(jnp.bfloat16)
+        return lax.all_to_all(pieces, AXES, 0, 0, tiled=True).reshape(count * piece, D)
+    square_all = lax.all_gather(square_state.astype(jnp.bfloat16), AXES, axis=1, tiled=True)
+    tall_all = lax.all_gather(tall_state.astype(jnp.bfloat16), AXES, axis=1, tiled=True)
+    joined = jnp.concatenate([square_all.reshape(-1, D), tall_all.reshape(-1, D)], axis=0)
+    own = joined.shape[0] // count
+    return lax.dynamic_slice_in_dim(joined, lax.axis_index(AXES) * own, own, axis=0)
+
+
+def from_owner_rows(rows_out, count, square_rows, tall_rows):
+    group = count // 16
+    rows_out = rows_out.astype(jnp.bfloat16)
+    if square_rows % group == 0:
+        piece = square_rows // group
+        back = lax.all_to_all(rows_out.reshape(count, piece, D), AXES, 0, 0, tiled=True)
+        return (
+            back[: 8 * group].reshape(8, square_rows, D),
+            back[8 * group :].reshape(2, tall_rows, D),
+        )
+    joined = lax.all_gather(rows_out, AXES, axis=0, tiled=True)
+    square_all = joined[: 8 * square_rows * count].reshape(8, square_rows * count, D)
+    tall_all = joined[8 * square_rows * count :].reshape(2, tall_rows * count, D)
+    index = lax.axis_index(AXES)
+    return (
+        lax.dynamic_slice_in_dim(square_all, index * square_rows, square_rows, axis=1),
+        lax.dynamic_slice_in_dim(tall_all, index * tall_rows, tall_rows, axis=1),
+    )
+
+
+def orthogonal_rows(rows_in):
+    rows_in = rows_in.astype(jnp.float32)
+    gram = lax.psum(
+        jnp.einsum("rd,re->de", rows_in, rows_in, precision=lax.Precision.HIGHEST), "row"
+    )
+    is_tall = lax.axis_index("tall") >= 2
+    wide = lax.psum(jnp.where(is_tall, gram, 0.0), "square")
+    gram = jnp.where(is_tall, wide, gram)
+    eye = (jnp.arange(D)[:, None] == jnp.arange(D)[None, :]).astype(jnp.float32)
+    scale = 1.0 / (jnp.sqrt(jnp.sum(gram * eye)) + FLOOR_EPSILON)
+    gram = gram * (scale * scale)
+    current = rows_in * scale
+
+    for sweep in range(ITERS):
+        poly = FIRST_TERM * eye + SECOND_TERM * gram + THIRD_TERM * matmul3(gram, gram)
+        current = matmul3(current, poly)
+        if sweep < ITERS - 1:
+            gram = matmul3(matmul3(gram, poly), poly)
+    return current
 
 
 def local(
@@ -182,9 +209,11 @@
     head_scale,
     relative,
 ):
+    count = lax.axis_size(AXES)
+    index = lax.axis_index(AXES)
     square_copy, tall_copy = (
-        lax.all_gather(square_master.astype(jnp.bfloat16), ("dp", "upd"), axis=1, tiled=True),
-        lax.all_gather(tall_master.astype(jnp.bfloat16), ("dp", "upd"), axis=1, tiled=True),
+        lax.all_gather(square_master.astype(jnp.bfloat16), AXES, axis=1, tiled=True),
+        lax.all_gather(tall_master.astype(jnp.bfloat16), AXES, axis=1, tiled=True),
     )
     params = (
         square_copy.astype(jnp.float32),
@@ -206,19 +235,42 @@
         cotangent.astype(jnp.float32) * valid[:, :, None]
     )
     square_slope, tall_slope, vector_slope, feed_slope, scale_slope, bias_slope = param_slopes
-    total, scale_sum, bias_sum = lax.psum(
-        (jnp.sum(lengths).astype(jnp.float32), scale_slope, bias_slope), ("dp", "upd")
-    )
-    square_sum, tall_sum, vector_sum, feed_sum = (
-        lax.psum_scatter(square_slope, ("dp", "upd"), scatter_dimension=1, tiled=True),
-        lax.psum_scatter(tall_slope, ("dp", "upd"), scatter_dimension=1, tiled=True),
-        lax.psum_scatter(vector_slope, ("dp", "upd"), scatter_dimension=1, tiled=True),
-        lax.psum_scatter(feed_slope, ("dp", "upd"), scatter_dimension=1, tiled=True),
-    )
-    factor = inputs.shape[0] * lax.axis_size("dp") * lax.axis_size("upd") / total
+    tall_sum = lax.psum_scatter(
+        tall_slope.astype(jnp.bfloat16), AXES, scatter_dimension=1, tiled=True
+    ).astype(jnp.float32)
+    square_sum = lax.psum_scatter(
+        square_slope.astype(jnp.bfloat16), AXES, scatter_dimension=1, tiled=True
+    ).astype(jnp.float32)
+    small = [
+        jnp.sum(lengths).astype(jnp.float32).reshape(1),
+        scale_slope.reshape(-1),
+        bias_slope.reshape(-1),
+        vector_slope.reshape(-1),
+        feed_slope.reshape(-1),
+    ]
+    sizes = [piece.shape[0] for piece in small]
+    summed = lax.psum(jnp.concatenate(small), AXES)
+    starts = [sum(sizes[:i]) for i in range(len(sizes) + 1)]
+    total, scale_sum, bias_sum, vector_sum, feed_sum = (
+        summed[starts[i] : starts[i + 1]] for i in range(len(sizes))
+    )
+    factor = inputs.shape[0] * count / total[0]
+    bias_sum = bias_sum.reshape(bias_slope.shape)
+    width = vector_slope.shape[1] // count
+    vector_sum = lax.dynamic_slice_in_dim(
+        vector_sum.reshape(vector_slope.shape), index * width, width, axis=1
+    )
+    width = feed_slope.shape[1] // count
+    feed_sum = lax.dynamic_slice_in_dim(
+        feed_sum.reshape(feed_slope.shape), index * width, width, axis=1
+    )
     square_state = MOMENTUM_DECAY * square_momentum + factor * square_sum
     tall_state = MOMENTUM_DECAY * tall_momentum + factor * tall_sum
-    square, tall = shared_rows(square_state, tall_state)
+    rows_out = orthogonal_rows(to_owner_rows(square_state, tall_state, count))
+    square, tall = from_owner_rows(
+        rows_out, count, square_state.shape[1], tall_state.shape[1]
+    )
+    square, tall = square.astype(jnp.float32), tall.astype(jnp.float32)
     square_weight = square_master * (1.0 - LEARN_RATE * WEIGHT_DECAY) - LEARN_RATE * square
     tall_weight = (
         tall_master * (1.0 - LEARN_RATE * WEIGHT_DECAY)
@@ -240,16 +292,18 @@
 
 
 def solution(mesh):
+    count = mesh.devices.size
+    grouped = Mesh(mesh.devices.reshape(4, 4, count // 16), AXES)
     placed = (
-        P(("dp", "upd"), None, None),
-        P(("dp", "upd"), None, None),
-        P(("dp", "upd"), None, None),
-        P(("dp", "upd")),
-        P(("dp", "upd")),
-        P(None, ("dp", "upd"), None),
-        P(None, ("dp", "upd"), None),
-        P(None, ("dp", "upd"), None),
-        P(None, ("dp", "upd"), None),
+        P(AXES, None, None),
+        P(AXES, None, None),
+        P(AXES, None, None),
+        P(AXES),
+        P(AXES),
+        P(None, AXES, None),
+        P(None, AXES, None),
+        P(None, AXES, None),
+        P(None, AXES, None),
         P(),
         P(),
         P(),
@@ -257,18 +311,18 @@
     )
     return jax.shard_map(
         local,
-        mesh=mesh,
+        mesh=grouped,
         in_specs=placed,
         out_specs=(
-            P(("dp", "upd"), None, None),
-            P(("dp", "upd"), None, None),
-            P(("dp", "upd"), None, None),
-            P(None, ("dp", "upd"), None),
-            P(None, ("dp", "upd"), None),
-            P(None, ("dp", "upd"), None),
-            P(None, ("dp", "upd"), None),
-            P(None, ("dp", "upd")),
-            P(None, ("dp", "upd")),
+            P(AXES, None, None),
+            P(AXES, None, None),
+            P(AXES, None, None),
+            P(None, AXES, None),
+            P(None, AXES, None),
+            P(None, AXES, None),
+            P(None, AXES, None),
+            P(None, AXES),
+            P(None, AXES),
             P(),
             P(),
         ),

time: 2770 us -> 1130 us (0.41)
  waiting for transfers between devices: 1960 us -> 495 us
  matrix products: 401 us -> 283 us
  blocking collectives: 82.7 us -> 24 us
  other arithmetic: 235 us -> 206 us
    reduce_scatter x7 -> x1, waiting for transfers between devices: 1350 us -> 140 us  [local(): lax.psum_scatter(tall_slope.astype(jnp.bfloat16), AXES, scatter_dimension...]
    all_gather x7 -> x2, waiting for transfers between devices: 533 us -> 65.3 us  [the longest x1 65.3 us: local(): lax.all_gather(square_master.astype(jnp.bfloat16), AXES, axis=1, tiled=True)]
    psum x0 -> x3, waiting for transfers between devices: none -> 138 us  [the longest x1 66.3 us: local(): summed = lax.psum(jnp.concatenate(small), AXES)]
    dot_general x30 -> x19, matrix products: 191 us -> 61.2 us  [the longest x18 58.9 us: matmul3(): return jnp.matmul(left, right, precision=lax.Precision.HIGH)]
    psum x2 -> x0, blocking collectives: 82.7 us -> none  [the longest x1 42.2 us: local(): lax.psum((jnp.sum(lengths).astype(jnp.float32), scale_slope, bias_slope),...]
    unnamed x16 -> x8, waiting for transfers between devices: 79.8 us -> 138 us
    concatenate x5 -> x1, other arithmetic: 41.1 us -> 1.09 us  [to_owner_rows(): jnp.concatenate([square_state.reshape(8 * group, piece, D), tall_state.re...]
  transfers between devices with their start and end apart: 15 -> 8, of which waited for: 13 -> 7; matrix products, arithmetic and copies ran while one was open for 12% -> 19% of each run, Pallas kernels for 0% -> 0%
where the time goes in v1:
time: 1130 us; the launch traced here: 1120 us
  waiting for transfers between devices  495 us (44%)
  matrix products  283 us (25%)
  other arithmetic  206 us (18%)
  local copies, waits for them, and re-layouts  86.5 us (8%)
  blocking collectives  24 us (2%)
  between operations  18.5 us (2%)
    reduce_scatter x1, waiting for transfers between devices, local(): lax.psum_scatter(tall_slope.astype(jnp.bfloat16), AXES, scatter_dimension...  140 us
    unnamed x8, waiting for transfers between devices  138 us
    psum x1, waiting for transfers between devices, local(): summed = lax.psum(jnp.concatenate(small), AXES)  66.3 us
    all_gather x1, waiting for transfers between devices, local(): lax.all_gather(square_master.astype(jnp.bfloat16), AXES, axis=1, tiled=True)  65.3 us
    dot_general x18, matrix products, matmul3(): return jnp.matmul(left, right, precision=lax.Precision.HIGH)  58.9 us
    psum x1, waiting for transfers between devices, orthogonal_rows(): wide = lax.psum(jnp.where(is_tall, gram, 0.0), 'square')  58.7 us
    dot_general x6, matrix products, attend(): return round_gradient(jnp.einsum('bhqk,bkhe->bqhe', weights, values))  39 us
    reduce_sum x3, other arithmetic, norm_rows(): center = values - jnp.mean(values, axis=-1, keepdims=True)  38.3 us
  transfers between devices with their start and end apart: 8, of which 7 were waited for; matrix products, arithmetic and copies ran while one was open for 19% of the time, Pallas kernels for 0%

profile of v1, /device:TPU:0, one launch (start us, length us, event | category | flops | bytes accessed | tf_op | source)
XLA Modules:
  0.0 1119.0 jit_solution(6008614789562303462)
XLA Ops:
  31.1 65.3 %all-gather.3.cloned.1.call-done = bf16[8,768,768]{2,1,0:T(8,128)(2,1)} async-done(((bf16[8,24,768]{2,1,0:T(8,128)(2,1)}), bf16[8,768,768]{2,1,0:T(8,128)(2,1)}) %all-gather.3.cloned.1.call-update) | async-done | bytes 9437200 | tf_op jit(solution)/shard_map/all_gather | solution.py:215
  116.6 5.6 convert_reduce_fusion.4
  128.6 6.1 fusion.210
  174.5 6.1 divide_convert_fusion
  190.7 7.9 bitcast_reduce_fusion
  212.2 13.1 %fusion.39 = (u8[128,3072]{1,0:T(8,128)(4,1)S(1)}, u8[128,3072]{1,0:T(8,128)(4,1)S(1)}, f32[8,128,3072]{2,1,0:T(8,128)}) fusion(f32[3072]{0:T(1024)S(1)} %bitcast.313, bf16[8,128,768]{2,1,0:T(8,128)(2,1)} %add_convert_fusion.9, bf16[2,3072,768]{2,1,0:T(8,128)(2,1)} %all-gather.5.cloned.1.call-done), kind=kOutput, calls=%fused_computation.136 | convolution fusion | flops 4875091968 | bytes 19673088 | tf_op jit(solution)/shard_map/jvp()/dot_general | solution.py:122
  225.3 35.2 %fusion.208 = (f32[8,128]{1,0:T(8,128)S(1)}, f32[8,128,3072]{2,1,0:T(8,128)S(1)}, f32[8,128,3072]{2,1,0:T(8,128)}) fusion(f32[8,128,3072]{2,1,0:T(8,128)} %get-tuple-element.99, f32[3072]{0:T(1024)S(1)} %bitcast.314, u8[128,3072]{1,0:T(8,128)(4,1)S(1)} %get-tuple-element.14, u8[128,3072]{1,0:T(8,128)(4,1)S(1)} %get-tuple-element.13), kind=kLoop, calls=%fused_computation.381 | loop fusion | flops 223345664 | bytes 38551552 | tf_op jit(solution)/shard_map/jvp()/reduce_sum | solution.py:59
  260.4 12.2 %multiply_reduce_fusion.2 = (f32[8,128]{1,0:T(8,128)S(1)}, f32[8,128]{1,0:T(8,128)S(1)}, f32[3072]{0:T(1024)}, f32[8,128,3072]{2,1,0:T(8,128)}) fusion(f32[8,128,3072]{2,1,0:T(8,128)S(1)} %get-tuple-element.71, f32[3072]{0:T(1024)S(1)} %bitcast.310, f32[8,128]{1,0:T(8,128)S(1)} %broadcast_multiply_fusion, bf16[8,128,768]{2,1,0:T(8,128)(2,1)S(1)} %copy-done.47, ...), kind=kOutput, calls=%fused_computation.17 | convolution fusion | flops 4853853184 | bytes 31494144 | tf_op jit(solution)/shard_map/transpose(jvp())/dot_general | solution.py:126
  272.7 7.6 multiply_reduce_fusion
  280.3 19.7 %add_convert_fusion.2 = (bf16[8,128,3072]{2,1,0:T(8,128)(2,1)}, bf16[8,128,3072]{2,1,0:T(8,128)(2,1)}) fusion(f32[8,128,3072]{2,1,0:T(8,128)} %get-tuple-element.72, f32[8,128,3072]{2,1,0:T(8,128)} %get-tuple-element.99, f32[8,128]{1,0:T(8,128)S(1)} %negate_multiply_fusion.6, f32[3072]{0:T(1024)S(1)} %bitcast.315, f32[8,128]{1,0:T(8,128)S(1)} %get-tuple-element.86, ...), kind=kLoop, calls=%fused_computation.16 | loop fusion | flops 81788928 | bytes 62967808 | tf_op jit(solution)/shard_map/transpose(jvp())/convert_element_type | solution.py:55
  304.4 9.8 multiply_reduce_fusion.8
  329.5 6.2 convolution_convert_fusion.1
  335.6 10.8 multiply_reduce_fusion.1
  346.5 11.4 %convert_reduce_fusion.1 = (f32[8,12,128]{2,1,0:T(8,128)S(1)}, pred[8,12,128,256]{3,2,1,0:T(8,128)(4,1)}, f32[8,12,128]{2,1,0:T(8,128)S(1)}) fusion(f32[8,12,128]{2,1,0:T(8,128)S(1)} %get-tuple-element.93, f32[8,12,128,256]{3,2,1,0:T(8,128)S(1)} %bitcast.273, pred[8,256]{1,0:T(8,128)(4,1)S(1)} %iota_compare_fusion.10, f32[8,12,128]{2,1,0:T(8,128)S(1)} %neg.48, ...), kind=kLoop, calls=%fused_computation.13 | loop fusion | flops 28286976 | bytes 28559360 | tf_op jit(solution)/shard_map/jvp()/reduce_sum | solution.py:67
  358.0 10.1 select_convert_fusion
  368.0 7.2 convolution_convert_fusion.6
  427.1 7.7 convolution_bitcast_fusion
  461.4 5.7 fusion.134
  468.7 7.7 convolution_bitcast_fusion.1
  476.5 9.4 add_convert_fusion
  513.0 8.7 copy.161
  521.7 66.3 %all-reduce.34.cloned.1.call-done = f32[23821]{0:T(1024)} async-done(((f32[23821]{0:T(1024)}), f32[23821]{0:T(1024)}) %all-reduce.34.cloned.1.call-update) | async-done | bytes 95300 | tf_op jit(solution)/shard_map/psum | solution.py:252
  589.9 140.4 %reduce-scatter.5.cloned.1.call-done = bf16[2,96,768]{2,1,0:T(8,128)(2,1)} async-done(((bf16[2,3072,768]{2,1,0:T(8,128)(2,1)}), bf16[2,96,768]{2,1,0:T(8,128)(2,1)}) %reduce-scatter.5.cloned.1.call-update) | async-done | bytes 294928 | tf_op jit(solution)/shard_map/reduce_scatter | solution.py:238
  733.5 138.1 %reduce-scatter.7.cloned.1.call-done = bf16[24,6144]{1,0:T(8,128)(2,1)} async-done(((bf16[768,6144]{1,0:T(8,128)(2,1)}), bf16[24,6144]{1,0:T(8,128)(2,1)}) %reduce-scatter.7.cloned.1.call-update) | async-done | bytes 294928
  877.6 24.0 %all_to_all.10 = bf16[32,12,768]{2,1,0:T(8,128)(2,1)S(1)} all-to-all(bf16[32,12,768]{2,1,0:T(8,128)(2,1)S(1)} %pad_maximum_fusion), channel_id=1, replica_groups=mesh['tall'=4,'square'=4,'row'=2] {'tall','square','row'}, dimensions={0} | all-to-all | bytes 1179648 | tf_op jit(solution)/shard_map/all_to_all | solution.py:148
  904.9 7.6 fusion.137
  912.4 13.2 %all-reduce.36.cloned.1.call-done = f32[768,768]{1,0:T(8,128)} async-done(((f32[768,768]{1,0:T(8,128)}), f32[768,768]{1,0:T(8,128)}) %all-reduce.36.cloned.1.call-update) | async-done | bytes 2359312 | tf_op jit(solution)/shard_map/psum | solution.py:178
  927.3 8.6 add_convert_fusion.4
  935.9 9.7 add_convert_fusion.8
  945.6 58.7 %all-reduce.38.cloned.1.call-done = f32[768,768]{1,0:T(8,128)} async-done(((f32[768,768]{1,0:T(8,128)}), f32[768,768]{1,0:T(8,128)}) %all-reduce.38.cloned.1.call-update) | async-done | bytes 2359312 | tf_op jit(solution)/shard_map/psum | solution.py:182
  1009.1 6.5 fusion.40
  1088.2 13.0 %all-to-all-done.1 = bf16[32,12,768]{2,1,0:T(8,128)(2,1)} async-done(((bf16[32,12,768]{2,1,0:T(8,128)(2,1)}), bf16[32,12,768]{2,1,0:T(8,128)(2,1)}, u32[]{:S(2)}, u32[]{:S(2)}) %all-to-all-start.1) | async-done | bytes 589856 | tf_op jit(solution)/shard_map/all_to_all | solution.py:161
  (487 shorter events, 341.1 us)
Async XLA Ops:
  7.2 147.5 %copy-start = (bf16[8,256,768]{2,1,0:T(8,128)(2,1)S(1)}, bf16[8,256,768]{2,1,0:T(8,128)(2,1)}, u32[]{:S(2)}) copy-start(bf16[8,256,768]{2,1,0:T(8,128)(2,1)} %param.14) | copy-start | bytes 9437188
  7.2 89.2 %all-gather.3.cloned.1.call-start = ((), (), s32[]{:S(2)}) async-start(), calls=%async_computation.4 | async-start | bytes 9732096 | tf_op jit(solution)/shard_map/all_gather | solution.py:215
  9.2 203.0 %all-gather.5.cloned.1.call-start = ((), (), s32[]{:S(2)}) async-start(), calls=%async_computation.5 | async-start | bytes 9732096 | tf_op jit(solution)/shard_map/all_gather | solution.py:216
  11.1 576.9 %all-reduce.34.cloned.1.call-start = ((), (), s32[]{:S(2)}) async-start(), calls=%async_computation.6 | async-start | bytes 196608 | tf_op jit(solution)/shard_map/psum | solution.py:252
  12.7 128.1 %copy-start.99 = (f32[768]{0:T(1024)}, f32[768]{0:T(1024)S(1)}, u32[]{:S(2)}) copy-start(f32[768]{0:T(1024)S(1)} %get-tuple-element.49) | copy-start | bytes 9220
  12.7 133.0 %copy-start.101 = (f32[768]{0:T(1024)}, f32[768]{0:T(1024)S(1)}, u32[]{:S(2)}) copy-start(f32[768]{0:T(1024)S(1)} %get-tuple-element.45) | copy-start | bytes 9220
  16.4 9.3 copy-start.106
  16.5 9.3 copy-start.133
  16.5 9.3 copy-start.130
  18.3 9.3 copy-start.103
  23.3 7.7 copy-start.131
  23.3 7.8 copy-start.104
  25.8 102.8 %copy-start.128 = (f32[12]{0:T(128)}, f32[12]{0:T(128)S(1)}, u32[]{:S(2)}) copy-start(f32[12]{0:T(128)S(1)} %convert_element_type.257) | copy-start | bytes 148
  31.0 84.7 %copy-start.78 = (pred[128,128]{0,1:T(8,128)(4,1)}, pred[128,128]{0,1:T(8,128)(4,1)S(1)}, u32[]{:S(2)}) copy-start(pred[128,128]{0,1:T(8,128)(4,1)S(1)} %iota_compare_fusion.9) | copy-start | bytes 49156
  116.6 95.0 %copy-start.76 = (f32[8,12,128]{2,1,0:T(8,128)}, f32[8,12,128]{2,1,0:T(8,128)S(1)}, u32[]{:S(2)}) copy-start(f32[8,12,128]{2,1,0:T(8,128)S(1)} %fusion.140) | copy-start | bytes 147460
  225.3 35.2 %copy-start.47 = (bf16[8,128,768]{2,1,0:T(8,128)(2,1)S(1)}, bf16[8,128,768]{2,1,0:T(8,128)(2,1)}, u32[]{:S(2)}) copy-start(bf16[8,128,768]{2,1,0:T(8,128)(2,1)} %copy-done.46) | copy-start | bytes 4718596
  329.5 17.0 %slice-start = ((s8[12582912]{0:T(1024)(128)(4,1)}), s8[4194304]{0:T(1024)(128)(4,1)S(1)}, s32[]{:S(2)}) async-start(s8[12582912]{0:T(1024)(128)(4,1)} %bitcast.272), calls=%async_computation.11 | async-start | bytes 8388608
  335.6 10.9 slice-start.1
  335.6 10.9 slice-start.2
  400.3 7.9 copy-start.38
  404.6 8.2 slice-start.3
  427.1 7.7 copy-start.105
  427.1 7.7 copy-start.119
  468.7 261.7 %reduce-scatter.5.cloned.1.call-start = ((), (), s32[]{:S(2)}) async-start(), calls=%async_computation.7 | async-start | bytes 9732096 | tf_op jit(solution)/shard_map/reduce_scatter | solution.py:238
  485.9 385.7 %reduce-scatter.7.cloned.1.call-start = ((), (), s32[]{:S(2)}) async-start(), calls=%async_computation.10 | async-start | bytes 9732096
  490.6 15.0 %copy-start.45 = (bf16[8,12,256,64]{2,3,1,0:T(8,128)(2,1)}, bf16[8,12,256,64]{2,3,1,0:T(8,128)(2,1)S(1)}, u32[]{:S(2)}) copy-start(bf16[8,12,256,64]{2,3,1,0:T(8,128)(2,1)S(1)} %convolution_convert_fusion) | copy-start | bytes 9437188
  521.6 404.0 %all-reduce.36.cloned.1.call-start = ((), (), s32[]{:S(2)}) async-start(), calls=%async_computation.8 | async-start | bytes 4718592 | tf_op jit(solution)/shard_map/psum | solution.py:178
  904.8 99.5 %all-reduce.38.cloned.1.call-start = ((), (), s32[]{:S(2)}) async-start(), calls=%async_computation.9 | async-start | bytes 4718592 | tf_op jit(solution)/shard_map/psum | solution.py:182
  912.4 14.8 %copy-start.118 = (f32[8,128]{1,0:T(8,128)S(1)}, f32[8,128]{1,0:T(8,128)}, u32[]{:S(2)}) copy-start(f32[8,128]{1,0:T(8,128)} %get-tuple-element.27) | copy-start | bytes 12292
  927.3 8.6 copy-start.31
  927.3 8.6 copy-start.127
  1075.8 25.3 %all-to-all-start.1 = ((bf16[32,12,768]{2,1,0:T(8,128)(2,1)}), bf16[32,12,768]{2,1,0:T(8,128)(2,1)}, u32[]{:S(2)}, u32[]{:S(2)}) async-start(bf16[32,12,768]{2,1,0:T(8,128)(2,1)} %reshape.472), calls=%async_computation.2 | async-start | bytes 1572864 | tf_op jit(solution)/shard_map/all_to_all | solution.py:161
  (117 other events, 384.0 us)
Sparse Core Ops, SparseCore 0:
  11.5 84.8 all-gather.2
  99.9 80.6 all-gather.4
  468.8 119.1 all-reduce.33
  593.8 136.5 reduce-scatter.4
  737.1 134.4 reduce-scatter.6
  904.9 20.6 all-reduce.35
  929.1 75.2 all-reduce.37

commit v2 on v1

--- a/solution.py
+++ b/solution.py
@@ -1,6 +1,10 @@
+import functools
+
 import jax
 import jax.numpy as jnp
 from jax import lax
+from jax.experimental import pallas as pl
+from jax.experimental.pallas import tpu as pltpu
 from jax.sharding import Mesh, PartitionSpec as P
 
 D = 768
@@ -75,9 +79,7 @@
     )
 
 
-def layer_block(
-    inputs, memory, memory_len, square, tall, vectors, feed_vectors, head_scale, relative
-):
+def attention_block(inputs, memory, memory_len, square, vectors, head_scale, relative):
     item_count, query_count, model_width = inputs.shape
     head_count = head_scale.shape[0]
     memory_slots = memory.shape[1]
@@ -117,7 +119,10 @@
     mixed = round_value(
         norm_rows(mixed.reshape(item_count, query_count, model_width), vectors[12], vectors[13])
     )
-    hidden = hidden + round_gradient(jnp.matmul(mixed, square[7]) + vectors[11])
+    return hidden + round_gradient(jnp.matmul(mixed, square[7]) + vectors[11])
+
+
+def feed_block(hidden, tall, vectors, feed_vectors):
     normed = round_value(norm_rows(hidden, vectors[14], vectors[15]))
     inner = round_gradient(jnp.matmul(normed, tall[0].T) + feed_vectors[0])
     active = round_value(
@@ -127,6 +132,331 @@
 
 
 AXES = ("tall", "square", "row")
+MESH = pl.DeviceIdType.MESH
+
+
+def place():
+    z, plane, core = lax.axis_index("tall"), lax.axis_index("square"), lax.axis_index("row")
+    return z, lax.div(plane, 2), lax.rem(plane, 2), core
+
+
+def device(z, y, x, core):
+    return (z, y * 2 + x, core)
+
+
+def greet(partners):
+    barrier = pltpu.get_barrier_semaphore()
+    for partner in partners:
+        pl.semaphore_signal(barrier, inc=1, device_id=partner, device_id_type=MESH)
+    pl.semaphore_wait(barrier, len(partners))
+
+
+def reduce_kernel(groups, has_small, *refs):
+    n = len(groups)
+    ins, refs = refs[:n], refs[n:]
+    if has_small:
+        small, refs = refs[0], refs[1:]
+    outs, refs = refs[:n], refs[n:]
+    if has_small:
+        small_out, refs = refs[0], refs[1:]
+    z, y, x, core = place()
+    other = 1 - core
+    sibling = device(z, y, x, other)
+    across = {"x": device(z, y, 1 - x, core), "y": device(z, 1 - y, x, core)}
+    along = [device(lax.rem(z + k, 4), y, x, core) for k in (1, 2, 3)]
+    greet([sibling, across["x"], across["y"]] + along)
+    mine = core * 384
+    theirs = other * 384
+
+    if has_small:
+        held, total, refs = refs[0], refs[1], refs[2:]
+        small_send, small_recv, refs = refs[0], refs[1], refs[2:]
+
+        def small_copies(stage):
+            source = small if stage == 0 else total.at[stage - 1]
+            if stage < 3:
+                partner = (sibling, across["x"], across["y"])[stage]
+                return [
+                    pltpu.make_async_remote_copy(
+                        source, held.at[stage], small_send.at[stage], small_recv.at[stage],
+                        device_id=partner, device_id_type=MESH,
+                    )
+                ]
+            return [
+                pltpu.make_async_remote_copy(
+                    source, held.at[3 + z], small_send.at[3 + k], small_recv.at[3 + k],
+                    device_id=along[k], device_id_type=MESH,
+                )
+                for k in range(3)
+            ]
+
+        for copy in small_copies(0):
+            copy.start()
+
+        def small_step(stage):
+            for copy in small_copies(stage):
+                copy.wait_recv()
+            if stage < 3:
+                own = small if stage == 0 else total.at[stage - 1]
+                total[stage] = own[...] + held[stage]
+                if stage == 2:
+                    held[3 + z] = total[2]
+                for copy in small_copies(stage + 1):
+                    copy.start()
+            else:
+                small_out[...] = ((held[3] + held[4]) + held[5]) + held[6]
+    else:
+        def small_step(stage):
+            pass
+
+    plans = []
+    for g, (pieces, rows, width, by_column) in enumerate(groups):
+        r0, r1, r2, r3, f3, r4, send, recv = refs[8 * g : 8 * g + 8]
+        plans.append((pieces, rows, width, by_column, ins[g], outs[g], r0, r1, r2, r3, f3, r4, send, recv))
+
+    def where(plan, order, i):
+        pieces, by_column, width = plan[0], plan[3], plan[2]
+        j = i + order * (pieces // 2)
+        if by_column:
+            return j, order, pl.multiple_of(i * width, 128)
+        return j, j, 0
+
+    def copies(plan, stage, order, i):
+        pieces, rows, width, by_column, src, out, r0, r1, r2, r3, f3, r4, send, recv = plan
+        j, matrix, column = where(plan, order, i)
+        first = "xy"[order]
+
+        def make(source, target, slot, partner):
+            return pltpu.make_async_remote_copy(
+                source, target, send.at[slot, j], recv.at[slot, j],
+                device_id=partner, device_id_type=MESH,
+            )
+
+        if stage == 0:
+            lanes = pl.ds(pl.multiple_of(theirs + column, 128), width)
+            return [make(src.at[matrix, :, :, :, :, lanes], r0.at[j], 0, sibling)]
+        if stage == 1:
+            part = r0.at[j, :, :, 1 - x] if order == 0 else r0.at[j, :, 1 - y]
+            return [make(part, r1.at[j], 1, across[first])]
+        if stage == 2:
+            return [
+                make(r1.at[j, lax.rem(z + k + 1, 4)], r2.at[j, k], 2 + k, along[k])
+                for k in range(3)
+            ]
+        if stage == 3:
+            part = r2.at[j, 0, 1 - y] if order == 0 else r2.at[j, 0, 1 - x]
+            return [make(part, r3.at[j], 5, across["yx"[order]])]
+        share = rows // 2
+        return [make(f3.at[j, pl.ds(pl.multiple_of(other * share, 8), share)], r4.at[j], 6, sibling)]
+
+    f32 = jnp.float32
+
+    def add(plan, stage, order, i):
+        pieces, rows, width, by_column, src, out, r0, r1, r2, r3, f3, r4, send, recv = plan
+        j, matrix, column = where(plan, order, i)
+        if stage == 0:
+            lanes = pl.ds(pl.multiple_of(mine + column, 128), width)
+
+            @pl.loop(0, 16)
+            def _(block):
+                a, b, d = lax.div(block, 4), lax.rem(lax.div(block, 2), 2), lax.rem(block, 2)
+                r0[j, a, b, d] = (
+                    r0[j, a, b, d].astype(f32) + src[matrix, a, b, d, :, lanes].astype(f32)
+                ).astype(jnp.bfloat16)
+        elif stage == 1:
+            @pl.loop(0, 8)
+            def _(block):
+                a, b = lax.div(block, 2), lax.rem(block, 2)
+                own = r0[j, a, b, x] if order == 0 else r0[j, a, y, b]
+                r1[j, a, b] = (r1[j, a, b].astype(f32) + own.astype(f32)).astype(jnp.bfloat16)
+        elif stage == 2:
+            for b in range(2):
+                r2[j, 0, b] = (
+                    (r2[j, 0, b].astype(f32) + r2[j, 1, b].astype(f32))
+                    + (r2[j, 2, b].astype(f32) + r1[j, z, b].astype(f32))
+                ).astype(jnp.bfloat16)
+        elif stage == 3:
+            own = r2[j, 0, y] if order == 0 else r2[j, 0, x]
+            f3[j] = r3[j].astype(f32) + own.astype(f32)
+        else:
+            share = rows // 2
+            lanes = pl.ds(pl.multiple_of(mine + column, 128), width)
+            out[matrix, :, lanes] = f3[j, pl.ds(pl.multiple_of(core * share, 8), share)]
+            lanes = pl.ds(pl.multiple_of(theirs + column, 128), width)
+            out[matrix, :, lanes] = r4[j]
+
+    def each(plan, body):
+        @pl.loop(0, plan[0] // 2)
+        def _(i):
+            for order in range(2):
+                body(order, i)
+
+    def start(plan, stage):
+        def body(order, i):
+            for copy in copies(plan, stage, order, i):
+                copy.start()
+
+        each(plan, body)
+
+    def step(plan, stage):
+        def body(order, i):
+            for copy in copies(plan, stage, order, i):
+                copy.wait_recv()
+            add(plan, stage, order, i)
+            if stage < 4:
+                for copy in copies(plan, stage + 1, order, i):
+                    copy.start()
+
+        each(plan, body)
+
+    def finish(plan, stage):
+        def body(order, i):
+            for copy in copies(plan, stage, order, i):
+                copy.wait_send()
+
+        each(plan, body)
+
+    for plan in plans:
+        start(plan, 0)
+    for stage in range(5):
+        if stage < 4:
+            small_step(stage)
+        for plan in plans:
+            step(plan, stage)
+    for stage in range(5):
+        for plan in plans:
+            finish(plan, stage)
+    if has_small:
+        for stage in range(4):
+            for copy in small_copies(stage):
+                copy.wait_send()
+
+
+def reduce_scatter(arrays, small, collective_id):
+    groups, views, outs, scratch = [], [], [], []
+    bf16, f32 = jnp.bfloat16, jnp.float32
+    if small is not None:
+        scratch += [
+            pltpu.VMEM((7,) + small.shape, f32),
+            pltpu.VMEM((3,) + small.shape, f32),
+            pltpu.SemaphoreType.DMA((6,)),
+            pltpu.SemaphoreType.DMA((6,)),
+        ]
+    for array in arrays:
+        matrices, height, width_all = array.shape
+        rows = height // 16
+        by_column = matrices == 2
+        pieces, width = (6, 128) if by_column else (matrices, 384)
+        groups.append((pieces, rows, width, by_column))
+        views.append(array.reshape(matrices, 4, 2, 2, rows, width_all))
+        outs.append(jax.ShapeDtypeStruct((matrices, rows // 2, width_all), f32))
+        scratch += [
+            pltpu.VMEM((pieces, 4, 2, 2, rows, width), bf16),
+            pltpu.VMEM((pieces, 4, 2, rows, width), bf16),
+            pltpu.VMEM((pieces, 3, 2, rows, width), bf16),
+            pltpu.VMEM((pieces, rows, width), bf16),
+            pltpu.VMEM((pieces, rows, width), f32),
+            pltpu.VMEM((pieces, rows // 2, width), f32),
+            pltpu.SemaphoreType.DMA((7, pieces)),
+            pltpu.SemaphoreType.DMA((7, pieces)),
+        ]
+    if small is not None:
+        views.append(small)
+        outs.append(jax.ShapeDtypeStruct(small.shape, f32))
+    vmem = pl.BlockSpec(memory_space=pltpu.VMEM)
+    return pl.pallas_call(
+        functools.partial(reduce_kernel, tuple(groups), small is not None),
+        out_shape=tuple(outs),
+        in_specs=[vmem] * len(views),
+        out_specs=tuple([vmem] * len(outs)),
+        scratch_shapes=scratch,
+        compiler_params=pltpu.CompilerParams(
+            collective_id=collective_id, has_side_effects=True, vmem_limit_bytes=60 << 20
+        ),
+    )(*views)
+
+
+def gram_kernel(gram, out, other_sum, half_a, half_b, final, send, recv):
+    z, y, x, core = place()
+    sibling = device(z, y, x, 1 - core)
+    x_side, y_side = device(z, y, 1 - x, core), device(z, 1 - y, x, core)
+    greet([sibling, x_side, y_side])
+    side = gram.shape[0] // 2
+    rows = pl.ds(pl.multiple_of(core * side, 8), side)
+    rest = pl.ds(pl.multiple_of((1 - core) * side, 8), side)
+
+    def send_to(source, target, slot, partner):
+        return pltpu.make_async_remote_copy(
+            source, target, send.at[slot], recv.at[slot], device_id=partner, device_id_type=MESH
+        )
+
+    first = send_to(gram.at[rest], other_sum.at[rest], 0, sibling)
+    second = send_to(gram.at[rows], other_sum.at[rows], 1, sibling)
+    first.start()
+    second.start()
+    mine = send_to(gram.at[rows], other_sum.at[rows], 0, sibling)
+    mine.wait_recv()
+    out[rows] = gram[rows] + other_sum[rows]
+    theirs = send_to(gram.at[rest], other_sum.at[rest], 1, sibling)
+    theirs.wait_recv()
+
+    @pl.when(z < 2)
+    def _():
+        out[rest] = gram[rest] + other_sum[rest]
+
+    @pl.when(z >= 2)
+    def _():
+        def pair(one, two):
+            step = send_to(out.at[rows], half_a, 2, one)
+            step.start()
+            step.wait_recv()
+            step.wait_send()
+            half_b[...] = out[rows] + half_a[...]
+            step = send_to(half_b, final, 3, two)
+            step.start()
+            step.wait_recv()
+            out[rows] = half_b[...] + final[...]
+            step.wait_send()
+
+        @pl.when(core == 0)
+        def _():
+            pair(x_side, y_side)
+
+        @pl.when(core == 1)
+        def _():
+            pair(y_side, x_side)
+
+        last = send_to(out.at[rows], out.at[rows], 4, sibling)
+        last.start()
+        arrive = send_to(out.at[rest], out.at[rest], 4, sibling)
+        arrive.wait_recv()
+        last.wait_send()
+
+    first.wait_send()
+    second.wait_send()
+
+
+def gram_sum(gram, collective_id):
+    f32 = jnp.float32
+    side = gram.shape[0] // 2
+    vmem = pl.BlockSpec(memory_space=pltpu.VMEM)
+    return pl.pallas_call(
+        gram_kernel,
+        out_shape=jax.ShapeDtypeStruct(gram.shape, f32),
+        in_specs=[vmem],
+        out_specs=vmem,
+        scratch_shapes=[
+            pltpu.VMEM(gram.shape, f32),
+            pltpu.VMEM((side, gram.shape[1]), f32),
+            pltpu.VMEM((side, gram.shape[1]), f32),
+            pltpu.VMEM((side, gram.shape[1]), f32),
+            pltpu.SemaphoreType.DMA((5,)),
+            pltpu.SemaphoreType.DMA((5,)),
+        ],
+        compiler_params=pltpu.CompilerParams(
+            collective_id=collective_id, has_side_effects=True, vmem_limit_bytes=32 << 20
+        ),
+    )(gram)
 
 
 def matmul3(left, right):
@@ -173,14 +503,15 @@
     )
 
 
-def orthogonal_rows(rows_in):
+def orthogonal_rows(rows_in, kernels):
     rows_in = rows_in.astype(jnp.float32)
-    gram = lax.psum(
-        jnp.einsum("rd,re->de", rows_in, rows_in, precision=lax.Precision.HIGHEST), "row"
-    )
-    is_tall = lax.axis_index("tall") >= 2
-    wide = lax.psum(jnp.where(is_tall, gram, 0.0), "square")
-    gram = jnp.where(is_tall, wide, gram)
+    gram = jnp.einsum("rd,re->de", rows_in, rows_in, precision=lax.Precision.HIGHEST)
+    if kernels:
+        gram = gram_sum(gram, 2)
+    else:
+        gram = lax.psum(gram, "row")
+        is_tall = lax.axis_index("tall") >= 2
+        gram = jnp.where(is_tall, lax.psum(jnp.where(is_tall, gram, 0.0), "square"), gram)
     eye = (jnp.arange(D)[:, None] == jnp.arange(D)[None, :]).astype(jnp.float32)
     scale = 1.0 / (jnp.sqrt(jnp.sum(gram * eye)) + FLOOR_EPSILON)
     gram = gram * (scale * scale)
@@ -210,6 +541,7 @@
     relative,
 ):
     count = lax.axis_size(AXES)
+    kernels = count == 32
     index = lax.axis_index(AXES)
     square_copy, tall_copy = (
         lax.all_gather(square_master.astype(jnp.bfloat16), AXES, axis=1, tiled=True),
@@ -224,23 +556,38 @@
         relative.astype(jnp.float32),
     )
 
-    def forward(params, inputs_full, memory_full):
-        return layer_block(inputs_full, memory_full, memory_len, *params)
-
-    output, pullback = jax.vjp(
-        forward, params, inputs.astype(jnp.float32), memory.astype(jnp.float32)
-    )
+    square, tall, gains, feed_gains, scales, biases = params
+
+    def attention(square, gains, scales, biases, inputs_full, memory_full):
+        return attention_block(
+            inputs_full, memory_full, memory_len, square, gains, scales, biases
+        )
+
+    hidden, attention_back = jax.vjp(
+        attention,
+        square,
+        gains,
+        scales,
+        biases,
+        inputs.astype(jnp.float32),
+        memory.astype(jnp.float32),
+    )
+    output, feed_back = jax.vjp(feed_block, hidden, tall, gains, feed_gains)
     valid = (jnp.arange(inputs.shape[1])[None, :] < lengths[:, None]).astype(jnp.float32)
-    param_slopes, input_slope, memory_slope = pullback(
+    hidden_slope, tall_slope, late_slope, feed_slope = feed_back(
         cotangent.astype(jnp.float32) * valid[:, :, None]
     )
-    square_slope, tall_slope, vector_slope, feed_slope, scale_slope, bias_slope = param_slopes
-    tall_sum = lax.psum_scatter(
-        tall_slope.astype(jnp.bfloat16), AXES, scatter_dimension=1, tiled=True
-    ).astype(jnp.float32)
-    square_sum = lax.psum_scatter(
-        square_slope.astype(jnp.bfloat16), AXES, scatter_dimension=1, tiled=True
-    ).astype(jnp.float32)
+    tall_slope, hidden_slope = lax.optimization_barrier(
+        (tall_slope.astype(jnp.bfloat16), hidden_slope)
+    )
+    tall_sum = lax.psum_scatter(tall_slope, AXES, scatter_dimension=1, tiled=True).astype(
+        jnp.float32
+    )
+    square_slope, vector_slope, scale_slope, bias_slope, input_slope, memory_slope = (
+        attention_back(hidden_slope)
+    )
+    vector_slope = vector_slope + late_slope
+    square_slope = square_slope.astype(jnp.bfloat16)
     small = [
         jnp.sum(lengths).astype(jnp.float32).reshape(1),
         scale_slope.reshape(-1),
@@ -249,8 +596,19 @@
         feed_slope.reshape(-1),
     ]
     sizes = [piece.shape[0] for piece in small]
-    summed = lax.psum(jnp.concatenate(small), AXES)
     starts = [sum(sizes[:i]) for i in range(len(sizes) + 1)]
+    if kernels:
+        lines = -(-starts[-1] // 1024) * 8
+        small.append(jnp.zeros((lines * 128 - starts[-1],), jnp.float32))
+        square_sum, summed = reduce_scatter(
+            [square_slope], jnp.concatenate(small).reshape(lines, 128), 1
+        )
+        summed = summed.reshape(-1)
+    else:
+        square_sum = lax.psum_scatter(
+            square_slope, AXES, scatter_dimension=1, tiled=True
+        ).astype(jnp.float32)
+        summed = lax.psum(jnp.concatenate(small), AXES)
     total, scale_sum, bias_sum, vector_sum, feed_sum = (
         summed[starts[i] : starts[i + 1]] for i in range(len(sizes))
     )
@@ -266,7 +624,7 @@
     )
     square_state = MOMENTUM_DECAY * square_momentum + factor * square_sum
     tall_state = MOMENTUM_DECAY * tall_momentum + factor * tall_sum
-    rows_out = orthogonal_rows(to_owner_rows(square_state, tall_state, count))
+    rows_out = orthogonal_rows(to_owner_rows(square_state, tall_state, count), kernels)
     square, tall = from_owner_rows(
         rows_out, count, square_state.shape[1], tall_state.shape[1]
     )

time: 1130 us -> 826 us (0.73)
  waiting for transfers between devices: 495 us -> 84.6 us
  Pallas kernels: 0 us -> 111 us
  starting transfers between devices: 5.22 us -> 41.6 us
  blocking collectives: 24 us -> 0 us
    reduce_scatter x1, waiting for transfers between devices: 140 us -> 0.01 us  [local(): lax.psum_scatter(tall_slope, AXES, scatter_dimension=1, tiled=True)]
    psum x3 -> x0, waiting for transfers between devices: 138 us -> none  [the longest x1 66.3 us: local(): summed = lax.psum(jnp.concatenate(small), AXES)]
    unnamed x8 -> x3, waiting for transfers between devices: 138 us -> 0.05 us
    pallas_call x0 -> x2, Pallas kernels: none -> 111 us  [the longest x1 105 us: reduce_scatter(): pl.pallas_call(functools.partial(reduce_kernel, tuple(groups), small is n...]
    all_to_all x1, starting transfers between devices: 4.71 us -> 35.9 us  [from_owner_rows(): lax.all_to_all(rows_out.reshape(count, piece, D), AXES, 0, 0, tiled=True)]
    all_to_all x1 -> x0, blocking collectives: 24 us -> none  [to_owner_rows(): lax.all_to_all(pieces, AXES, 0, 0, tiled=True).reshape(count * piece, D)]
    unnamed x284 -> x262, local copies, waits for them, and re-layouts: 25 us -> 21.1 us
  transfers between devices with their start and end apart: 8 -> 5, of which waited for: 7 -> 3; matrix products, arithmetic and copies ran while one was open for 19% -> 28% of each run, Pallas kernels for 0% -> 13%
where the time goes in v2:
time: 826 us; the launch traced here: 814 us
  matrix products  281 us (34%)
  other arithmetic  195 us (24%)
  Pallas kernels  111 us (13%)
  waiting for transfers between devices  84.6 us (10%)
  local copies, waits for them, and re-layouts  82.3 us (10%)
  starting transfers between devices  41.6 us (5%)
  between operations  18.1 us (2%)
    pallas_call x1, Pallas kernels, reduce_scatter(): pl.pallas_call(functools.partial(reduce_kernel, tuple(groups), small is n...  105 us
    all_gather x1, waiting for transfers between devices, local(): lax.all_gather(square_master.astype(jnp.bfloat16), AXES, axis=1, tiled=True)  64.5 us
    dot_general x18, matrix products, matmul3(): return jnp.matmul(left, right, precision=lax.Precision.HIGH)  58.9 us
    dot_general x6, matrix products, attend(): return round_gradient(jnp.einsum('bhqk,bkhe->bqhe', weights, values))  38.8 us
    reduce_sum x3, other arithmetic, norm_rows(): center = values - jnp.mean(values, axis=-1, keepdims=True)  38.1 us
    convert_element_type x7, other arithmetic, round_gradient(): return wrapped(values)  37.7 us
    all_to_all x1, starting transfers between devices, from_owner_rows(): lax.all_to_all(rows_out.reshape(count, piece, D), AXES, 0, 0, tiled=True)  35.9 us
    dot_general x6, matrix products, attend(): scores = jnp.einsum('bqhe,bkhe->bhqk', query, keys) + bias  30.4 us
  transfers between devices with their start and end apart: 5, of which 3 were waited for; matrix products, arithmetic and copies ran while one was open for 28% of the time, Pallas kernels for 13%

profile of v2, /device:TPU:0, one launch (start us, length us, event | category | flops | bytes accessed | tf_op | source)
XLA Modules:
  0.0 813.8 jit_solution(16308235563026572719)
XLA Ops:
  31.7 64.5 %all-gather.3.cloned.1.call-done = bf16[8,768,768]{2,1,0:T(8,128)(2,1)} async-done(((bf16[8,24,768]{2,1,0:T(8,128)(2,1)}), bf16[8,768,768]{2,1,0:T(8,128)(2,1)}) %all-gather.3.cloned.1.call-update) | async-done | bytes 9437200 | tf_op jit(solution)/shard_map/all_gather | solution.py:547
  116.3 5.6 convert_reduce_fusion.4
  128.3 6.1 fusion.209
  154.6 5.3 convolution_convert_fusion.2
  164.5 5.3 select_reduce_fusion
  174.4 6.0 divide_convert_fusion
  180.4 5.2 add_convert_fusion.5
  190.5 7.8 bitcast_reduce_fusion
  212.5 13.1 %fusion.39 = (u8[128,3072]{1,0:T(8,128)(4,1)S(1)}, u8[128,3072]{1,0:T(8,128)(4,1)S(1)}, f32[8,128,3072]{2,1,0:T(8,128)}) fusion(f32[3072]{0:T(1024)S(1)} %bitcast.306, bf16[8,128,768]{2,1,0:T(8,128)(2,1)} %add_convert_fusion.9, bf16[2,3072,768]{2,1,0:T(8,128)(2,1)} %all-gather.5.cloned.1.call-done), kind=kOutput, calls=%fused_computation.136 | convolution fusion | flops 4875091968 | bytes 19673088 | tf_op jit(solution)/shard_map/jvp()/dot_general | solution.py:127
  225.6 35.1 %fusion.207 = (f32[8,128]{1,0:T(8,128)S(1)}, f32[8,128,3072]{2,1,0:T(8,128)S(1)}, f32[8,128,3072]{2,1,0:T(8,128)}) fusion(f32[8,128,3072]{2,1,0:T(8,128)} %get-tuple-element.103, f32[3072]{0:T(1024)S(1)} %bitcast.307, u8[128,3072]{1,0:T(8,128)(4,1)S(1)} %get-tuple-element.22, u8[128,3072]{1,0:T(8,128)(4,1)S(1)} %get-tuple-element.21), kind=kLoop, calls=%fused_computation.378 | loop fusion | flops 223345664 | bytes 38551552 | tf_op jit(solution)/shard_map/jvp()/reduce_sum | solution.py:63
  260.7 12.0 %multiply_reduce_fusion.2 = (f32[8,128]{1,0:T(8,128)S(1)}, f32[8,128]{1,0:T(8,128)S(1)}, f32[3072]{0:T(1024)}, f32[8,128,3072]{2,1,0:T(8,128)}) fusion(f32[8,128,3072]{2,1,0:T(8,128)S(1)} %get-tuple-element.75, f32[3072]{0:T(1024)S(1)} %bitcast.303, f32[8,128]{1,0:T(8,128)S(1)} %broadcast_multiply_fusion, bf16[8,128,768]{2,1,0:T(8,128)(2,1)S(1)} %copy-done.51, ...), kind=kOutput, calls=%fused_computation.17 | convolution fusion | flops 4853853184 | bytes 31494144 | tf_op jit(solution)/shard_map/transpose(jvp())/dot_general | solution.py:131
  272.8 7.6 multiply_reduce_fusion
  280.4 20.1 %add_convert_fusion.2 = (bf16[8,128,3072]{2,1,0:T(8,128)(2,1)}, bf16[8,128,3072]{2,1,0:T(8,128)(2,1)}) fusion(f32[8,128,3072]{2,1,0:T(8,128)} %get-tuple-element.76, f32[8,128,3072]{2,1,0:T(8,128)} %get-tuple-element.103, f32[8,128]{1,0:T(8,128)S(1)} %negate_multiply_fusion.6, f32[3072]{0:T(1024)S(1)} %bitcast.308, f32[8,128]{1,0:T(8,128)S(1)} %get-tuple-element.90, ...), kind=kLoop, calls=%fused_computation.16 | loop fusion | flops 81788928 | bytes 62967808 | tf_op jit(solution)/shard_map/transpose(jvp())/convert_element_type | solution.py:59
  305.0 7.0 convolution_bitcast_fusion
  312.1 8.3 %fusion.201 = (f32[768]{0:T(1024)}, f32[8,128]{1,0:T(8,128)S(1)}, f32[8,128,768]{2,1,0:T(8,128)S(1)}) fusion(f32[768]{0:T(1024)S(1)} %get-tuple-element.47, f32[8,128,768]{2,1,0:T(8,128)S(1)} %copy-done.16, f32[8,128]{1,0:T(8,128)S(1)} %broadcast_multiply_fusion.1, bf16[8,128,3072]{2,1,0:T(8,128)(2,1)S(1)} %copy-done.42, ...), kind=kOutput, calls=%fused_computation.373 | convolution fusion | flops 4835768320 | bytes 17315840 | tf_op jit(solution)/shard_map/transpose(jvp())/dot_general | solution.py:127
  324.6 5.4 convolution_bitcast_fusion.1
  347.6 6.0 convolution_convert_fusion.1
  353.6 11.0 %multiply_reduce_fusion.1 = (f32[8,12,128]{2,1,0:T(8,128)S(1)}, f32[8,12,128,256]{3,2,1,0:T(8,128)S(1)}) fusion(f32[8,12,128]{2,1,0:T(8,128)S(1)} %multiply_divide_fusion.1, f32[8,12,128]{2,1,0:T(8,128)S(1)} %get-tuple-element.97, f32[8,12,128,256]{3,2,1,0:T(8,128)} %copy-done.3, pred[8,256]{1,0:T(8,128)(4,1)S(1)} %iota_compare_fusion.10, ...), kind=kOutput, calls=%fused_computation.15 | convolution fusion | flops 418369536 | bytes 30033920 | tf_op jit(solution)/shard_map/transpose(jvp(bhqk,bkhe->bqhe))/dot_general | solution.py:73
  364.6 11.7 %convert_reduce_fusion.1 = (f32[8,12,128]{2,1,0:T(8,128)S(1)}, pred[8,12,128,256]{3,2,1,0:T(8,128)(4,1)}, f32[8,12,128]{2,1,0:T(8,128)S(1)}) fusion(f32[8,12,128]{2,1,0:T(8,128)S(1)} %get-tuple-element.97, f32[8,12,128,256]{3,2,1,0:T(8,128)S(1)} %bitcast.267, pred[8,256]{1,0:T(8,128)(4,1)S(1)} %iota_compare_fusion.10, f32[8,12,128]{2,1,0:T(8,128)S(1)} %neg.48, ...), kind=kLoop, calls=%fused_computation.13 | loop fusion | flops 28286976 | bytes 28559360 | tf_op jit(solution)/shard_map/jvp()/reduce_sum | solution.py:71
  376.3 10.1 %select_convert_fusion = bf16[8,12,128,256]{3,2,1,0:T(8,128)(2,1)} fusion(pred[8,12,128,256]{3,2,1,0:T(8,128)(4,1)} %get-tuple-element.73, f32[8,12,128]{2,1,0:T(8,128)S(1)} %negate_divide_fusion.1, pred[8,256]{1,0:T(8,128)(4,1)S(1)} %iota_compare_fusion.10, f32[8,12,128]{2,1,0:T(8,128)S(1)} %get-tuple-element.97, f32[8,12,128,256]{3,2,1,0:T(8,128)S(1)} %bitcast.267, ...), kind=kLoop, calls=%fused_computation.12 | loop fusion | flops 28311552 | bytes 34801664 | tf_op jit(solution)/shard_map/transpose(jvp())/convert_element_type | solution.py:59
  386.4 7.1 convolution_convert_fusion.6
  469.8 6.4 convolution_convert_fusion
  502.1 105.1 %shard_map.212 = (f32[8,24,768]{2,1,0:T(8,128)}, f32[192,128]{1,0:T(8,128)}) custom-call(bf16[8,4,2,2,48,768]{5,4,3,2,1,0:T(8,128)(2,1)} %bitcast.272, f32[192,128]{1,0:T(8,128)} %bitcast.302), custom_call_target="tpu_custom_call" | custom-call | tf_op jit(solution)/shard_map/pallas_call | solution.py:367
  618.8 7.7 fusion.137
  634.7 5.6 all-to-all-start
  643.0 8.4 %add_convert_fusion.4 = bf16[8,256,768]{2,1,0:T(8,128)(2,1)} fusion(f32[8,256,768]{2,1,0:T(8,128)} %fusion.137, bf16[8,256,768]{1,2,0:T(8,128)(2,1)} %bitcast.291, bf16[8,768,768]{2,1,0:T(8,128)(2,1)} %all-gather.3.cloned.1.call-done), kind=kOutput, calls=%fused_computation.42 | convolution fusion | flops 2419064832 | bytes 13762560 | tf_op jit(solution)/shard_map/transpose(jvp())/dot_general | solution.py:109
  651.4 9.4 %all-to-all-done = bf16[32,12,768]{2,1,0:T(8,128)(2,1)} async-done(((bf16[32,12,768]{2,1,0:T(8,128)(2,1)}), bf16[32,12,768]{2,1,0:T(8,128)(2,1)}, u32[]{:S(2)}, u32[]{:S(2)}) %all-to-all-start) | async-done | bytes 589856 | tf_op jit(solution)/shard_map/all_to_all | solution.py:478
  663.1 5.8 shard_map.213
  671.8 6.5 fusion.40
  739.7 35.9 %all-to-all-start.1 = ((bf16[32,12,768]{2,1,0:T(8,128)(2,1)}), bf16[32,12,768]{2,1,0:T(8,128)(2,1)}, u32[]{:S(2)}, u32[]{:S(2)}) async-start(bf16[32,12,768]{2,1,0:T(8,128)(2,1)} %reshape.484), calls=%async_computation.2 | async-start | bytes 1572864 | tf_op jit(solution)/shard_map/all_to_all | solution.py:491
  775.7 9.9 %add_convert_fusion.8 = bf16[8,128,768]{2,1,0:T(8,128)(2,1)} fusion(f32[8,128,768]{2,1,0:T(8,128)} %copy-done.15, bf16[8,128,3072]{2,1,0:T(8,128)(2,1)} %get-tuple-element.81, bf16[2,3072,768]{2,1,0:T(8,128)(2,1)} %all-gather.5.cloned.1.call-done, f32[768]{0:T(1024)S(1)} %copy-done.116), kind=kOutput, calls=%fused_computation.123 | convolution fusion | flops 4834197504 | bytes 15731712 | tf_op jit(solution)/shard_map/jvp()/dot_general | solution.py:131
  785.6 10.7 %all-to-all-done.1 = bf16[32,12,768]{2,1,0:T(8,128)(2,1)} async-done(((bf16[32,12,768]{2,1,0:T(8,128)(2,1)}), bf16[32,12,768]{2,1,0:T(8,128)(2,1)}, u32[]{:S(2)}, u32[]{:S(2)}) %all-to-all-start.1) | async-done | bytes 589856 | tf_op jit(solution)/shard_map/all_to_all | solution.py:491
  (457 shorter events, 324.2 us)
Async XLA Ops:
  7.2 147.4 %copy-start = (bf16[8,256,768]{2,1,0:T(8,128)(2,1)S(1)}, bf16[8,256,768]{2,1,0:T(8,128)(2,1)}, u32[]{:S(2)}) copy-start(bf16[8,256,768]{2,1,0:T(8,128)(2,1)} %param.14) | copy-start | bytes 9437188
  7.2 89.0 %all-gather.3.cloned.1.call-start = ((), (), s32[]{:S(2)}) async-start(), calls=%async_computation.3 | async-start | bytes 9732096 | tf_op jit(solution)/shard_map/all_gather | solution.py:547
  9.2 203.3 %all-gather.5.cloned.1.call-start = ((), (), s32[]{:S(2)}) async-start(), calls=%async_computation.4 | async-start | bytes 9732096 | tf_op jit(solution)/shard_map/all_gather | solution.py:548
  11.1 617.7 %reduce-scatter.2.cloned.1.call-start = ((), (), s32[]{:S(2)}) async-start(), calls=%async_computation.5 | async-start | bytes 9732096 | tf_op jit(solution)/shard_map/reduce_scatter | solution.py:583
  12.7 128.0 %copy-start.93 = (f32[768]{0:T(1024)}, f32[768]{0:T(1024)S(1)}, u32[]{:S(2)}) copy-start(f32[768]{0:T(1024)S(1)} %get-tuple-element.57) | copy-start | bytes 9220
  12.7 132.9 %copy-start.104 = (f32[768]{0:T(1024)}, f32[768]{0:T(1024)S(1)}, u32[]{:S(2)}) copy-start(f32[768]{0:T(1024)S(1)} %get-tuple-element.53) | copy-start | bytes 9220
  16.4 9.9 %copy-start.106 = (f32[8,128]{1,0:T(8,128)}, f32[8,128]{1,0:T(8,128)S(1)}, u32[]{:S(2)}) copy-start(f32[8,128]{1,0:T(8,128)S(1)} %fusion.26) | copy-start | bytes 12292
  16.5 9.9 %copy-start.123 = (bf16[12]{0:T(256)(128)(2,1)S(1)}, bf16[12]{0:T(256)(128)(2,1)}, u32[]{:S(2)}) copy-start(bf16[12]{0:T(256)(128)(2,1)} %param.24) | copy-start | bytes 76
  16.5 9.9 %copy-start.120 = (s32[8]{0:T(128)S(1)}, s32[8]{0:T(128)}, u32[]{:S(2)}) copy-start(s32[8]{0:T(128)} %param.16) | copy-start | bytes 100
  23.9 7.7 copy-start.121
  23.9 7.8 copy-start.97
  26.4 101.9 %copy-start.117 = (f32[12]{0:T(128)}, f32[12]{0:T(128)S(1)}, u32[]{:S(2)}) copy-start(f32[12]{0:T(128)S(1)} %convert_element_type.254) | copy-start | bytes 148
  26.4 74.0 %copy-start.100 = (f32[8,128]{1,0:T(8,128)}, f32[8,128]{1,0:T(8,128)S(1)}, u32[]{:S(2)}) copy-start(f32[8,128]{1,0:T(8,128)S(1)} %fusion.146) | copy-start | bytes 12292
  31.6 83.8 %copy-start.75 = (pred[128,128]{0,1:T(8,128)(4,1)}, pred[128,128]{0,1:T(8,128)(4,1)S(1)}, u32[]{:S(2)}) copy-start(pred[128,128]{0,1:T(8,128)(4,1)S(1)} %iota_compare_fusion.9) | copy-start | bytes 49156
  225.6 35.2 %copy-start.51 = (bf16[8,128,768]{2,1,0:T(8,128)(2,1)S(1)}, bf16[8,128,768]{2,1,0:T(8,128)(2,1)}, u32[]{:S(2)}) copy-start(bf16[8,128,768]{2,1,0:T(8,128)(2,1)} %copy-done.50) | copy-start | bytes 4718596
  305.0 7.1 copy-start.16
  353.6 11.0 %slice-start = ((s8[12582912]{0:T(1024)(128)(4,1)}), s8[4194304]{0:T(1024)(128)(4,1)S(1)}, s32[]{:S(2)}) async-start(s8[12582912]{0:T(1024)(128)(4,1)} %bitcast.266), calls=%async_computation.6 | async-start | bytes 8388608
  353.6 11.0 %slice-start.1 = ((s8[12582912]{0:T(1024)(128)(4,1)}), s8[4194304]{0:T(1024)(128)(4,1)S(1)}, s32[]{:S(2)}) async-start(s8[12582912]{0:T(1024)(128)(4,1)} %bitcast.266), calls=%async_computation.7 | async-start | bytes 8388608
  353.6 11.0 %slice-start.2 = ((s8[12582912]{0:T(1024)(128)(4,1)}), s8[4194304]{0:T(1024)(128)(4,1)S(1)}, s32[]{:S(2)}) async-start(s8[12582912]{0:T(1024)(128)(4,1)} %bitcast.266), calls=%async_computation.8 | async-start | bytes 8388608
  416.3 7.8 copy-start.45
  420.6 8.1 slice-start.3
  469.7 8.7 %copy-start.79 = (f32[13056]{0:T(1024)S(1)}, f32[13056]{0:T(1024)}, u32[]{:S(2)}) copy-start(f32[13056]{0:T(1024)} %reshape.478) | copy-start | bytes 156676
  469.7 8.7 %copy-start.82 = (f32[9216]{0:T(1024)S(1)}, f32[9216]{0:T(1024)}, u32[]{:S(2)}) copy-start(f32[9216]{0:T(1024)} %reshape.479) | copy-start | bytes 110596
  469.8 8.7 %copy-start.119 = (f32[12]{0:T(128)S(1)}, f32[12]{0:T(128)}, u32[]{:S(2)}) copy-start(f32[12]{0:T(128)} %get-tuple-element.83) | copy-start | bytes 148
  618.7 7.7 copy-start.14
  618.7 7.7 copy-start.18
  618.7 7.7 copy-start.35
  618.7 7.7 copy-start.41
  618.7 7.7 copy-start.99
  634.7 26.2 %all-to-all-start = ((bf16[32,12,768]{2,1,0:T(8,128)(2,1)}), bf16[32,12,768]{2,1,0:T(8,128)(2,1)}, u32[]{:S(2)}, u32[]{:S(2)}) async-start(bf16[32,12,768]{2,1,0:T(8,128)(2,1)} %pad_maximum_fusion), calls=%async_computation.1 | async-start | bytes 1572864 | tf_op jit(solution)/shard_map/all_to_all | solution.py:478
  735.1 40.6 %copy-start.116 = (f32[768]{0:T(1024)S(1)}, f32[768]{0:T(1024)}, u32[]{:S(2)}) copy-start(f32[768]{0:T(1024)} %get-tuple-element.45) | copy-start | bytes 9220
  739.7 56.5 %all-to-all-start.1 = ((bf16[32,12,768]{2,1,0:T(8,128)(2,1)}), bf16[32,12,768]{2,1,0:T(8,128)(2,1)}, u32[]{:S(2)}, u32[]{:S(2)}) async-start(bf16[32,12,768]{2,1,0:T(8,128)(2,1)} %reshape.484), calls=%async_computation.2 | async-start | bytes 1572864 | tf_op jit(solution)/shard_map/all_to_all | solution.py:491
  (104 other events, 330.9 us)
Sparse Core Ops, SparseCore 0:
  11.5 84.5 all-gather.2
  99.7 80.6 all-gather.4
  439.3 160.0 reduce-scatter.1

commit v3 on v2

--- a/solution.py
+++ b/solution.py
@@ -23,112 +23,414 @@
 NEGATIVE_LARGE = -1e30
 
 
-def plain_round(values):
-    return lax.optimization_barrier(values.astype(jnp.bfloat16)).astype(jnp.float32)
-
-
-def same_value(values):
-    return values
-
-
-def value_keep(values):
-    return (plain_round(values), None)
-
-
-def value_pass(kept, slope):
-    return (slope,)
-
-
-def gradient_keep(values):
-    return (values, None)
-
-
-def gradient_round(kept, slope):
-    return (plain_round(slope),)
-
-
-def round_value(values):
-    wrapped = jax.custom_vjp(plain_round)
-    wrapped.defvjp(value_keep, value_pass)
-    return wrapped(values)
-
-
-def round_gradient(values):
-    wrapped = jax.custom_vjp(same_value)
-    wrapped.defvjp(gradient_keep, gradient_round)
-    return wrapped(values)
-
-
-def norm_rows(values, gain, shift):
+F32, BF16 = jnp.float32, jnp.bfloat16
+TOKENS = 256
+SLOTS = 512
+LANES = 128
+
+
+def times(left, right):
+    return jnp.dot(left, right, preferred_element_type=F32)
+
+
+def times_back(left, right):
+    return lax.dot_general(left, right, (((1,), (1,)), ((), ())), preferred_element_type=F32)
+
+
+def times_down(left, right):
+    return lax.dot_general(left, right, (((0,), (0,)), ((), ())), preferred_element_type=F32)
+
+
+def standard(values):
     center = values - jnp.mean(values, axis=-1, keepdims=True)
-    spread = jnp.mean(center * center, axis=-1, keepdims=True)
-    return center * lax.rsqrt(spread + NORM_EPSILON) * gain + shift
-
-
-def attend(query, keys, values, allowed, bias):
-    scores = jnp.einsum("bqhe,bkhe->bhqk", query, keys) + bias
-    scores = jnp.where(allowed, round_gradient(scores), NEGATIVE_LARGE)
+    scale = lax.rsqrt(jnp.mean(center * center, axis=-1, keepdims=True) + NORM_EPSILON)
+    return center * scale, scale
+
+
+def norm(values, gain, shift):
+    return standard(values)[0] * gain + shift
+
+
+def norm_back(values, slope, gain):
+    hat, scale = standard(values)
+    inner = slope * gain
+    back = scale * (
+        inner
+        - jnp.mean(inner, axis=-1, keepdims=True)
+        - hat * jnp.mean(inner * hat, axis=-1, keepdims=True)
+    )
+    return back, down(slope * hat), down(slope)
+
+
+def down(values):
+    return jnp.sum(values, axis=0, keepdims=True)
+
+
+def head_masks():
+    lane = lax.broadcasted_iota(jnp.int32, (1, LANES), 1)
+    even = jnp.where(lane < LANES // 2, 1.0, 0.0)
+    return even.astype(BF16), (1.0 - even).astype(BF16)
+
+
+def stacked(pair, masks):
+    return jnp.concatenate([pair * masks[0], pair * masks[1]], axis=0)
+
+
+def side_by_side(rows):
+    half = rows.shape[0] // 2
+    return jnp.concatenate([rows[:half], rows[half:]], axis=1)
+
+
+def soften(scores):
     weights = jnp.exp(scores - jnp.max(scores, axis=-1, keepdims=True))
-    weights = round_value(weights / jnp.sum(weights, axis=-1, keepdims=True))
-    return round_gradient(jnp.einsum("bhqk,bkhe->bqhe", weights, values))
-
-
-def split_heads(values, head_count):
-    return values.reshape(
-        values.shape[0], values.shape[1], head_count, values.shape[2] // head_count
-    )
-
-
-def attention_block(inputs, memory, memory_len, square, vectors, head_scale, relative):
-    item_count, query_count, model_width = inputs.shape
-    head_count = head_scale.shape[0]
-    memory_slots = memory.shape[1]
-    normed = round_value(norm_rows(inputs, vectors[0], vectors[1]))
-    query = round_gradient(round_value((jnp.matmul(normed, square[0]) + vectors[2]) * 0.125))
-    keys = round_gradient(round_value(jnp.matmul(normed, square[1])))
-    values = round_gradient(round_value(jnp.matmul(normed, square[2]) + vectors[3]))
-    query_index = jnp.arange(query_count)[:, None]
-    key_index = jnp.arange(query_count)[None, :]
-    distance = jnp.clip(query_index - key_index, 0, query_count - 1)
-    position_table = (distance[:, :, None] == jnp.arange(query_count)[None, None, :]).astype(
-        jnp.float32
-    )
-    bias = jnp.einsum("hd,qkd->hqk", relative, position_table)[None]
-    mixed = attend(
-        split_heads(query, head_count),
-        split_heads(keys, head_count),
-        split_heads(values, head_count),
-        (query_index >= key_index)[None, None],
-        bias,
-    )
-    mixed = (mixed * head_scale[None, None, :, None]).reshape(item_count, query_count, model_width)
-    mixed = round_value(norm_rows(mixed, vectors[5], vectors[6]))
-    hidden = inputs + round_gradient(jnp.matmul(mixed, square[3]) + vectors[4])
-    normed = round_value(norm_rows(hidden, vectors[7], vectors[8]))
-    query = round_gradient(round_value((jnp.matmul(normed, square[4]) + vectors[9]) * 0.125))
-    keys = round_gradient(round_value(jnp.matmul(memory, square[5])))
-    values = round_gradient(round_value(jnp.matmul(memory, square[6]) + vectors[10]))
-    allowed = (jnp.arange(memory_slots)[None, :] < memory_len[:, None])[:, None, None, :]
-    mixed = attend(
-        split_heads(query, head_count),
-        split_heads(keys, head_count),
-        split_heads(values, head_count),
-        allowed,
-        0.0,
-    )
-    mixed = round_value(
-        norm_rows(mixed.reshape(item_count, query_count, model_width), vectors[12], vectors[13])
-    )
-    return hidden + round_gradient(jnp.matmul(mixed, square[7]) + vectors[11])
-
-
-def feed_block(hidden, tall, vectors, feed_vectors):
-    normed = round_value(norm_rows(hidden, vectors[14], vectors[15]))
-    inner = round_gradient(jnp.matmul(normed, tall[0].T) + feed_vectors[0])
-    active = round_value(
-        norm_rows(jax.nn.gelu(inner, approximate=False), feed_vectors[1], feed_vectors[2])
-    )
-    return hidden + round_gradient(jnp.matmul(active, tall[1]) + vectors[16])
+    return (weights * (1.0 / jnp.sum(weights, axis=-1, keepdims=True))).astype(BF16)
+
+
+def soften_back(weights, slope):
+    weights = weights.astype(F32)
+    product = weights * slope
+    return (product - weights * jnp.sum(product, axis=-1, keepdims=True)).astype(BF16)
+
+
+def attention_kernel(
+    memory_len, x_in, memory, w, vec, hs, bias,
+    n1, q, k, v, p, o, m1, h1, n2, cq, ck, cv, pc, co, m2, h2,
+):
+    step = pl.program_id(0)
+    masks = head_masks()
+    x = x_in[...].astype(F32)
+    n1[...] = norm(x, vec[0:1], vec[1:2]).astype(BF16)
+    q[...] = ((times(n1[...], w[0]) + vec[2:3]) * 0.125).astype(BF16)
+    k[...] = times(n1[...], w[1]).astype(BF16)
+    v[...] = (times(n1[...], w[2]) + vec[3:4]).astype(BF16)
+    items = TOKENS // 128
+
+    @pl.loop(0, 6)
+    def _(pair):
+        lanes = pl.ds(pl.multiple_of(pair * LANES, LANES), LANES)
+        for item in range(items):
+            rows = slice(item * 128, item * 128 + 128)
+            scores = times_back(stacked(q[rows, lanes], masks), k[rows, lanes]) + bias[pair]
+            weights = soften(scores)
+            p[item, pair] = weights
+            o[rows, lanes] = times(side_by_side(weights), stacked(v[rows, lanes], masks))
+
+    m1[...] = norm(o[...] * hs[...], vec[5:6], vec[6:7]).astype(BF16)
+    h1[...] = x + (times(m1[...], w[3]) + vec[4:5])
+    n2[...] = norm(h1[...], vec[7:8], vec[8:9]).astype(BF16)
+    cq[...] = ((times(n2[...], w[4]) + vec[9:10]) * 0.125).astype(BF16)
+    ck[...] = times(memory[...], w[5]).astype(BF16)
+    cv[...] = (times(memory[...], w[6]) + vec[10:11]).astype(BF16)
+    slots = SLOTS // items
+    column = lax.broadcasted_iota(jnp.int32, (1, slots), 1)
+
+    @pl.loop(0, 6)
+    def _(pair):
+        lanes = pl.ds(pl.multiple_of(pair * LANES, LANES), LANES)
+        for item in range(items):
+            rows = slice(item * 128, item * 128 + 128)
+            keys = slice(item * slots, item * slots + slots)
+            limit = memory_len[step * items + item]
+            scores = times_back(stacked(cq[rows, lanes], masks), ck[keys, lanes])
+            weights = soften(jnp.where(column < limit, scores, NEGATIVE_LARGE))
+            pc[item, pair] = weights
+            co[rows, lanes] = times(side_by_side(weights), stacked(cv[keys, lanes], masks))
+
+    m2[...] = norm(co[...], vec[12:13], vec[13:14]).astype(BF16)
+    h2[...] = h1[...] + (times(m2[...], w[7]) + vec[11:12])
+
+
+def whole(shape):
+    return pl.BlockSpec(shape, lambda *_: (0,) * len(shape), pipeline_mode=pl.Buffered(1))
+
+
+def by_rows(rows, width):
+    return pl.BlockSpec((rows, width), lambda i: (i, 0))
+
+
+def by_items(items, *rest):
+    return pl.BlockSpec((items,) + rest, lambda i: (i,) + (0,) * len(rest))
+
+
+def attention_forward(inputs, memory, memory_len, square, vectors, head_row, bias):
+    tokens, width = inputs.shape
+    slots = memory.shape[0]
+    steps = tokens // TOKENS
+    items = TOKENS // 128
+    shapes = [
+        (BF16, "t"), (BF16, "t"), (BF16, "t"), (BF16, "t"), (BF16, "p"), (F32, "t"), (BF16, "t"), (F32, "t"),
+        (BF16, "t"), (BF16, "t"), (BF16, "m"), (BF16, "m"), (BF16, "c"), (F32, "t"), (BF16, "t"), (F32, "t"),
+    ]
+    full = {"t": (tokens, width), "m": (slots, width), "p": (steps * items, 6, 256, 128), "c": (steps * items, 6, 256, SLOTS // items)}
+    spec = {
+        "t": by_rows(TOKENS, width), "m": by_rows(SLOTS, width),
+        "p": by_items(items, 6, 256, 128), "c": by_items(items, 6, 256, SLOTS // items),
+    }
+    return pl.pallas_call(
+        attention_kernel,
+        grid=(steps,),
+        out_shape=tuple(jax.ShapeDtypeStruct(full[kind], kept) for kept, kind in shapes),
+        in_specs=[
+            pl.BlockSpec(memory_space=pltpu.SMEM),
+            spec["t"], spec["m"], whole(square.shape), whole(vectors.shape), whole(head_row.shape), whole(bias.shape),
+        ],
+        out_specs=tuple(spec[kind] for _, kind in shapes),
+        compiler_params=pltpu.CompilerParams(vmem_limit_bytes=60 << 20),
+        cost_estimate=pl.CostEstimate(flops=14_000_000_000, bytes_accessed=60_000_000, transcendentals=5_000_000),
+    )(memory_len, inputs, memory, square, vectors, head_row, bias)
+
+
+ROOT_HALF = 0.7071067811865476
+INVERSE_ROOT = 0.3989422804014327
+CHUNK = 512
+
+
+def feed_kernel(
+    lengths, h2_in, cot, tall, vec, feed,
+    out, dh2, n3, r, du, dy, dvec, dfeed,
+    u, g, dr, total,
+):
+    step = pl.program_id(0)
+    items = TOKENS // 128
+    width = tall.shape[1]
+    chunks = width // CHUNK
+
+    @pl.when(step == 0)
+    def _():
+        dvec[...] = jnp.zeros_like(dvec)
+        dfeed[...] = jnp.zeros_like(dfeed)
+
+    h2 = h2_in[...]
+    n3[...] = norm(h2, vec[14:15], vec[15:16]).astype(BF16)
+
+    def at(i):
+        return pl.ds(pl.multiple_of(i * CHUNK, CHUNK), CHUNK)
+
+    def first(i, total):
+        some = at(i)
+        inner = times_back(n3[...], tall[0, some]) + feed[0:1, some]
+        bell = 0.5 + 0.5 * lax.erf(inner * ROOT_HALF)
+        active = inner * bell
+        g[:, some] = active
+        u[:, some] = bell + inner * (jnp.exp(-0.5 * inner * inner) * INVERSE_ROOT)
+        return total + jnp.sum(active, axis=-1, keepdims=True)
+
+    zero = jnp.zeros((TOKENS, 1), F32)
+    mean = lax.fori_loop(0, chunks, first, zero) * (1.0 / width)
+
+    def second(i, total):
+        center = g[:, at(i)] - mean
+        return total + jnp.sum(center * center, axis=-1, keepdims=True)
+
+    spread = lax.fori_loop(0, chunks, second, zero) * (1.0 / width)
+    scale = lax.rsqrt(spread + NORM_EPSILON)
+    row = lax.broadcasted_iota(jnp.int32, (128, 1), 0)
+    valid = jnp.concatenate(
+        [jnp.where(row < lengths[step * items + item], 1.0, 0.0) for item in range(items)], axis=0
+    )
+    dy32 = cot[...].astype(F32) * valid
+    dy[...] = dy32.astype(BF16)
+    total[...] = h2 + vec[16:17]
+
+    def third(i, sums):
+        some = at(i)
+        hat = (g[:, some] - mean) * scale
+        g[:, some] = hat
+        gain = feed[1:2, some]
+        active = (hat * gain + feed[2:3, some]).astype(BF16)
+        r[:, some] = active
+        total[...] += times(active, tall[1, some])
+        slope = times_back(dy[...], tall[1, some])
+        dfeed[1:2, some] += down(slope * hat)
+        dfeed[2:3, some] += down(slope)
+        inner = slope * gain
+        dr[:, some] = inner
+        return (
+            sums[0] + jnp.sum(inner, axis=-1, keepdims=True),
+            sums[1] + jnp.sum(inner * hat, axis=-1, keepdims=True),
+        )
+
+    one, two = lax.fori_loop(0, chunks, third, (zero, zero))
+    out[...] = total[...].astype(BF16)
+    one, two = one * (1.0 / width), two * (1.0 / width)
+    dh2[...] = jnp.zeros_like(dh2)
+
+    def fourth(i, carry):
+        some = at(i)
+        back = scale * (dr[:, some] - one - g[:, some] * two)
+        slope = (back * u[:, some]).astype(BF16)
+        du[:, some] = slope
+        dfeed[0:1, some] += down(slope.astype(F32))
+        dh2[...] += times(slope, tall[0, some])
+        return carry
+
+    lax.fori_loop(0, chunks, fourth, 0)
+    back, gain_sum, shift_sum = norm_back(h2, dh2[...], vec[14:15])
+    dvec[0:1] += gain_sum
+    dvec[1:2] += shift_sum
+    dvec[2:3] += down(dy32)
+    dh2[...] = dy32 + back
+
+
+def feed_both(hidden, cotangent, lengths, tall, vectors, feed_vectors):
+    tokens, width = hidden.shape
+    wide = tall.shape[1]
+    steps = tokens // TOKENS
+    some = by_rows(TOKENS, width)
+    much = by_rows(TOKENS, wide)
+    return pl.pallas_call(
+        feed_kernel,
+        grid=(steps,),
+        out_shape=(
+            jax.ShapeDtypeStruct((tokens, width), BF16),
+            jax.ShapeDtypeStruct((tokens, width), F32),
+            jax.ShapeDtypeStruct((tokens, width), BF16),
+            jax.ShapeDtypeStruct((tokens, wide), BF16),
+            jax.ShapeDtypeStruct((tokens, wide), BF16),
+            jax.ShapeDtypeStruct((tokens, width), BF16),
+            jax.ShapeDtypeStruct((3, width), F32),
+            jax.ShapeDtypeStruct((3, wide), F32),
+        ),
+        in_specs=[
+            pl.BlockSpec(memory_space=pltpu.SMEM),
+            some, some, whole(tall.shape), whole(vectors.shape), whole(feed_vectors.shape),
+        ],
+        out_specs=(
+            some, some, some, much, much, some,
+            pl.BlockSpec((3, width), lambda i: (0, 0)),
+            pl.BlockSpec((3, wide), lambda i: (0, 0)),
+        ),
+        scratch_shapes=[pltpu.VMEM((TOKENS, wide), F32)] * 3 + [pltpu.VMEM((TOKENS, width), F32)],
+        compiler_params=pltpu.CompilerParams(vmem_limit_bytes=60 << 20),
+        cost_estimate=pl.CostEstimate(flops=20_000_000_000, bytes_accessed=40_000_000, transcendentals=7_000_000),
+    )(lengths, hidden, cotangent, tall, vectors, feed_vectors)
+
+
+def attention_back_kernel(
+    x_in, dh2, w, vec, hs,
+    q, k, v, p, o, h1, cq, ck, cv, pc, co,
+    dx, dmem, dy2, dcq, dck, dcv, dy1, dq, dk, dv, dvec, drel,
+    do, dh1, dbias,
+):
+    step = pl.program_id(0)
+    masks = head_masks()
+    items = TOKENS // 128
+    slots = SLOTS // items
+
+    @pl.when(step == 0)
+    def _():
+        dvec[...] = jnp.zeros_like(dvec)
+        dbias[...] = jnp.zeros_like(dbias)
+
+    def note(row, value):
+        dvec[row : row + 1] += value
+
+    dy2[...] = dh2[...].astype(BF16)
+    note(11, down(dy2[...].astype(F32)))
+    back, gain_sum, shift_sum = norm_back(co[...], times_back(dy2[...], w[7]), vec[12:13])
+    note(12, gain_sum)
+    note(13, shift_sum)
+    do[...] = back.astype(BF16)
+
+    def through(pair, item, keys, query, key, value, weights, dquery, dkey, dvalue, with_bias):
+        lanes = pl.ds(pl.multiple_of(pair * LANES, LANES), LANES)
+        rows = slice(item * 128, item * 128 + 128)
+        kept = weights[item, pair]
+        grad = stacked(do[rows, lanes], masks)
+        dvalue[keys, lanes] = times_down(kept, grad).astype(BF16)
+        slope = soften_back(kept, times_back(grad, value[keys, lanes]))
+        dquery[rows, lanes] = (
+            times(side_by_side(slope), stacked(key[keys, lanes], masks)).astype(BF16) * 0.125
+        ).astype(BF16)
+        dkey[keys, lanes] = times_down(slope, stacked(query[rows, lanes], masks)).astype(BF16)
+        if with_bias:
+            dbias[pair] += slope.astype(F32)
+
+    @pl.loop(0, 6)
+    def _(pair):
+        for item in range(items):
+            keys = slice(item * slots, item * slots + slots)
+            through(pair, item, keys, cq, ck, cv, pc, dcq, dck, dcv, False)
+
+    note(9, down(dcq[...].astype(F32)))
+    note(10, down(dcv[...].astype(F32)))
+    dmem[...] = (times_back(dck[...], w[5]) + times_back(dcv[...], w[6])).astype(BF16)
+    back, gain_sum, shift_sum = norm_back(h1[...], times_back(dcq[...], w[4]), vec[7:8])
+    note(7, gain_sum)
+    note(8, shift_sum)
+    dh1[...] = dh2[...] + back
+    dy1[...] = dh1[...].astype(BF16)
+    note(4, down(dy1[...].astype(F32)))
+    back, gain_sum, shift_sum = norm_back(o[...] * hs[...], times_back(dy1[...], w[3]), vec[5:6])
+    note(5, gain_sum)
+    note(6, shift_sum)
+    note(17, down(back * o[...]))
+    do[...] = (back * hs[...]).astype(BF16)
+
+    @pl.loop(0, 6)
+    def _(pair):
+        for item in range(items):
+            rows = slice(item * 128, item * 128 + 128)
+            through(pair, item, rows, q, k, v, p, dq, dk, dv, True)
+
+    note(2, down(dq[...].astype(F32)))
+    note(3, down(dv[...].astype(F32)))
+    slope = times_back(dq[...], w[0]) + times_back(dk[...], w[1]) + times_back(dv[...], w[2])
+    back, gain_sum, shift_sum = norm_back(x_in[...].astype(F32), slope, vec[0:1])
+    note(0, gain_sum)
+    note(1, shift_sum)
+    dx[...] = (dh1[...] + back).astype(BF16)
+
+    @pl.when(step == pl.num_programs(0) - 1)
+    def _():
+        row = lax.broadcasted_iota(jnp.int32, (128, 128), 0)
+        column = lax.broadcasted_iota(jnp.int32, (128, 128), 1)
+        mirror = jnp.where(row + column == 127, 1.0, 0.0).astype(BF16)
+        for head in range(12):
+            part = dbias[head // 2, (head % 2) * 128 : (head % 2) * 128 + 128]
+            high = part.astype(BF16)
+            rest = part - high.astype(F32)
+            middle = rest.astype(BF16)
+            low = (rest - middle.astype(F32)).astype(BF16)
+            flipped = times(high, mirror) + times(middle, mirror) + times(low, mirror)
+            drel[head : head + 1] = down(pltpu.roll(flipped, 0, 1, stride=1, stride_axis=0))
+
+
+def attention_backward(inputs, dh2, square, vectors, head_row, kept):
+    tokens, width = inputs.shape
+    q, k, v, p, o, h1, cq, ck, cv, pc, co = kept
+    steps = tokens // TOKENS
+    items = TOKENS // 128
+    slots = ck.shape[0]
+    t, m = by_rows(TOKENS, width), by_rows(SLOTS, width)
+    ps, cs = by_items(items, 6, 256, 128), by_items(items, 6, 256, SLOTS // items)
+    token = jax.ShapeDtypeStruct((tokens, width), BF16)
+    slot = jax.ShapeDtypeStruct((slots, width), BF16)
+    return pl.pallas_call(
+        attention_back_kernel,
+        grid=(steps,),
+        out_shape=(
+            token, slot, token, token, slot, slot, token, token, token, token,
+            jax.ShapeDtypeStruct((18, width), F32),
+            jax.ShapeDtypeStruct((12, 128), F32),
+        ),
+        in_specs=[
+            t, t, whole(square.shape), whole(vectors.shape), whole(head_row.shape),
+            t, t, t, ps, t, t, t, m, m, cs, t,
+        ],
+        out_specs=(
+            t, m, t, t, m, m, t, t, t, t,
+            pl.BlockSpec((18, width), lambda i: (0, 0)),
+            pl.BlockSpec((12, 128), lambda i: (0, 0)),
+        ),
+        scratch_shapes=[
+            pltpu.VMEM((TOKENS, width), BF16),
+            pltpu.VMEM((TOKENS, width), F32),
+            pltpu.VMEM((6, 256, 128), F32),
+        ],
+        compiler_params=pltpu.CompilerParams(vmem_limit_bytes=60 << 20),
+        cost_estimate=pl.CostEstimate(flops=16_000_000_000, bytes_accessed=60_000_000, transcendentals=0),
+    )(inputs, dh2, square, vectors, head_row, q, k, v, p, o, h1, cq, ck, cv, pc, co)
 
 
 AXES = ("tall", "square", "row")
@@ -547,47 +849,48 @@
         lax.all_gather(square_master.astype(jnp.bfloat16), AXES, axis=1, tiled=True),
         lax.all_gather(tall_master.astype(jnp.bfloat16), AXES, axis=1, tiled=True),
     )
-    params = (
-        square_copy.astype(jnp.float32),
-        tall_copy.astype(jnp.float32),
-        vectors.astype(jnp.float32),
-        feed_vectors.astype(jnp.float32),
-        head_scale.astype(jnp.float32),
-        relative.astype(jnp.float32),
-    )
-
-    square, tall, gains, feed_gains, scales, biases = params
-
-    def attention(square, gains, scales, biases, inputs_full, memory_full):
-        return attention_block(
-            inputs_full, memory_full, memory_len, square, gains, scales, biases
+    width = inputs.shape[2]
+    vec, feed = vectors.astype(F32), feed_vectors.astype(F32)
+    head_row = jnp.repeat(head_scale.astype(F32), width // head_scale.shape[0])[None]
+    at = jnp.arange(inputs.shape[1])
+    distance = at[:, None] - at[None, :]
+    table = (jnp.maximum(distance, 0)[:, :, None] == at[None, None, :]).astype(BF16)
+    bias = jnp.einsum("hd,qkd->hqk", relative, table, preferred_element_type=F32)
+    bias = jnp.where(distance >= 0, bias, NEGATIVE_LARGE).reshape(6, 256, 128)
+    flat_in, flat_memory = inputs.reshape(-1, width), memory.reshape(-1, width)
+    n1, q, k, v, p, o, m1, h1, n2, cq, ck, cv, pc, co, m2, h2 = attention_forward(
+        flat_in, flat_memory, memory_len, square_copy, vec, head_row, bias
+    )
+    output, dh2, n3, r, du, dy, late_slope, feed_slope = feed_both(
+        h2, cotangent.reshape(-1, width), lengths, tall_copy, vec, feed
+    )
+
+    def weight_slope(left, right):
+        return lax.dot_general(
+            left, right, (((0,), (0,)), ((), ())), preferred_element_type=F32
+        ).astype(BF16)
+
+    tall_slope = jnp.stack([weight_slope(du, n3), weight_slope(r, dy)])
+    tall_slope, dh2 = lax.optimization_barrier((tall_slope, dh2))
+    tall_sum = lax.psum_scatter(tall_slope, AXES, scatter_dimension=1, tiled=True).astype(F32)
+    input_slope, memory_slope, dy2, dcq, dck, dcv, dy1, dq, dk, dv, early_slope, bias_slope = (
+        attention_backward(
+            flat_in, dh2, square_copy, vec, head_row,
+            (q, k, v, p, o, h1, cq, ck, cv, pc, co),
         )
-
-    hidden, attention_back = jax.vjp(
-        attention,
-        square,
-        gains,
-        scales,
-        biases,
-        inputs.astype(jnp.float32),
-        memory.astype(jnp.float32),
-    )
-    output, feed_back = jax.vjp(feed_block, hidden, tall, gains, feed_gains)
-    valid = (jnp.arange(inputs.shape[1])[None, :] < lengths[:, None]).astype(jnp.float32)
-    hidden_slope, tall_slope, late_slope, feed_slope = feed_back(
-        cotangent.astype(jnp.float32) * valid[:, :, None]
-    )
-    tall_slope, hidden_slope = lax.optimization_barrier(
-        (tall_slope.astype(jnp.bfloat16), hidden_slope)
-    )
-    tall_sum = lax.psum_scatter(tall_slope, AXES, scatter_dimension=1, tiled=True).astype(
-        jnp.float32
-    )
-    square_slope, vector_slope, scale_slope, bias_slope, input_slope, memory_slope = (
-        attention_back(hidden_slope)
-    )
-    vector_slope = vector_slope + late_slope
-    square_slope = square_slope.astype(jnp.bfloat16)
+    )
+    square_slope = jnp.stack(
+        [
+            weight_slope(left, right)
+            for left, right in (
+                (n1, dq), (n1, dk), (n1, dv), (m1, dy1),
+                (n2, dcq), (flat_memory, dck), (flat_memory, dcv), (m2, dy2),
+            )
+        ]
+    )
+    vector_slope = jnp.concatenate([early_slope[:14], late_slope], axis=0)
+    scale_slope = jnp.sum(early_slope[17].reshape(head_scale.shape[0], -1), axis=1)
+    bias_slope = jnp.roll(bias_slope, 1, axis=1)
     small = [
         jnp.sum(lengths).astype(jnp.float32).reshape(1),
         scale_slope.reshape(-1),
@@ -635,9 +938,9 @@
         - LEARN_RATE * max(1.0, FF / D) ** 0.5 * tall
     )
     return (
-        output.astype(jnp.bfloat16),
-        input_slope.astype(jnp.bfloat16),
-        memory_slope.astype(jnp.bfloat16),
+        output.reshape(inputs.shape),
+        input_slope.reshape(inputs.shape),
+        memory_slope.reshape(memory.shape),
         square_state,
         tall_state,
         square_weight,

time: 826 us -> 627 us (0.76)
  matrix products: 281 us -> 90.2 us
  Pallas kernels: 111 us -> 292 us
  other arithmetic: 195 us -> 25.4 us
  local copies, waits for them, and re-layouts: 82.3 us -> 23.3 us
  waiting for transfers between devices: 84.6 us -> 111 us
  blocking collectives: 0 us -> 25.2 us
    pallas_call x0 -> x3, Pallas kernels: none -> 200 us  [the longest x1 72.2 us: attention_backward(): pl.pallas_call(attention_back_kernel, grid=(steps,), out_shape=(token, sl...]
    dot_general x44 -> x11, matrix products: 220 us -> 37.8 us  [the longest x10 32.6 us: weight_slope(): lax.dot_general(left, right, (((0,), (0,)), ((), ())), preferred_element_...]
    reduce_sum x28 -> x1, other arithmetic: 102 us -> 0.12 us  [local(): jnp.sum(early_slope[17].reshape(head_scale.shape[0], -1), axis=1)]
    convert_element_type x19 -> x2, other arithmetic: 61.3 us -> 1.27 us  [local(): vec, feed = (vectors.astype(F32), feed_vectors.astype(F32))]
    all_to_all x0 -> x1, blocking collectives: none -> 25.2 us  [to_owner_rows(): lax.all_to_all(pieces, AXES, 0, 0, tiled=True).reshape(count * piece, D)]
    optimization_barrier x8 -> x0, local copies, waits for them, and re-layouts: 25.1 us -> none  [the longest x6 19.9 us: plain_round(): lax.optimization_barrier(values.astype(jnp.bfloat16)).astype(jnp.float32)]
    pallas_call x1, Pallas kernels: 105 us -> 85.5 us  [reduce_scatter(): pl.pallas_call(functools.partial(reduce_kernel, tuple(groups), small is n...]
    all_gather x1, waiting for transfers between devices: 0.01 us -> 15.8 us  [local(): lax.all_gather(tall_master.astype(jnp.bfloat16), AXES, axis=1, tiled=True)]
  transfers between devices with their start and end apart: 5 -> 4, of which waited for: 3 -> 3; matrix products, arithmetic and copies ran while one was open for 28% -> 7% of each run, Pallas kernels for 13% -> 37%
where the time goes in v3:
time: 627 us; the launch traced here: 619 us
  Pallas kernels  292 us (47%)
  waiting for transfers between devices  111 us (18%)
  matrix products  90.2 us (14%)
  starting transfers between devices  35.6 us (6%)
  other arithmetic  25.4 us (4%)
  blocking collectives  25.2 us (4%)
  local copies, waits for them, and re-layouts  23.3 us (4%)
  between operations  16.8 us (3%)
    pallas_call x1, Pallas kernels, reduce_scatter(): pl.pallas_call(functools.partial(reduce_kernel, tuple(groups), small is n...  85.5 us
    all_gather x1, waiting for transfers between devices, local(): lax.all_gather(square_master.astype(jnp.bfloat16), AXES, axis=1, tiled=True)  76.8 us
    pallas_call x1, Pallas kernels, attention_backward(): pl.pallas_call(attention_back_kernel, grid=(steps,), out_shape=(token, sl...  72.2 us
    pallas_call x1, Pallas kernels, attention_forward(): pl.pallas_call(attention_kernel, grid=(steps,), out_shape=tuple((jax.Shap...  68.4 us
    pallas_call x1, Pallas kernels, feed_both(): pl.pallas_call(feed_kernel, grid=(steps,), out_shape=(jax.ShapeDtypeStruc...  59.6 us
    dot_general x18, matrix products, matmul3(): return jnp.matmul(left, right, precision=lax.Precision.HIGH)  51.5 us
    all_to_all x1, starting transfers between devices, from_owner_rows(): lax.all_to_all(rows_out.reshape(count, piece, D), AXES, 0, 0, tiled=True)  35.5 us
    dot_general x10, matrix products, weight_slope(): lax.dot_general(left, right, (((0,), (0,)), ((), ())), preferred_element_...  32.6 us
  transfers between devices with their start and end apart: 4, of which 3 were waited for; matrix products, arithmetic and copies ran while one was open for 7% of the time, Pallas kernels for 37%

profile of v3, /device:TPU:0, one launch (start us, length us, event | category | flops | bytes accessed | tf_op | source)
XLA Modules:
  0.0 618.5 jit_solution(11000882852713081779)
XLA Ops:
  13.1 5.3 fusion.38
  19.5 76.8 %all-gather.3.cloned.1.call-done.w = bf16[8,768,768]{2,1,0:T(8,128)(2,1)} async-done(((bf16[8,24,768]{2,1,0:T(8,128)(2,1)}), bf16[8,768,768]{2,1,0:T(8,128)(2,1)}) %all-gather.3.cloned.1.call-update) | async-done | bytes 9437200 | tf_op jit(solution)/shard_map/all_gather | solution.py:849
  96.4 68.4 %shard_map.212 = (bf16[1024,768]{1,0:T(8,128)(2,1)}, bf16[1024,768]{1,0:T(8,128)(2,1)}, bf16[1024,768]{1,0:T(8,128)(2,1)}, bf16[1024,768]{1,0:T(8,128)(2,1)}, bf...) custom-call(s32[8]{0:T(128)} %memory_len.1, ...), custom_call_target="tpu_custom_call" | custom-call | flops 14000000000 | bytes 60000000 | tf_op jit(solution)/shard_map/pallas_call | solution.py:169
  164.8 15.8 %all-gather.5.cloned.1.call-done.tall = bf16[2,3072,768]{2,1,0:T(8,128)(2,1)} async-done(((bf16[2,96,768]{2,1,0:T(8,128)(2,1)}), bf16[2,3072,768]{2,1,0:T(8,128)(2,1)}) %all-gather.5.cloned.1.call-update) | async-done | bytes 9437200 | tf_op jit(solution)/shard_map/all_gather | solution.py:850
  180.6 59.6 %shard_map.213 = (bf16[1024,768]{1,0:T(8,128)(2,1)}, f32[1024,768]{1,0:T(8,128)}, bf16[1024,768]{1,0:T(8,128)(2,1)}, bf16[1024,3072]{1,0:T(8,128)(2,1)}, bf16[10...) custom-call(s32[8]{0:T(128)} %lengths.1, ...), custom_call_target="tpu_custom_call" | custom-call | flops 20000000000 | bytes 40000000 | tf_op jit(solution)/shard_map/pallas_call | solution.py:281
  240.2 9.3 %fusion.1 = bf16[1,3072,768]{2,1,0:T(8,128)(2,1)} fusion(bf16[1024,3072]{1,0:T(8,128)(2,1)} %get-tuple-element.53, bf16[1024,768]{1,0:T(8,128)(2,1)} %get-tuple-element.54), kind=kOutput, calls=%fused_computation.10 | convolution fusion | flops 4834197504 | bytes 12582912 | tf_op jit(solution)/shard_map/dot_general | solution.py:869
  249.6 7.3 %fusion.2 = bf16[1,3072,768]{2,1,0:T(8,128)(2,1)} fusion(bf16[1024,3072]{1,0:T(8,128)(2,1)S(1)} %copy-done.25, bf16[1024,768]{1,0:T(8,128)(2,1)S(1)} %copy-done.26), kind=kOutput, calls=%fused_computation.11 | convolution fusion | flops 4834197504 | bytes 12582912 | tf_op jit(solution)/shard_map/dot_general | solution.py:869
  256.9 8.3 %pad_maximum_fusion = bf16[2,3072,768]{2,1,0:T(8,128)(2,1)} fusion(bf16[1,3072,768]{2,1,0:T(8,128)(2,1)} %fusion.2, bf16[1,3072,768]{2,1,0:T(8,128)(2,1)} %fusion.1), kind=kLoop, calls=%fused_computation | loop fusion | flops 4718592 | bytes 18874368 | tf_op jit(solution)/shard_map/stack | solution.py:873
  267.2 72.2 %shard_map.214 = (bf16[1024,768]{1,0:T(8,128)(2,1)}, bf16[2048,768]{1,0:T(8,128)(2,1)}, bf16[1024,768]{1,0:T(8,128)(2,1)}, bf16[1024,768]{1,0:T(8,128)(2,1)}, bf...) custom-call(bf16[1024,768]{1,0:T(8,128)(2,1)} %bitcast.103, ...), custom_call_target="tpu_custom_call" | custom-call | flops 16000000000 | bytes 60000000 | tf_op jit(solution)/shard_map/pallas_call | solution.py:409
  343.5 3.0 convolution_convert_fusion.9
  361.6 2.8 convolution_convert_fusion.4
  365.4 3.0 convolution_convert_fusion.3
  372.8 85.5 %shard_map.215 = (f32[8,24,768]{2,1,0:T(8,128)}, f32[192,128]{1,0:T(8,128)}) custom-call(bf16[8,4,2,2,48,768]{5,4,3,2,1,0:T(8,128)(2,1)} %constant_dynamic-update-slice_fusion.refs_0_, f32[192,128]{1,0:T(8,128)} %bitcast.91), custom_call_target="tpu_custom_call" | custom-call | tf_op jit(solution)/shard_map/pallas_call | solution.py:669
  460.3 2.0 fusion.129
  462.4 1.9 fusion.130
  464.5 25.2 %all_to_all.10 = bf16[32,12,768]{2,1,0:T(8,128)(2,1)S(1)} all-to-all(bf16[32,12,768]{2,1,0:T(8,128)(2,1)S(1)} %pad_maximum_fusion.1), channel_id=1, replica_groups=mesh['tall'=4,'square'=4,'row'=2] {'tall','square','row'}, dimensions={0} | all-to-all | bytes 1179648 | tf_op jit(solution)/shard_map/all_to_all | solution.py:780
  490.5 5.8 shard_map.216
  500.7 3.3 fusion.4
  504.0 3.2 fusion.13
  507.1 3.2 fusion.132
  512.2 3.6 fusion.133
  515.7 3.2 fusion.33
  520.8 3.2 fusion.31
  524.0 3.3 fusion.134
  527.4 3.2 fusion.27
  532.4 3.2 fusion.25
  535.6 3.1 fusion.135
  538.8 3.5 fusion.21
  544.0 3.2 fusion.19
  547.3 3.2 fusion.136
  553.3 35.5 %all-to-all-start.1 = ((bf16[32,12,768]{2,1,0:T(8,128)(2,1)}), bf16[32,12,768]{2,1,0:T(8,128)(2,1)S(1)}, u32[]{:S(2)}, u32[]{:S(2)}) async-start(bf16[32,12,768]{2,1,0:T(8,128)(2,1)} %reshape.140), calls=%async_computation.2 | async-start | bytes 1572864 | tf_op jit(solution)/shard_map/all_to_all | solution.py:793
  591.6 17.8 %all-to-all-done.1 = bf16[32,12,768]{2,1,0:T(8,128)(2,1)S(1)} async-done(((bf16[32,12,768]{2,1,0:T(8,128)(2,1)}), bf16[32,12,768]{2,1,0:T(8,128)(2,1)S(1)}, u32[]{:S(2)}, u32[]{:S(2)}) %all-to-all-start.1) | async-done | bytes 589856 | tf_op jit(solution)/shard_map/all_to_all | solution.py:793
  (122 shorter events, 53.8 us)
Async XLA Ops:
  7.2 5.9 copy-start
  7.2 3.8 copy-start.11
  7.2 4.6 copy-start.9
  7.2 5.2 copy-start.8
  7.2 89.1 %all-gather.3.cloned.1.call-start = ((), (), s32[]{:S(2)}) async-start(), calls=%async_computation.3 | async-start | bytes 9732096 | tf_op jit(solution)/shard_map/all_gather | solution.py:849
  9.1 171.5 %all-gather.5.cloned.1.call-start = ((), (), s32[]{:S(2)}) async-start(), calls=%async_computation.4 | async-start | bytes 9732096 | tf_op jit(solution)/shard_map/all_gather | solution.py:850
  11.0 451.4 %reduce-scatter.2.cloned.1.call-start = ((), (), s32[]{:S(2)}) async-start(), calls=%async_computation.5 | async-start | bytes 9732096 | tf_op jit(solution)/shard_map/reduce_scatter | solution.py:875
  240.2 9.3 %copy-start.25 = (bf16[1024,3072]{1,0:T(8,128)(2,1)S(1)}, bf16[1024,3072]{1,0:T(8,128)(2,1)}, u32[]{:S(2)}) copy-start(bf16[1024,3072]{1,0:T(8,128)(2,1)} %get-tuple-element.55) | copy-start | bytes 18874372
  240.2 9.3 %copy-start.26 = (bf16[1024,768]{1,0:T(8,128)(2,1)S(1)}, bf16[1024,768]{1,0:T(8,128)(2,1)}, u32[]{:S(2)}) copy-start(bf16[1024,768]{1,0:T(8,128)(2,1)} %get-tuple-element.56) | copy-start | bytes 4718596
  265.2 0.7 copy-start.13
  265.2 1.9 copy-start.7
  267.2 74.6 %copy-start.10 = (f32[3,768]{1,0:T(4,128)S(1)}, f32[3,768]{1,0:T(4,128)}, u32[]{:S(2)}) copy-start(f32[3,768]{1,0:T(4,128)} %get-tuple-element.86) | copy-start | bytes 27652
  267.2 76.3 %copy-start.17 = (bf16[1024,768]{1,0:T(8,128)(2,1)S(1)}, bf16[1024,768]{1,0:T(8,128)(2,1)}, u32[]{:S(2)}) copy-start(bf16[1024,768]{1,0:T(8,128)(2,1)} %get-tuple-element.72) | copy-start | bytes 4718596
  346.4 1.8 copy-start.22
  349.7 1.8 copy-start.21
  351.6 2.6 copy-start.20
  353.0 1.9 copy-start.16
  354.9 2.5 copy-start.19
  356.3 1.8 copy-start.15
  358.1 2.6 copy-start.12
  358.1 3.4 copy-start.24
  361.6 3.9 copy-start.23
  365.4 4.1 copy-start.18
  368.4 1.8 copy-start.14
  372.8 87.5 %copy-start.4 = (f32[8,24,768]{2,1,0:T(8,128)S(1)}, f32[8,24,768]{2,1,0:T(8,128)}, u32[]{:S(2)}) copy-start(f32[8,24,768]{2,1,0:T(8,128)} %param.20) | copy-start | bytes 1769476
  458.3 4.1 copy-start.5
  552.3 36.6 %copy-start.6 = (f32[192,128]{1,0:T(8,128)S(1)}, f32[192,128]{1,0:T(8,128)}, u32[]{:S(2)}) copy-start(f32[192,128]{1,0:T(8,128)} %get-tuple-element.88) | copy-start | bytes 294916
  553.3 56.1 %all-to-all-start.1 = ((bf16[32,12,768]{2,1,0:T(8,128)(2,1)}), bf16[32,12,768]{2,1,0:T(8,128)(2,1)S(1)}, u32[]{:S(2)}, u32[]{:S(2)}) async-start(bf16[32,12,768]{2,1,0:T(8,128)(2,1)} %reshape.140), calls=%async_computation.2 | async-start | bytes 1572864 | tf_op jit(solution)/shard_map/all_to_all | solution.py:793
  588.8 20.9 %copy-start.2 = (f32[2,96,768]{2,1,0:T(8,128)S(1)}, f32[2,96,768]{2,1,0:T(8,128)}, u32[]{:S(2)}) copy-start(f32[2,96,768]{2,1,0:T(8,128)} %param.19) | copy-start | bytes 1769476
  609.6 1.1 copy-start.3
  609.7 1.9 copy-start.1
Sparse Core Ops, SparseCore 0:
  11.6 84.7 all-gather.2
  99.9 80.6 all-gather.4
  265.3 138.9 reduce-scatter.1

commit v4 on v3

--- a/solution.py
+++ b/solution.py
@@ -94,18 +94,18 @@
 
 def attention_kernel(
     memory_len, x_in, memory, w, vec, hs, bias,
-    n1, q, k, v, p, o, m1, h1, n2, cq, ck, cv, pc, co, m2, h2,
+    left, q, k, v, p, o, h1, cq, ck, cv, pc, co, h2,
 ):
     step = pl.program_id(0)
     masks = head_masks()
     x = x_in[...].astype(F32)
-    n1[...] = norm(x, vec[0:1], vec[1:2]).astype(BF16)
-    q[...] = ((times(n1[...], w[0]) + vec[2:3]) * 0.125).astype(BF16)
-    k[...] = times(n1[...], w[1]).astype(BF16)
-    v[...] = (times(n1[...], w[2]) + vec[3:4]).astype(BF16)
+    left[0] = norm(x, vec[0:1], vec[1:2]).astype(BF16)
+    q[...] = ((times(left[0], w[0]) + vec[2:3]) * 0.125).astype(BF16)
+    k[...] = times(left[0], w[1]).astype(BF16)
+    v[...] = (times(left[0], w[2]) + vec[3:4]).astype(BF16)
     items = TOKENS // 128
 
-    @pl.loop(0, 6)
+    @pl.loop(0, 6, unroll=True)
     def _(pair):
         lanes = pl.ds(pl.multiple_of(pair * LANES, LANES), LANES)
         for item in range(items):
@@ -115,16 +115,16 @@
             p[item, pair] = weights
             o[rows, lanes] = times(side_by_side(weights), stacked(v[rows, lanes], masks))
 
-    m1[...] = norm(o[...] * hs[...], vec[5:6], vec[6:7]).astype(BF16)
-    h1[...] = x + (times(m1[...], w[3]) + vec[4:5])
-    n2[...] = norm(h1[...], vec[7:8], vec[8:9]).astype(BF16)
-    cq[...] = ((times(n2[...], w[4]) + vec[9:10]) * 0.125).astype(BF16)
+    left[1] = norm(o[...] * hs[...], vec[5:6], vec[6:7]).astype(BF16)
+    h1[...] = x + (times(left[1], w[3]) + vec[4:5])
+    left[2] = norm(h1[...], vec[7:8], vec[8:9]).astype(BF16)
+    cq[...] = ((times(left[2], w[4]) + vec[9:10]) * 0.125).astype(BF16)
     ck[...] = times(memory[...], w[5]).astype(BF16)
     cv[...] = (times(memory[...], w[6]) + vec[10:11]).astype(BF16)
     slots = SLOTS // items
     column = lax.broadcasted_iota(jnp.int32, (1, slots), 1)
 
-    @pl.loop(0, 6)
+    @pl.loop(0, 6, unroll=True)
     def _(pair):
         lanes = pl.ds(pl.multiple_of(pair * LANES, LANES), LANES)
         for item in range(items):
@@ -136,8 +136,8 @@
             pc[item, pair] = weights
             co[rows, lanes] = times(side_by_side(weights), stacked(cv[keys, lanes], masks))
 
-    m2[...] = norm(co[...], vec[12:13], vec[13:14]).astype(BF16)
-    h2[...] = h1[...] + (times(m2[...], w[7]) + vec[11:12])
+    left[3] = norm(co[...], vec[12:13], vec[13:14]).astype(BF16)
+    h2[...] = h1[...] + (times(left[3], w[7]) + vec[11:12])
 
 
 def whole(shape):
@@ -146,6 +146,10 @@
 
 def by_rows(rows, width):
     return pl.BlockSpec((rows, width), lambda i: (i, 0))
+
+
+def by_blocks(blocks, rows, width):
+    return pl.BlockSpec((blocks, rows, width), lambda i: (0, i, 0))
 
 
 def by_items(items, *rest):
@@ -158,11 +162,12 @@
     steps = tokens // TOKENS
     items = TOKENS // 128
     shapes = [
-        (BF16, "t"), (BF16, "t"), (BF16, "t"), (BF16, "t"), (BF16, "p"), (F32, "t"), (BF16, "t"), (F32, "t"),
-        (BF16, "t"), (BF16, "t"), (BF16, "m"), (BF16, "m"), (BF16, "c"), (F32, "t"), (BF16, "t"), (F32, "t"),
+        (BF16, "l"), (BF16, "t"), (BF16, "t"), (BF16, "t"), (BF16, "p"), (F32, "t"), (F32, "t"),
+        (BF16, "t"), (BF16, "m"), (BF16, "m"), (BF16, "c"), (F32, "t"), (F32, "t"),
     ]
-    full = {"t": (tokens, width), "m": (slots, width), "p": (steps * items, 6, 256, 128), "c": (steps * items, 6, 256, SLOTS // items)}
+    full = {"l": (4, tokens, width), "t": (tokens, width), "m": (slots, width), "p": (steps * items, 6, 256, 128), "c": (steps * items, 6, 256, SLOTS // items)}
     spec = {
+        "l": by_blocks(4, TOKENS, width),
         "t": by_rows(TOKENS, width), "m": by_rows(SLOTS, width),
         "p": by_items(items, 6, 256, 128), "c": by_items(items, 6, 256, SLOTS // items),
     }
@@ -182,12 +187,12 @@
 
 ROOT_HALF = 0.7071067811865476
 INVERSE_ROOT = 0.3989422804014327
-CHUNK = 512
+CHUNK = 1024
 
 
 def feed_kernel(
     lengths, h2_in, cot, tall, vec, feed,
-    out, dh2, n3, r, du, dy, dvec, dfeed,
+    out, dh2, narrow, wide, dvec, dfeed,
     u, g, dr, total,
 ):
     step = pl.program_id(0)
@@ -201,14 +206,14 @@
         dfeed[...] = jnp.zeros_like(dfeed)
 
     h2 = h2_in[...]
-    n3[...] = norm(h2, vec[14:15], vec[15:16]).astype(BF16)
+    narrow[0] = norm(h2, vec[14:15], vec[15:16]).astype(BF16)
 
     def at(i):
         return pl.ds(pl.multiple_of(i * CHUNK, CHUNK), CHUNK)
 
     def first(i, total):
         some = at(i)
-        inner = times_back(n3[...], tall[0, some]) + feed[0:1, some]
+        inner = times_back(narrow[0], tall[0, some]) + feed[0:1, some]
         bell = 0.5 + 0.5 * lax.erf(inner * ROOT_HALF)
         active = inner * bell
         g[:, some] = active
@@ -216,20 +221,20 @@
         return total + jnp.sum(active, axis=-1, keepdims=True)
 
     zero = jnp.zeros((TOKENS, 1), F32)
-    mean = lax.fori_loop(0, chunks, first, zero) * (1.0 / width)
+    mean = lax.fori_loop(0, chunks, first, zero, unroll=True) * (1.0 / width)
 
     def second(i, total):
         center = g[:, at(i)] - mean
         return total + jnp.sum(center * center, axis=-1, keepdims=True)
 
-    spread = lax.fori_loop(0, chunks, second, zero) * (1.0 / width)
+    spread = lax.fori_loop(0, chunks, second, zero, unroll=True) * (1.0 / width)
     scale = lax.rsqrt(spread + NORM_EPSILON)
     row = lax.broadcasted_iota(jnp.int32, (128, 1), 0)
     valid = jnp.concatenate(
         [jnp.where(row < lengths[step * items + item], 1.0, 0.0) for item in range(items)], axis=0
     )
     dy32 = cot[...].astype(F32) * valid
-    dy[...] = dy32.astype(BF16)
+    narrow[1] = dy32.astype(BF16)
     total[...] = h2 + vec[16:17]
 
     def third(i, sums):
@@ -238,9 +243,9 @@
         g[:, some] = hat
         gain = feed[1:2, some]
         active = (hat * gain + feed[2:3, some]).astype(BF16)
-        r[:, some] = active
+        wide[1, :, some] = active
         total[...] += times(active, tall[1, some])
-        slope = times_back(dy[...], tall[1, some])
+        slope = times_back(narrow[1], tall[1, some])
         dfeed[1:2, some] += down(slope * hat)
         dfeed[2:3, some] += down(slope)
         inner = slope * gain
@@ -250,7 +255,7 @@
             sums[1] + jnp.sum(inner * hat, axis=-1, keepdims=True),
         )
 
-    one, two = lax.fori_loop(0, chunks, third, (zero, zero))
+    one, two = lax.fori_loop(0, chunks, third, (zero, zero), unroll=True)
     out[...] = total[...].astype(BF16)
     one, two = one * (1.0 / width), two * (1.0 / width)
     dh2[...] = jnp.zeros_like(dh2)
@@ -259,12 +264,12 @@
         some = at(i)
         back = scale * (dr[:, some] - one - g[:, some] * two)
         slope = (back * u[:, some]).astype(BF16)
-        du[:, some] = slope
+        wide[0, :, some] = slope
         dfeed[0:1, some] += down(slope.astype(F32))
         dh2[...] += times(slope, tall[0, some])
         return carry
 
-    lax.fori_loop(0, chunks, fourth, 0)
+    lax.fori_loop(0, chunks, fourth, 0, unroll=True)
     back, gain_sum, shift_sum = norm_back(h2, dh2[...], vec[14:15])
     dvec[0:1] += gain_sum
     dvec[1:2] += shift_sum
@@ -277,17 +282,14 @@
     wide = tall.shape[1]
     steps = tokens // TOKENS
     some = by_rows(TOKENS, width)
-    much = by_rows(TOKENS, wide)
     return pl.pallas_call(
         feed_kernel,
         grid=(steps,),
         out_shape=(
             jax.ShapeDtypeStruct((tokens, width), BF16),
             jax.ShapeDtypeStruct((tokens, width), F32),
-            jax.ShapeDtypeStruct((tokens, width), BF16),
-            jax.ShapeDtypeStruct((tokens, wide), BF16),
-            jax.ShapeDtypeStruct((tokens, wide), BF16),
-            jax.ShapeDtypeStruct((tokens, width), BF16),
+            jax.ShapeDtypeStruct((2, tokens, width), BF16),
+            jax.ShapeDtypeStruct((2, tokens, wide), BF16),
             jax.ShapeDtypeStruct((3, width), F32),
             jax.ShapeDtypeStruct((3, wide), F32),
         ),
@@ -296,7 +298,7 @@
             some, some, whole(tall.shape), whole(vectors.shape), whole(feed_vectors.shape),
         ],
         out_specs=(
-            some, some, some, much, much, some,
+            some, some, by_blocks(2, TOKENS, width), by_blocks(2, TOKENS, wide),
             pl.BlockSpec((3, width), lambda i: (0, 0)),
             pl.BlockSpec((3, wide), lambda i: (0, 0)),
         ),
@@ -309,7 +311,7 @@
 def attention_back_kernel(
     x_in, dh2, w, vec, hs,
     q, k, v, p, o, h1, cq, ck, cv, pc, co,
-    dx, dmem, dy2, dcq, dck, dcv, dy1, dq, dk, dv, dvec, drel,
+    dx, dmem, right, far, dvec, drel,
     do, dh1, dbias,
 ):
     step = pl.program_id(0)
@@ -325,9 +327,9 @@
     def note(row, value):
         dvec[row : row + 1] += value
 
-    dy2[...] = dh2[...].astype(BF16)
-    note(11, down(dy2[...].astype(F32)))
-    back, gain_sum, shift_sum = norm_back(co[...], times_back(dy2[...], w[7]), vec[12:13])
+    right[5] = dh2[...].astype(BF16)
+    note(11, down(right[5].astype(F32)))
+    back, gain_sum, shift_sum = norm_back(co[...], times_back(right[5], w[7]), vec[12:13])
     note(12, gain_sum)
     note(13, shift_sum)
     do[...] = back.astype(BF16)
@@ -346,36 +348,36 @@
         if with_bias:
             dbias[pair] += slope.astype(F32)
 
-    @pl.loop(0, 6)
+    @pl.loop(0, 6, unroll=True)
     def _(pair):
         for item in range(items):
             keys = slice(item * slots, item * slots + slots)
-            through(pair, item, keys, cq, ck, cv, pc, dcq, dck, dcv, False)
-
-    note(9, down(dcq[...].astype(F32)))
-    note(10, down(dcv[...].astype(F32)))
-    dmem[...] = (times_back(dck[...], w[5]) + times_back(dcv[...], w[6])).astype(BF16)
-    back, gain_sum, shift_sum = norm_back(h1[...], times_back(dcq[...], w[4]), vec[7:8])
+            through(pair, item, keys, cq, ck, cv, pc, right.at[4], far.at[0], far.at[1], False)
+
+    note(9, down(right[4].astype(F32)))
+    note(10, down(far[1].astype(F32)))
+    dmem[...] = (times_back(far[0], w[5]) + times_back(far[1], w[6])).astype(BF16)
+    back, gain_sum, shift_sum = norm_back(h1[...], times_back(right[4], w[4]), vec[7:8])
     note(7, gain_sum)
     note(8, shift_sum)
     dh1[...] = dh2[...] + back
-    dy1[...] = dh1[...].astype(BF16)
-    note(4, down(dy1[...].astype(F32)))
-    back, gain_sum, shift_sum = norm_back(o[...] * hs[...], times_back(dy1[...], w[3]), vec[5:6])
+    right[3] = dh1[...].astype(BF16)
+    note(4, down(right[3].astype(F32)))
+    back, gain_sum, shift_sum = norm_back(o[...] * hs[...], times_back(right[3], w[3]), vec[5:6])
     note(5, gain_sum)
     note(6, shift_sum)
     note(17, down(back * o[...]))
     do[...] = (back * hs[...]).astype(BF16)
 
-    @pl.loop(0, 6)
+    @pl.loop(0, 6, unroll=True)
     def _(pair):
         for item in range(items):
             rows = slice(item * 128, item * 128 + 128)
-            through(pair, item, rows, q, k, v, p, dq, dk, dv, True)
-
-    note(2, down(dq[...].astype(F32)))
-    note(3, down(dv[...].astype(F32)))
-    slope = times_back(dq[...], w[0]) + times_back(dk[...], w[1]) + times_back(dv[...], w[2])
+            through(pair, item, rows, q, k, v, p, right.at[0], right.at[1], right.at[2], True)
+
+    note(2, down(right[0].astype(F32)))
+    note(3, down(right[2].astype(F32)))
+    slope = times_back(right[0], w[0]) + times_back(right[1], w[1]) + times_back(right[2], w[2])
     back, gain_sum, shift_sum = norm_back(x_in[...].astype(F32), slope, vec[0:1])
     note(0, gain_sum)
     note(1, shift_sum)
@@ -410,7 +412,9 @@
         attention_back_kernel,
         grid=(steps,),
         out_shape=(
-            token, slot, token, token, slot, slot, token, token, token, token,
+            token, slot,
+            jax.ShapeDtypeStruct((6, tokens, width), BF16),
+            jax.ShapeDtypeStruct((2, slots, width), BF16),
             jax.ShapeDtypeStruct((18, width), F32),
             jax.ShapeDtypeStruct((12, 128), F32),
         ),
@@ -419,7 +423,7 @@
             t, t, t, ps, t, t, t, m, m, cs, t,
         ],
         out_specs=(
-            t, m, t, t, m, m, t, t, t, t,
+            t, m, by_blocks(6, TOKENS, width), by_blocks(2, SLOTS, width),
             pl.BlockSpec((18, width), lambda i: (0, 0)),
             pl.BlockSpec((12, 128), lambda i: (0, 0)),
         ),
@@ -431,6 +435,47 @@
         compiler_params=pltpu.CompilerParams(vmem_limit_bytes=60 << 20),
         cost_estimate=pl.CostEstimate(flops=16_000_000_000, bytes_accessed=60_000_000, transcendentals=0),
     )(inputs, dh2, square, vectors, head_row, q, k, v, p, o, h1, cq, ck, cv, pc, co)
+
+
+def slope_kernel(left, right, memory, far, out):
+    step = pl.program_id(0)
+    width = out.shape[1]
+
+    def product(from_left, from_right):
+        @pl.loop(0, width // 256)
+        def _(tile):
+            some = pl.ds(pl.multiple_of(tile * 256, 256), 256)
+            out[0, some] = times_down(from_left[:, some], from_right[...]).astype(BF16)
+
+    @pl.when(step < 6)
+    def _():
+        product(left.at[0], right.at[0])
+
+    @pl.when(step >= 6)
+    def _():
+        product(memory, far.at[0])
+
+
+def square_slopes(left, right, memory, far):
+    _, tokens, width = left.shape
+    slots = memory.shape[0]
+    return pl.pallas_call(
+        slope_kernel,
+        grid=(8,),
+        out_shape=jax.ShapeDtypeStruct((8, width, width), BF16),
+        in_specs=[
+            pl.BlockSpec((1, tokens, width), lambda g: (jnp.clip(g - 2, 0, 3), 0, 0)),
+            pl.BlockSpec((1, tokens, width), lambda g: (jnp.minimum(g, 5), 0, 0)),
+            whole(memory.shape),
+            pl.BlockSpec((1, slots, width), lambda g: (jnp.maximum(g - 6, 0), 0, 0)),
+        ],
+        out_specs=pl.BlockSpec(
+            (1, width, width),
+            lambda g: (jnp.where(g < 5, g, jnp.where(g == 5, 7, g - 1)), 0, 0),
+        ),
+        compiler_params=pltpu.CompilerParams(vmem_limit_bytes=60 << 20),
+        cost_estimate=pl.CostEstimate(flops=12_000_000_000, bytes_accessed=30_000_000, transcendentals=0),
+    )(left, right, memory, far)
 
 
 AXES = ("tall", "square", "row")
@@ -512,19 +557,17 @@
             pass
 
     plans = []
-    for g, (pieces, rows, width, by_column) in enumerate(groups):
+    for g, (pieces, rows, width, parts) in enumerate(groups):
         r0, r1, r2, r3, f3, r4, send, recv = refs[8 * g : 8 * g + 8]
-        plans.append((pieces, rows, width, by_column, ins[g], outs[g], r0, r1, r2, r3, f3, r4, send, recv))
+        plans.append((pieces, rows, width, parts, ins[g], outs[g], r0, r1, r2, r3, f3, r4, send, recv))
 
     def where(plan, order, i):
-        pieces, by_column, width = plan[0], plan[3], plan[2]
+        pieces, parts, width = plan[0], plan[3], plan[2]
         j = i + order * (pieces // 2)
-        if by_column:
-            return j, order, pl.multiple_of(i * width, 128)
-        return j, j, 0
+        return j, lax.div(j, parts), pl.multiple_of(lax.rem(j, parts) * width, 128)
 
     def copies(plan, stage, order, i):
-        pieces, rows, width, by_column, src, out, r0, r1, r2, r3, f3, r4, send, recv = plan
+        pieces, rows, width, parts, src, out, r0, r1, r2, r3, f3, r4, send, recv = plan
         j, matrix, column = where(plan, order, i)
         first = "xy"[order]
 
@@ -541,20 +584,20 @@
             part = r0.at[j, :, :, 1 - x] if order == 0 else r0.at[j, :, 1 - y]
             return [make(part, r1.at[j], 1, across[first])]
         if stage == 2:
+            part = r1.at[j, :, 1 - y] if order == 0 else r1.at[j, :, 1 - x]
+            return [make(part, r2.at[j], 2, across["yx"[order]])]
+        if stage == 3:
             return [
-                make(r1.at[j, lax.rem(z + k + 1, 4)], r2.at[j, k], 2 + k, along[k])
+                make(r2.at[j, lax.rem(z + k + 1, 4)], r3.at[j, k], 3 + k, along[k])
                 for k in range(3)
             ]
-        if stage == 3:
-            part = r2.at[j, 0, 1 - y] if order == 0 else r2.at[j, 0, 1 - x]
-            return [make(part, r3.at[j], 5, across["yx"[order]])]
         share = rows // 2
         return [make(f3.at[j, pl.ds(pl.multiple_of(other * share, 8), share)], r4.at[j], 6, sibling)]
 
     f32 = jnp.float32
 
     def add(plan, stage, order, i):
-        pieces, rows, width, by_column, src, out, r0, r1, r2, r3, f3, r4, send, recv = plan
+        pieces, rows, width, parts, src, out, r0, r1, r2, r3, f3, r4, send, recv = plan
         j, matrix, column = where(plan, order, i)
         if stage == 0:
             lanes = pl.ds(pl.multiple_of(mine + column, 128), width)
@@ -572,14 +615,14 @@
                 own = r0[j, a, b, x] if order == 0 else r0[j, a, y, b]
                 r1[j, a, b] = (r1[j, a, b].astype(f32) + own.astype(f32)).astype(jnp.bfloat16)
         elif stage == 2:
-            for b in range(2):
-                r2[j, 0, b] = (
-                    (r2[j, 0, b].astype(f32) + r2[j, 1, b].astype(f32))
-                    + (r2[j, 2, b].astype(f32) + r1[j, z, b].astype(f32))
-                ).astype(jnp.bfloat16)
+            @pl.loop(0, 4)
+            def _(a):
+                own = r1[j, a, y] if order == 0 else r1[j, a, x]
+                r2[j, a] = (r2[j, a].astype(f32) + own.astype(f32)).astype(jnp.bfloat16)
         elif stage == 3:
-            own = r2[j, 0, y] if order == 0 else r2[j, 0, x]
-            f3[j] = r3[j].astype(f32) + own.astype(f32)
+            f3[j] = (r3[j, 0].astype(f32) + r3[j, 1].astype(f32)) + (
+                r3[j, 2].astype(f32) + r2[j, z].astype(f32)
+            )
         else:
             share = rows // 2
             lanes = pl.ds(pl.multiple_of(mine + column, 128), width)
@@ -600,16 +643,13 @@
 
         each(plan, body)
 
-    def step(plan, stage):
-        def body(order, i):
-            for copy in copies(plan, stage, order, i):
-                copy.wait_recv()
-            add(plan, stage, order, i)
-            if stage < 4:
-                for copy in copies(plan, stage + 1, order, i):
-                    copy.start()
-
-        each(plan, body)
+    def step(plan, stage, order, i):
+        for copy in copies(plan, stage, order, i):
+            copy.wait_recv()
+        add(plan, stage, order, i)
+        if stage < 4:
+            for copy in copies(plan, stage + 1, order, i):
+                copy.start()
 
     def finish(plan, stage):
         def body(order, i):
@@ -620,11 +660,23 @@
 
     for plan in plans:
         start(plan, 0)
-    for stage in range(5):
-        if stage < 4:
-            small_step(stage)
-        for plan in plans:
-            step(plan, stage)
+    for plan in plans:
+        turns = plan[0] // 2
+
+        @pl.loop(0, turns + 4)
+        def _(turn):
+            for stage in range(5):
+                @pl.when((turn >= stage) & (turn < turns + stage))
+                def _():
+                    for order in range(2):
+                        step(plan, stage, order, turn - stage)
+
+            if plan is plans[0]:
+                for stage in range(4):
+                    @pl.when(turn == stage)
+                    def _():
+                        small_step(stage)
+
     for stage in range(5):
         for plan in plans:
             finish(plan, stage)
@@ -634,7 +686,7 @@
                 copy.wait_send()
 
 
-def reduce_scatter(arrays, small, collective_id):
+def reduce_scatter(arrays, small, collective_id, split=1):
     groups, views, outs, scratch = [], [], [], []
     bf16, f32 = jnp.bfloat16, jnp.float32
     if small is not None:
@@ -647,16 +699,16 @@
     for array in arrays:
         matrices, height, width_all = array.shape
         rows = height // 16
-        by_column = matrices == 2
-        pieces, width = (6, 128) if by_column else (matrices, 384)
-        groups.append((pieces, rows, width, by_column))
+        parts = 3 if matrices == 2 else split
+        pieces, width = matrices * parts, 384 // parts
+        groups.append((pieces, rows, width, parts))
         views.append(array.reshape(matrices, 4, 2, 2, rows, width_all))
         outs.append(jax.ShapeDtypeStruct((matrices, rows // 2, width_all), f32))
         scratch += [
             pltpu.VMEM((pieces, 4, 2, 2, rows, width), bf16),
             pltpu.VMEM((pieces, 4, 2, rows, width), bf16),
-            pltpu.VMEM((pieces, 3, 2, rows, width), bf16),
-            pltpu.VMEM((pieces, rows, width), bf16),
+            pltpu.VMEM((pieces, 4, rows, width), bf16),
+            pltpu.VMEM((pieces, 3, rows, width), bf16),
             pltpu.VMEM((pieces, rows, width), f32),
             pltpu.VMEM((pieces, rows // 2, width), f32),
             pltpu.SemaphoreType.DMA((7, pieces)),
@@ -676,6 +728,126 @@
             collective_id=collective_id, has_side_effects=True, vmem_limit_bytes=60 << 20
         ),
     )(*views)
+
+
+def gather_kernel(split, own, full, theirs, send, recv):
+    z, y, x, core = place()
+    other = 1 - core
+    sibling = device(z, y, x, other)
+    across = {"x": device(z, y, 1 - x, core), "y": device(z, 1 - y, x, core)}
+    along = [device(lax.rem(z + k, 4), y, x, core) for k in (1, 2, 3)]
+    greet([sibling, across["x"], across["y"]] + along)
+    matrices, share, width = own.shape
+    half = width // 2
+    pieces, thin = matrices * split, half // split
+
+    def spot(j):
+        column = lax.rem(j, split) * thin
+        return (
+            lax.div(j, split),
+            pl.ds(pl.multiple_of(core * half + column, 128), thin),
+            pl.ds(pl.multiple_of(other * half + column, 128), thin),
+        )
+
+    def make(source, target, slot, j, partner):
+        return pltpu.make_async_remote_copy(
+            source, target, send.at[slot, j], recv.at[slot, j], device_id=partner, device_id_type=MESH
+        )
+
+    def copies(stage, order, i):
+        j = i + order * (pieces // 2)
+        m, mine, rest = spot(j)
+        first = "yx"[order]
+        if stage == 0:
+            return [make(own.at[m, :, rest], theirs.at[j], 0, j, sibling)]
+        if stage == 1:
+            part = full.at[m, z, y, x, :, mine]
+            return [make(part, part, 1 + k, j, along[k]) for k in range(3)]
+        if stage == 2:
+            part = full.at[m, :, y, x, :, mine]
+            return [make(part, part, 4, j, across[first])]
+        if stage == 3:
+            part = full.at[m, :, :, x, :, mine] if order == 0 else full.at[m, :, y, :, :, mine]
+            return [make(part, part, 5, j, across["xy"[order]])]
+        part = full.at[m, :, :, :, :, mine]
+        return [make(part, part, 6, j, sibling)]
+
+    def each(body):
+        @pl.loop(0, pieces // 2)
+        def _(i):
+            for order in range(2):
+                body(order, i)
+
+    def start(stage):
+        def body(order, i):
+            for copy in copies(stage, order, i):
+                copy.start()
+
+        each(body)
+
+    def step(stage, order, i):
+        for copy in copies(stage, order, i):
+            copy.wait_recv()
+        if stage == 0:
+            j = i + order * (pieces // 2)
+            m, mine, _ = spot(j)
+
+            @pl.when(core == 0)
+            def _():
+                full[m, z, y, x, :, mine] = jnp.concatenate(
+                    [own[m, :, mine], theirs[j]], axis=0
+                ).astype(jnp.bfloat16)
+
+            @pl.when(core == 1)
+            def _():
+                full[m, z, y, x, :, mine] = jnp.concatenate(
+                    [theirs[j], own[m, :, mine]], axis=0
+                ).astype(jnp.bfloat16)
+        if stage < 4:
+            for copy in copies(stage + 1, order, i):
+                copy.start()
+
+    def finish(stage):
+        def body(order, i):
+            for copy in copies(stage, order, i):
+                copy.wait_send()
+
+        each(body)
+
+    start(0)
+    turns = pieces // 2
+
+    @pl.loop(0, turns + 4)
+    def _(turn):
+        for stage in range(5):
+            @pl.when((turn >= stage) & (turn < turns + stage))
+            def _():
+                for order in range(2):
+                    step(stage, order, turn - stage)
+
+    for stage in range(5):
+        finish(stage)
+
+
+def gather_rows(own, collective_id, split=1):
+    matrices, share, width = own.shape
+    pieces = matrices * split
+    vmem = pl.BlockSpec(memory_space=pltpu.VMEM)
+    full = pl.pallas_call(
+        functools.partial(gather_kernel, split),
+        out_shape=jax.ShapeDtypeStruct((matrices, 4, 2, 2, 2 * share, width), jnp.bfloat16),
+        in_specs=[vmem],
+        out_specs=vmem,
+        scratch_shapes=[
+            pltpu.VMEM((pieces, share, width // 2 // split), jnp.float32),
+            pltpu.SemaphoreType.DMA((7, pieces)),
+            pltpu.SemaphoreType.DMA((7, pieces)),
+        ],
+        compiler_params=pltpu.CompilerParams(
+            collective_id=collective_id, has_side_effects=True, vmem_limit_bytes=32 << 20
+        ),
+    )(own)
+    return full.reshape(matrices, 32 * share, width)
 
 
 def gram_kernel(gram, out, other_sum, half_a, half_b, final, send, recv):
@@ -845,10 +1017,13 @@
     count = lax.axis_size(AXES)
     kernels = count == 32
     index = lax.axis_index(AXES)
-    square_copy, tall_copy = (
-        lax.all_gather(square_master.astype(jnp.bfloat16), AXES, axis=1, tiled=True),
-        lax.all_gather(tall_master.astype(jnp.bfloat16), AXES, axis=1, tiled=True),
-    )
+    if kernels:
+        square_copy = gather_rows(square_master, 3, 3)
+    else:
+        square_copy = lax.all_gather(
+            square_master.astype(jnp.bfloat16), AXES, axis=1, tiled=True
+        )
+    tall_copy = lax.all_gather(tall_master.astype(jnp.bfloat16), AXES, axis=1, tiled=True)
     width = inputs.shape[2]
     vec, feed = vectors.astype(F32), feed_vectors.astype(F32)
     head_row = jnp.repeat(head_scale.astype(F32), width // head_scale.shape[0])[None]
@@ -858,36 +1033,20 @@
     bias = jnp.einsum("hd,qkd->hqk", relative, table, preferred_element_type=F32)
     bias = jnp.where(distance >= 0, bias, NEGATIVE_LARGE).reshape(6, 256, 128)
     flat_in, flat_memory = inputs.reshape(-1, width), memory.reshape(-1, width)
-    n1, q, k, v, p, o, m1, h1, n2, cq, ck, cv, pc, co, m2, h2 = attention_forward(
+    left, q, k, v, p, o, h1, cq, ck, cv, pc, co, h2 = attention_forward(
         flat_in, flat_memory, memory_len, square_copy, vec, head_row, bias
     )
-    output, dh2, n3, r, du, dy, late_slope, feed_slope = feed_both(
+    output, dh2, narrow, wide, late_slope, feed_slope = feed_both(
         h2, cotangent.reshape(-1, width), lengths, tall_copy, vec, feed
     )
 
-    def weight_slope(left, right):
-        return lax.dot_general(
-            left, right, (((0,), (0,)), ((), ())), preferred_element_type=F32
-        ).astype(BF16)
-
-    tall_slope = jnp.stack([weight_slope(du, n3), weight_slope(r, dy)])
+    tall_slope = jnp.einsum("btf,btd->bfd", wide, narrow, preferred_element_type=F32).astype(BF16)
     tall_slope, dh2 = lax.optimization_barrier((tall_slope, dh2))
     tall_sum = lax.psum_scatter(tall_slope, AXES, scatter_dimension=1, tiled=True).astype(F32)
-    input_slope, memory_slope, dy2, dcq, dck, dcv, dy1, dq, dk, dv, early_slope, bias_slope = (
-        attention_backward(
-            flat_in, dh2, square_copy, vec, head_row,
-            (q, k, v, p, o, h1, cq, ck, cv, pc, co),
-        )
-    )
-    square_slope = jnp.stack(
-        [
-            weight_slope(left, right)
-            for left, right in (
-                (n1, dq), (n1, dk), (n1, dv), (m1, dy1),
-                (n2, dcq), (flat_memory, dck), (flat_memory, dcv), (m2, dy2),
-            )
-        ]
-    )
+    input_slope, memory_slope, right, far, early_slope, bias_slope = attention_backward(
+        flat_in, dh2, square_copy, vec, head_row, (q, k, v, p, o, h1, cq, ck, cv, pc, co)
+    )
+    square_slope = square_slopes(left, right, flat_memory, far)
     vector_slope = jnp.concatenate([early_slope[:14], late_slope], axis=0)
     scale_slope = jnp.sum(early_slope[17].reshape(head_scale.shape[0], -1), axis=1)
     bias_slope = jnp.roll(bias_slope, 1, axis=1)

time: 627 us -> 529 us (0.84)
  waiting for transfers between devices: 111 us -> 17.9 us
  Pallas kernels: 292 us -> 321 us
  matrix products: 90.2 us -> 73.9 us
  other arithmetic: 25.4 us -> 17.9 us
  local copies, waits for them, and re-layouts: 23.3 us -> 16 us
    pallas_call x0 -> x2, Pallas kernels: none -> 97 us  [the longest x1 72.8 us: gather_rows(): pl.pallas_call(functools.partial(gather_kernel, split), out_shape=jax.Sha...]
    all_gather x1 -> x0, waiting for transfers between devices: 76.8 us -> none  [local(): lax.all_gather(square_master.astype(jnp.bfloat16), AXES, axis=1, tiled=True)]
    pallas_call x1, Pallas kernels: 68.4 us -> 37.9 us  [attention_forward(): pl.pallas_call(attention_kernel, grid=(steps,), out_shape=tuple((jax.Shap...]
    pallas_call x1, Pallas kernels: 59.6 us -> 38.6 us  [feed_both(): pl.pallas_call(feed_kernel, grid=(steps,), out_shape=(jax.ShapeDtypeStruc...]
    dot_general x10 -> x1, matrix products: 32.6 us -> 16.3 us  [local(): jnp.einsum('btf,btd->bfd', wide, narrow, preferred_element_type=F32)]
    all_gather x1, waiting for transfers between devices: 15.8 us -> 0.02 us  [local(): lax.all_gather(tall_master.astype(jnp.bfloat16), AXES, axis=1, tiled=True)]
    pallas_call x1, Pallas kernels: 72.2 us -> 63.8 us  [attention_backward(): pl.pallas_call(attention_back_kernel, grid=(steps,), out_shape=(token, sl...]
    another operation x3 -> x2, other arithmetic: 12.2 us -> 3.88 us  [the longest x1 8.29 us: local(): tall_slope = jnp.stack([weight_slope(du, n3), weight_slope(r, dy)])]
  transfers between devices with their start and end apart: 4 -> 3, of which waited for: 3 -> 1; matrix products, arithmetic and copies ran while one was open for 7% -> 4% of each run, Pallas kernels for 37% -> 53%
where the time goes in v4:
time: 529 us; the launch traced here: 522 us
  Pallas kernels  321 us (61%)
  matrix products  73.9 us (14%)
  starting transfers between devices  35.6 us (7%)
  blocking collectives  23.6 us (4%)
  other arithmetic  17.9 us (3%)
  waiting for transfers between devices  17.9 us (3%)
  between operations  16.8 us (3%)
  local copies, waits for them, and re-layouts  16 us (3%)
    pallas_call x1, Pallas kernels, reduce_scatter(): pl.pallas_call(functools.partial(reduce_kernel, tuple(groups), small is n...  77.5 us
    pallas_call x1, Pallas kernels, gather_rows(): pl.pallas_call(functools.partial(gather_kernel, split), out_shape=jax.Sha...  72.8 us
    pallas_call x1, Pallas kernels, attention_backward(): pl.pallas_call(attention_back_kernel, grid=(steps,), out_shape=(token, sl...  63.8 us
    dot_general x18, matrix products, matmul3(): return jnp.matmul(left, right, precision=lax.Precision.HIGH)  51.4 us
    pallas_call x1, Pallas kernels, feed_both(): pl.pallas_call(feed_kernel, grid=(steps,), out_shape=(jax.ShapeDtypeStruc...  38.6 us
    pallas_call x1, Pallas kernels, attention_forward(): pl.pallas_call(attention_kernel, grid=(steps,), out_shape=tuple((jax.Shap...  37.9 us
    all_to_all x1, starting transfers between devices, from_owner_rows(): lax.all_to_all(rows_out.reshape(count, piece, D), AXES, 0, 0, tiled=True)  35.5 us
    pallas_call x1, Pallas kernels, square_slopes(): pl.pallas_call(slope_kernel, grid=(8,), out_shape=jax.ShapeDtypeStruct((8...  24.1 us
  transfers between devices with their start and end apart: 3, of which 1 were waited for; matrix products, arithmetic and copies ran while one was open for 4% of the time, Pallas kernels for 53%

profile of v4, /device:TPU:0, one launch (start us, length us, event | category | flops | bytes accessed | tf_op | source)
XLA Modules:
  0.0 522.2 jit_solution(16672319663047781350)
XLA Ops:
  13.4 5.3 %fusion.36 = f32[12,128,128]{2,0,1:T(8,128)S(1)} fusion(s32[128,128]{1,0:T(8,128)S(1)} %fusion.83, pred[128,128]{1,0:T(8,128)(4,1)S(1)} %fusion.84, bf16[12,128]{1,0:T(8,128)(2,1)S(1)} %copy-done), kind=kOutput, calls=%fused_computation.35 | convolution fusion | flops 52625408 | bytes 871424 | tf_op jit(solution)/shard_map/hd,qkd->hqk/dot_general | solution.py:1033
  19.8 72.8 %shard_map.212 = bf16[8,4,2,2,48,768]{5,4,3,2,1,0:T(8,128)(2,1)S(1)} custom-call(f32[8,24,768]{2,1,0:T(8,128)S(1)} %copy-done.3), custom_call_target="tpu_custom_call" | custom-call | tf_op jit(solution)/shard_map/pallas_call | solution.py:836
  92.7 3.6 copy-done.2
  96.2 37.9 %shard_map.213 = (bf16[4,1024,768]{2,1,0:T(8,128)(2,1)}, bf16[1024,768]{1,0:T(8,128)(2,1)}, bf16[1024,768]{1,0:T(8,128)(2,1)}, bf16[1024,768]{1,0:T(8,128)(2,1)}...) custom-call(s32[8]{0:T(128)} %memory_len.1, ...), custom_call_target="tpu_custom_call" | custom-call | flops 14000000000 | bytes 60000000 | tf_op jit(solution)/shard_map/pallas_call | solution.py:174
  134.1 38.6 %shard_map.214 = (bf16[1024,768]{1,0:T(8,128)(2,1)}, f32[1024,768]{1,0:T(8,128)}, bf16[2,1024,768]{2,1,0:T(8,128)(2,1)}, bf16[2,1024,3072]{2,1,0:T(8,128)(2,1)}, f32[3,768]{1,0:T(4,128)}, /*index=5*/f32[3,3072]{1,0:T(4,128)}) custom-call(s32[8]{0:T(128)} %lengths.1, f32[1024,768]{1,0:T(8,128)} %get-tuple-element.40.h2_in, bf16[1024,768]{1,0:T(8,128)(2,1)} %bitcast.63, ...), custom_call_target="tpu_custom_call" | custom-call | flops 20000000000 | bytes 40000000 | tf_op jit(solution)/shard_map/pallas_call | solution.py:285
  172.7 16.3 %convolution_convert_fusion = bf16[2,3072,768]{2,1,0:T(8,128)(2,1)} fusion(bf16[2,1024,3072]{2,1,0:T(8,128)(2,1)} %get-tuple-element.42, bf16[2,1024,768]{2,1,0:T(8,128)(2,1)} %get-tuple-element.43), kind=kOutput, calls=%fused_computation.2 | convolution fusion | flops 9668395008 | bytes 25165824 | tf_op jit(solution)/shard_map/btf,btd->bfd/dot_general | solution.py:1043
  191.1 63.8 %shard_map.215 = (bf16[1024,768]{1,0:T(8,128)(2,1)}, bf16[2048,768]{1,0:T(8,128)(2,1)}, bf16[6,1024,768]{2,1,0:T(8,128)(2,1)}, bf16[2,2048,768]{2,1,0:T(8,128)(2...) custom-call(bf16[1024,768]{1,0:T(8,128)(2,1)} %bitcast.65, f32[1024,768]{1,0:T(8,128)} %get-tuple-element.45.dh2, ...), custom_call_target="tpu_custom_call" | custom-call | flops 16000000000 | bytes 60000000 | tf_op jit(solution)/shard_map/pallas_call | solution.py:411
  259.0 24.1 %shard_map.216 = bf16[8,768,768]{2,1,0:T(8,128)(2,1)} custom-call(bf16[4,1024,768]{2,1,0:T(8,128)(2,1)} %get-tuple-element.59.left, bf16[6,1024,768]{2,1,0:T(8,128)(2,1)} %get-tuple-element.60.right, bf16[2048,768]{1,0:T(8,128)(2,1)} %bitcast.62, bf16[2,2048,768]{2,1,0:T(8,128)(2,1)} %get-tuple-element.61.far), custom_call_target="tpu_custom_call" | custom-call | flops 12000000000 | bytes 30000000 | tf_op jit(solution)/shard_map/pallas_call | solution.py:462
  283.1 77.5 %shard_map.217 = (f32[8,24,768]{2,1,0:T(8,128)}, f32[192,128]{1,0:T(8,128)}) custom-call(bf16[8,4,2,2,48,768]{5,4,3,2,1,0:T(8,128)(2,1)} %bitcast.52, f32[192,128]{1,0:T(8,128)} %bitcast.54), custom_call_target="tpu_custom_call" | custom-call | tf_op jit(solution)/shard_map/pallas_call | solution.py:721
  362.5 2.0 fusion.127
  364.7 1.9 fusion.128
  366.7 23.6 %all_to_all.10 = bf16[32,12,768]{2,1,0:T(8,128)(2,1)S(1)} all-to-all(bf16[32,12,768]{2,1,0:T(8,128)(2,1)S(1)} %pad_maximum_fusion), channel_id=1, replica_groups=mesh['tall'=4,'square'=4,'row'=2] {'tall','square','row'}, dimensions={0} | all-to-all | bytes 1179648 | tf_op jit(solution)/shard_map/all_to_all | solution.py:952
  392.1 5.8 %shard_map.218 = f32[768,768]{1,0:T(8,128)S(1)} custom-call(f32[768,768]{1,0:T(8,128)S(1)} %convolution_bitcast_fusion.gram), custom_call_target="tpu_custom_call" | custom-call | tf_op jit(solution)/shard_map/pallas_call | solution.py:917
  399.3 2.5 convert_multiply_fusion
  401.8 2.4 mul.172
  404.2 3.3 fusion.2
  407.6 3.2 fusion.11
  410.7 3.2 fusion.130
  413.9 1.8 fusion.129
  415.8 3.6 fusion.131
  419.3 3.2 fusion.31
  424.4 3.2 fusion.29
  427.6 3.3 fusion.132
  430.9 3.2 fusion.25
  436.0 3.2 fusion.23
  439.2 3.1 fusion.133
  442.4 3.5 fusion.19
  447.6 3.2 fusion.17
  450.9 3.2 fusion.134
  454.0 1.8 fusion.37
  456.9 35.5 %all-to-all-start.1 = ((bf16[32,12,768]{2,1,0:T(8,128)(2,1)}), bf16[32,12,768]{2,1,0:T(8,128)(2,1)S(1)}, u32[]{:S(2)}, u32[]{:S(2)}) async-start(bf16[32,12,768]{2,1,0:T(8,128)(2,1)} %reshape.131), calls=%async_computation.2 | async-start | bytes 1572864 | tf_op jit(solution)/shard_map/all_to_all | solution.py:965
  495.2 17.8 %all-to-all-done.1 = bf16[32,12,768]{2,1,0:T(8,128)(2,1)S(1)} async-done(((bf16[32,12,768]{2,1,0:T(8,128)(2,1)}), bf16[32,12,768]{2,1,0:T(8,128)(2,1)S(1)}, u32[]{:S(2)}, u32[]{:S(2)}) %all-to-all-start.1) | async-done | bytes 589856 | tf_op jit(solution)/shard_map/all_to_all | solution.py:965
  (74 shorter events, 27.9 us)
Async XLA Ops:
  7.2 6.2 %copy-start = (bf16[12,128]{1,0:T(8,128)(2,1)S(1)}, bf16[12,128]{1,0:T(8,128)(2,1)}, u32[]{:S(2)}) copy-start(bf16[12,128]{1,0:T(8,128)(2,1)} %param.25) | copy-start | bytes 9220
  7.2 126.9 %all-gather.2.cloned.1.call-start = ((), (), s32[]{:S(2)}) async-start(), calls=%async_computation.3 | async-start | bytes 9732096 | tf_op jit(solution)/shard_map/all_gather | solution.py:1026
  9.1 355.6 %reduce-scatter.2.cloned.1.call-start = ((), (), s32[]{:S(2)}) async-start(), calls=%async_computation.4 | async-start | bytes 9732096 | tf_op jit(solution)/shard_map/reduce_scatter | solution.py:1045
  11.9 7.9 %copy-start.3 = (f32[8,24,768]{2,1,0:T(8,128)S(1)}, f32[8,24,768]{2,1,0:T(8,128)}, u32[]{:S(2)}) copy-start(f32[8,24,768]{2,1,0:T(8,128)} %own.1) | copy-start | bytes 1769476
  92.7 3.6 copy-start.2
  189.1 0.7 copy-start.12
  189.1 1.9 copy-start.10
  191.0 66.3 %copy-start.11 = (f32[3,768]{1,0:T(4,128)S(1)}, f32[3,768]{1,0:T(4,128)}, u32[]{:S(2)}) copy-start(f32[3,768]{1,0:T(4,128)} %get-tuple-element.64) | copy-start | bytes 27652
  283.1 79.4 %copy-start.7 = (f32[8,24,768]{2,1,0:T(8,128)S(1)}, f32[8,24,768]{2,1,0:T(8,128)}, u32[]{:S(2)}) copy-start(f32[8,24,768]{2,1,0:T(8,128)} %param.20) | copy-start | bytes 1769476
  360.6 4.1 copy-start.8
  390.3 0.9 copy-start.5
  410.7 3.2 copy-start.4
  455.8 36.6 %copy-start.9 = (f32[192,128]{1,0:T(8,128)S(1)}, f32[192,128]{1,0:T(8,128)}, u32[]{:S(2)}) copy-start(f32[192,128]{1,0:T(8,128)} %get-tuple-element.66) | copy-start | bytes 294916
  456.9 56.1 %all-to-all-start.1 = ((bf16[32,12,768]{2,1,0:T(8,128)(2,1)}), bf16[32,12,768]{2,1,0:T(8,128)(2,1)S(1)}, u32[]{:S(2)}, u32[]{:S(2)}) async-start(bf16[32,12,768]{2,1,0:T(8,128)(2,1)} %reshape.131), calls=%async_computation.2 | async-start | bytes 1572864 | tf_op jit(solution)/shard_map/all_to_all | solution.py:965
  492.4 20.9 %copy-start.6 = (f32[2,96,768]{2,1,0:T(8,128)S(1)}, f32[2,96,768]{2,1,0:T(8,128)}, u32[]{:S(2)}) copy-start(f32[2,96,768]{2,1,0:T(8,128)} %param.19) | copy-start | bytes 1769476
  513.2 1.9 copy-start.1
Sparse Core Ops, SparseCore 0:
  11.5 104.2 all-gather.1
  189.2 148.7 reduce-scatter.1

commit v5 on v4

--- a/solution.py
+++ b/solution.py
@@ -93,11 +93,24 @@
 
 
 def attention_kernel(
-    memory_len, x_in, memory, w, vec, hs, bias,
+    memory_len, x_in, memory, w, vec, hs, mirrored,
     left, q, k, v, p, o, h1, cq, ck, cv, pc, co, h2,
+    bias,
 ):
     step = pl.program_id(0)
     masks = head_masks()
+
+    @pl.when(step == 0)
+    def _():
+        row = lax.broadcasted_iota(jnp.int32, (128, 128), 0)
+        column = lax.broadcasted_iota(jnp.int32, (128, 128), 1)
+        for head in range(12):
+            line = jnp.broadcast_to(mirrored[head : head + 1], (128, 128))
+            line = pltpu.roll(line, 0, 1, stride=1, stride_axis=0)
+            bias[head // 2, (head % 2) * 128 : (head % 2) * 128 + 128] = jnp.where(
+                row >= column, line, NEGATIVE_LARGE
+            )
+
     x = x_in[...].astype(F32)
     left[0] = norm(x, vec[0:1], vec[1:2]).astype(BF16)
     q[...] = ((times(left[0], w[0]) + vec[2:3]) * 0.125).astype(BF16)
@@ -180,6 +193,7 @@
             spec["t"], spec["m"], whole(square.shape), whole(vectors.shape), whole(head_row.shape), whole(bias.shape),
         ],
         out_specs=tuple(spec[kind] for _, kind in shapes),
+        scratch_shapes=[pltpu.VMEM((6, 256, 128), F32)],
         compiler_params=pltpu.CompilerParams(vmem_limit_bytes=60 << 20),
         cost_estimate=pl.CostEstimate(flops=14_000_000_000, bytes_accessed=60_000_000, transcendentals=5_000_000),
     )(memory_len, inputs, memory, square, vectors, head_row, bias)
@@ -933,6 +947,118 @@
     )(gram)
 
 
+SIDE = 256
+
+
+def sweep_kernel(packed, rows, out, gram, held, now, poly, step):
+    blocks = gram.shape[0] // SIDE
+    width = blocks * SIDE
+
+    def put(target, a, values):
+        for b in range(a, blocks):
+            block = values[:, (b - a) * SIDE : (b - a) * SIDE + SIDE]
+            for i, j, piece in ((a, b, block),) if a == b else ((a, b, block), (b, a, block.T)):
+                columns = slice(j * SIDE, j * SIDE + SIDE)
+                top = piece.astype(BF16)
+                target[i * SIDE : i * SIDE + SIDE, columns] = top
+                target[width + i * SIDE : width + i * SIDE + SIDE, columns] = (
+                    piece - top.astype(F32)
+                ).astype(BF16)
+                target[2 * width + i * SIDE : 2 * width + i * SIDE + SIDE, columns] = top
+
+    def exact(left, a, right):
+        high = left[a * SIDE : a * SIDE + SIDE]
+        low = left[width + a * SIDE : width + a * SIDE + SIDE]
+        return times(jnp.concatenate([high, high, low], axis=1), right[:, a * SIDE :])
+
+    index, trace = 0, jnp.zeros((1, 1), F32)
+    row = lax.broadcasted_iota(jnp.int32, (SIDE, SIDE), 0)
+    column = lax.broadcasted_iota(jnp.int32, (SIDE, SIDE), 1)
+    unit = jnp.where(row == column, 1.0, 0.0)
+    for a in range(blocks):
+        for b in range(a, blocks):
+            block = packed[index * SIDE : index * SIDE + SIDE]
+            gram[a * SIDE : a * SIDE + SIDE, b * SIDE : b * SIDE + SIDE] = block
+            if a == b:
+                trace = trace + jnp.sum(
+                    jnp.sum(block * unit, axis=1, keepdims=True), axis=0, keepdims=True
+                )
+            else:
+                gram[b * SIDE : b * SIDE + SIDE, a * SIDE : a * SIDE + SIDE] = block.T
+            index += 1
+    scale = 1.0 / (jnp.sqrt(trace) + FLOOR_EPSILON)
+
+    for a in range(blocks):
+        put(now, a, gram[a * SIDE : a * SIDE + SIDE, a * SIDE :] * (scale * scale))
+    count = rows.shape[0]
+
+    def keep(some, rest, values):
+        top = values.astype(BF16)
+        held[some] = top
+        held[rest] = (values - top.astype(F32)).astype(BF16)
+
+    keep(slice(0, count), slice(count, 2 * count), rows[...].astype(F32) * scale)
+
+    @pl.loop(0, ITERS)
+    def _(sweep):
+        for a in range(blocks):
+            row = lax.broadcasted_iota(jnp.int32, (SIDE, width - a * SIDE), 0)
+            column = lax.broadcasted_iota(jnp.int32, (SIDE, width - a * SIDE), 1)
+            lines = slice(a * SIDE, a * SIDE + SIDE)
+            below = slice(width + a * SIDE, width + a * SIDE + SIDE)
+            values = exact(now, a, now) * THIRD_TERM + SECOND_TERM * (
+                now[lines, a * SIDE :].astype(F32) + now[below, a * SIDE :].astype(F32)
+            )
+            put(poly, a, jnp.where(row == column, values + FIRST_TERM, values))
+
+        @pl.loop(0, count // 128)
+        def _(a):
+            some = pl.ds(pl.multiple_of(a * 128, 128), 128)
+            rest = pl.ds(pl.multiple_of(a * 128 + count, 128), 128)
+            high, low = held[some], held[rest]
+            keep(some, rest, times(jnp.concatenate([high, high, low], axis=1), poly[...]))
+
+        @pl.when(sweep < ITERS - 1)
+        def _():
+            for a in range(blocks):
+                put(step, a, exact(now, a, poly))
+            for a in range(blocks):
+                put(now, a, exact(step, a, poly))
+
+    out[...] = held[0:count]
+
+
+def sweeps(packed, rows):
+    width = rows.shape[1]
+    vmem = pl.BlockSpec(memory_space=pltpu.VMEM)
+    part = pltpu.VMEM((3 * width, width), BF16)
+    return pl.pallas_call(
+        sweep_kernel,
+        out_shape=jax.ShapeDtypeStruct(rows.shape, BF16),
+        in_specs=[vmem, vmem],
+        out_specs=vmem,
+        scratch_shapes=[
+            pltpu.VMEM((width, width), F32),
+            pltpu.VMEM((2 * rows.shape[0], width), BF16),
+        ]
+        + [part] * 3,
+        compiler_params=pltpu.CompilerParams(vmem_limit_bytes=48 << 20),
+        cost_estimate=pl.CostEstimate(flops=40_000_000_000, bytes_accessed=5_000_000, transcendentals=0),
+    )(packed, rows)
+
+
+def upper_blocks(gram):
+    blocks = gram.shape[0] // SIDE
+    return jnp.concatenate(
+        [
+            gram[a * SIDE : a * SIDE + SIDE, b * SIDE : b * SIDE + SIDE]
+            for a in range(blocks)
+            for b in range(a, blocks)
+        ],
+        axis=0,
+    )
+
+
 def matmul3(left, right):
     return jnp.matmul(left, right, precision=lax.Precision.HIGH)
 
@@ -978,14 +1104,15 @@
 
 
 def orthogonal_rows(rows_in, kernels):
+    gram = lax.dot_general(
+        rows_in, rows_in, (((0,), (0,)), ((), ())), preferred_element_type=jnp.float32
+    )
+    if kernels:
+        return sweeps(gram_sum(upper_blocks(gram), 2), rows_in)
     rows_in = rows_in.astype(jnp.float32)
-    gram = jnp.einsum("rd,re->de", rows_in, rows_in, precision=lax.Precision.HIGHEST)
-    if kernels:
-        gram = gram_sum(gram, 2)
-    else:
-        gram = lax.psum(gram, "row")
-        is_tall = lax.axis_index("tall") >= 2
-        gram = jnp.where(is_tall, lax.psum(jnp.where(is_tall, gram, 0.0), "square"), gram)
+    gram = lax.psum(gram, "row")
+    is_tall = lax.axis_index("tall") >= 2
+    gram = jnp.where(is_tall, lax.psum(jnp.where(is_tall, gram, 0.0), "square"), gram)
     eye = (jnp.arange(D)[:, None] == jnp.arange(D)[None, :]).astype(jnp.float32)
     scale = 1.0 / (jnp.sqrt(jnp.sum(gram * eye)) + FLOOR_EPSILON)
     gram = gram * (scale * scale)
@@ -1027,11 +1154,7 @@
     width = inputs.shape[2]
     vec, feed = vectors.astype(F32), feed_vectors.astype(F32)
     head_row = jnp.repeat(head_scale.astype(F32), width // head_scale.shape[0])[None]
-    at = jnp.arange(inputs.shape[1])
-    distance = at[:, None] - at[None, :]
-    table = (jnp.maximum(distance, 0)[:, :, None] == at[None, None, :]).astype(BF16)
-    bias = jnp.einsum("hd,qkd->hqk", relative, table, preferred_element_type=F32)
-    bias = jnp.where(distance >= 0, bias, NEGATIVE_LARGE).reshape(6, 256, 128)
+    bias = jnp.roll(relative.astype(F32)[:, ::-1], 1, axis=1)
     flat_in, flat_memory = inputs.reshape(-1, width), memory.reshape(-1, width)
     left, q, k, v, p, o, h1, cq, ck, cv, pc, co, h2 = attention_forward(
         flat_in, flat_memory, memory_len, square_copy, vec, head_row, bias

time: 529 us -> 489 us (0.924)
  matrix products: 73.9 us -> 17.2 us
  Pallas kernels: 321 us -> 351 us
  starting transfers between devices: 35.6 us -> 26.5 us
    dot_general x20 -> x1, matrix products: 57.6 us -> 0.86 us  [orthogonal_rows(): lax.dot_general(rows_in, rows_in, (((0,), (0,)), ((), ())), preferred_ele...]
    pallas_call x0 -> x1, Pallas kernels: none -> 37.8 us  [sweeps(): pl.pallas_call(sweep_kernel, out_shape=jax.ShapeDtypeStruct(rows.shape, B...]
    all_to_all x1, starting transfers between devices: 35.5 us -> 26.4 us  [from_owner_rows(): lax.all_to_all(rows_out.reshape(count, piece, D), AXES, 0, 0, tiled=True)]
  transfers between devices with their start and end apart: 3 -> 3, of which waited for: 1 -> 1; matrix products, arithmetic and copies ran while one was open for 4% -> 4% of each run, Pallas kernels for 53% -> 56%
where the time goes in v5:
time: 489 us; the launch traced here: 482 us
  Pallas kernels  351 us (72%)
  starting transfers between devices  26.5 us (5%)
  blocking collectives  23.9 us (5%)
  waiting for transfers between devices  17.9 us (4%)
  matrix products  17.2 us (4%)
  between operations  15.9 us (3%)
  other arithmetic  15.3 us (3%)
  local copies, waits for them, and re-layouts  14.4 us (3%)
    pallas_call x1, Pallas kernels, reduce_scatter(): pl.pallas_call(functools.partial(reduce_kernel, tuple(groups), small is n...  74.5 us
    pallas_call x1, Pallas kernels, gather_rows(): pl.pallas_call(functools.partial(gather_kernel, split), out_shape=jax.Sha...  69.2 us
    pallas_call x1, Pallas kernels, attention_backward(): pl.pallas_call(attention_back_kernel, grid=(steps,), out_shape=(token, sl...  64.1 us
    pallas_call x1, Pallas kernels, feed_both(): pl.pallas_call(feed_kernel, grid=(steps,), out_shape=(jax.ShapeDtypeStruc...  38.6 us
    pallas_call x1, Pallas kernels, attention_forward(): pl.pallas_call(attention_kernel, grid=(steps,), out_shape=tuple((jax.Shap...  38 us
    pallas_call x1, Pallas kernels, sweeps(): pl.pallas_call(sweep_kernel, out_shape=jax.ShapeDtypeStruct(rows.shape, B...  37.8 us
    all_to_all x1, starting transfers between devices, from_owner_rows(): lax.all_to_all(rows_out.reshape(count, piece, D), AXES, 0, 0, tiled=True)  26.4 us
    pallas_call x1, Pallas kernels, square_slopes(): pl.pallas_call(slope_kernel, grid=(8,), out_shape=jax.ShapeDtypeStruct((8...  24.3 us
  transfers between devices with their start and end apart: 3, of which 1 were waited for; matrix products, arithmetic and copies ran while one was open for 4% of the time, Pallas kernels for 56%

profile of v5, /device:TPU:0, one launch (start us, length us, event | category | flops | bytes accessed | tf_op | source)
XLA Modules:
  0.0 482.2 jit_solution(6880488664829446388)
XLA Ops:
  7.2 1.8 convert_element_type.36
  9.1 0.8 slice.82
  9.9 0.7 slice.81
  10.6 0.7 broadcast_in_dim.6
  12.0 1.4 convert_element_type.37.feed
  13.4 1.4 convert_element_type.33.vec
  14.8 1.1 copy-done.1
  15.9 69.2 %shard_map.212 = bf16[8,4,2,2,48,768]{5,4,3,2,1,0:T(8,128)(2,1)S(1)} custom-call(f32[8,24,768]{2,1,0:T(8,128)S(1)} %copy-done.1), custom_call_target="tpu_custom_call" | custom-call | tf_op jit(solution)/shard_map/pallas_call | solution.py:850
  85.0 3.6 copy-done
  89.3 38.0 %shard_map.213 = (bf16[4,1024,768]{2,1,0:T(8,128)(2,1)}, bf16[1024,768]{1,0:T(8,128)(2,1)}, bf16[1024,768]{1,0:T(8,128)(2,1)}, bf16[1024,768]{1,0:T(8,128)(2,1)}...) custom-call(s32[8]{0:T(128)} %memory_len.1, ...), custom_call_target="tpu_custom_call" | custom-call | flops 14000000000 | bytes 60000000 | tf_op jit(solution)/shard_map/pallas_call | solution.py:187
  127.3 38.6 %shard_map.214 = (bf16[1024,768]{1,0:T(8,128)(2,1)}, f32[1024,768]{1,0:T(8,128)}, bf16[2,1024,768]{2,1,0:T(8,128)(2,1)}, bf16[2,1024,3072]{2,1,0:T(8,128)(2,1)}, f32[3,768]{1,0:T(4,128)}, /*index=5*/f32[3,3072]{1,0:T(4,128)}) custom-call(s32[8]{0:T(128)} %lengths.1, f32[1024,768]{1,0:T(8,128)} %get-tuple-element.40.h2_in, bf16[1024,768]{1,0:T(8,128)(2,1)} %bitcast.33, ...), custom_call_target="tpu_custom_call" | custom-call | flops 20000000000 | bytes 40000000 | tf_op jit(solution)/shard_map/pallas_call | solution.py:299
  165.9 16.3 %convolution_convert_fusion = bf16[2,3072,768]{2,1,0:T(8,128)(2,1)} fusion(bf16[2,1024,3072]{2,1,0:T(8,128)(2,1)} %get-tuple-element.42, bf16[2,1024,768]{2,1,0:T(8,128)(2,1)} %get-tuple-element.43), kind=kOutput, calls=%fused_computation | convolution fusion | flops 9668395008 | bytes 25165824 | tf_op jit(solution)/shard_map/btf,btd->bfd/dot_general | solution.py:1166
  184.2 64.1 %shard_map.215 = (bf16[1024,768]{1,0:T(8,128)(2,1)}, bf16[2048,768]{1,0:T(8,128)(2,1)}, bf16[6,1024,768]{2,1,0:T(8,128)(2,1)}, bf16[2,2048,768]{2,1,0:T(8,128)(2...) custom-call(bf16[1024,768]{1,0:T(8,128)(2,1)} %bitcast.35, f32[1024,768]{1,0:T(8,128)} %get-tuple-element.45.dh2, ...), custom_call_target="tpu_custom_call" | custom-call | flops 16000000000 | bytes 60000000 | tf_op jit(solution)/shard_map/pallas_call | solution.py:425
  248.3 0.8 slice.68
  249.2 0.8 slice_reduce_fusion
  250.0 0.8 slice.66
  250.9 0.8 maximum_bitcast_fusion
  251.7 0.7 concatenate.23
  252.4 24.3 %shard_map.216 = bf16[8,768,768]{2,1,0:T(8,128)(2,1)} custom-call(bf16[4,1024,768]{2,1,0:T(8,128)(2,1)} %get-tuple-element.59.left, bf16[6,1024,768]{2,1,0:T(8,128)(2,1)} %get-tuple-element.60.right, bf16[2048,768]{1,0:T(8,128)(2,1)} %bitcast.32, bf16[2,2048,768]{2,1,0:T(8,128)(2,1)} %get-tuple-element.61.far), custom_call_target="tpu_custom_call" | custom-call | flops 12000000000 | bytes 30000000 | tf_op jit(solution)/shard_map/pallas_call | solution.py:476
  276.7 74.5 %shard_map.217 = (f32[8,24,768]{2,1,0:T(8,128)}, f32[192,128]{1,0:T(8,128)}) custom-call(bf16[8,4,2,2,48,768]{5,4,3,2,1,0:T(8,128)(2,1)} %bitcast.23, f32[192,128]{1,0:T(8,128)} %bitcast.24), custom_call_target="tpu_custom_call" | custom-call | tf_op jit(solution)/shard_map/pallas_call | solution.py:735
  351.3 1.2 slice.83
  353.3 2.0 fusion.2
  355.3 1.9 fusion.3
  357.4 23.9 %all_to_all.10 = bf16[32,12,768]{2,1,0:T(8,128)(2,1)S(1)} all-to-all(bf16[32,12,768]{2,1,0:T(8,128)(2,1)S(1)} %pad_maximum_fusion), channel_id=1, replica_groups=mesh['tall'=4,'square'=4,'row'=2] {'tall','square','row'}, dimensions={0} | all-to-all | bytes 1179648 | tf_op jit(solution)/shard_map/all_to_all | solution.py:1078
  381.3 0.9 convolution_bitcast_fusion
  382.3 4.7 shard_map.218.packed
  387.1 37.8 %shard_map.219 = bf16[384,768]{1,0:T(8,128)(2,1)S(1)} custom-call(f32[1536,256]{1,0:T(8,128)S(1)} %shard_map.218.packed, bf16[384,768]{1,0:T(8,128)(2,1)S(1)} %reshape.113.rows), custom_call_target="tpu_custom_call" | custom-call | flops 40000000000 | bytes 5000000 | tf_op jit(solution)/shard_map/pallas_call | solution.py:1035
  425.0 1.0 reshape.114
  426.0 26.4 %all-to-all-start.1 = ((bf16[32,12,768]{2,1,0:T(8,128)(2,1)}), bf16[32,12,768]{2,1,0:T(8,128)(2,1)S(1)}, u32[]{:S(2)}, u32[]{:S(2)}) async-start(bf16[32,12,768]{2,1,0:T(8,128)(2,1)} %reshape.114), calls=%async_computation.2 | async-start | bytes 1572864 | tf_op jit(solution)/shard_map/all_to_all | solution.py:1091
  455.3 17.8 %all-to-all-done.1 = bf16[32,12,768]{2,1,0:T(8,128)(2,1)S(1)} async-done(((bf16[32,12,768]{2,1,0:T(8,128)(2,1)}), bf16[32,12,768]{2,1,0:T(8,128)(2,1)S(1)}, u32[]{:S(2)}, u32[]{:S(2)}) %all-to-all-start.1) | async-done | bytes 589856 | tf_op jit(solution)/shard_map/all_to_all | solution.py:1091
  473.4 0.9 multiply_subtract_fusion
  474.3 0.9 multiply_subtract_fusion.1
  (54 shorter events, 6.7 us)
Async XLA Ops:
  7.2 120.1 %all-gather.2.cloned.1.call-start = ((), (), s32[]{:S(2)}) async-start(), calls=%async_computation.3 | async-start | bytes 9732096 | tf_op jit(solution)/shard_map/all_gather | solution.py:1153
  9.1 346.2 %reduce-scatter.2.cloned.1.call-start = ((), (), s32[]{:S(2)}) async-start(), calls=%async_computation.4 | async-start | bytes 9732096 | tf_op jit(solution)/shard_map/reduce_scatter | solution.py:1168
  14.8 1.1 copy-start.1
  85.0 3.6 copy-start
  182.2 0.7 copy-start.9
  182.2 1.9 copy-start.7
  184.2 66.5 %copy-start.8 = (f32[3,768]{1,0:T(4,128)S(1)}, f32[3,768]{1,0:T(4,128)}, u32[]{:S(2)}) copy-start(f32[3,768]{1,0:T(4,128)} %get-tuple-element.64) | copy-start | bytes 27652
  276.7 76.5 %copy-start.4 = (f32[8,24,768]{2,1,0:T(8,128)S(1)}, f32[8,24,768]{2,1,0:T(8,128)}, u32[]{:S(2)}) copy-start(f32[8,24,768]{2,1,0:T(8,128)} %param.20) | copy-start | bytes 1769476
  351.3 4.0 copy-start.5
  425.0 27.5 %copy-start.6 = (f32[192,128]{1,0:T(8,128)S(1)}, f32[192,128]{1,0:T(8,128)}, u32[]{:S(2)}) copy-start(f32[192,128]{1,0:T(8,128)} %get-tuple-element.66) | copy-start | bytes 294916
  426.0 47.0 %all-to-all-start.1 = ((bf16[32,12,768]{2,1,0:T(8,128)(2,1)}), bf16[32,12,768]{2,1,0:T(8,128)(2,1)S(1)}, u32[]{:S(2)}, u32[]{:S(2)}) async-start(bf16[32,12,768]{2,1,0:T(8,128)(2,1)} %reshape.114), calls=%async_computation.2 | async-start | bytes 1572864 | tf_op jit(solution)/shard_map/all_to_all | solution.py:1091
  452.4 20.9 %copy-start.3 = (f32[2,96,768]{2,1,0:T(8,128)S(1)}, f32[2,96,768]{2,1,0:T(8,128)}, u32[]{:S(2)}) copy-start(f32[2,96,768]{2,1,0:T(8,128)} %param.19) | copy-start | bytes 1769476
  473.3 1.1 copy-start.2
Sparse Core Ops, SparseCore 0:
  11.5 100.5 all-gather.1
  182.4 145.6 reduce-scatter.1

commit v6 on v5

--- a/solution.py
+++ b/solution.py
@@ -41,6 +41,12 @@
     return lax.dot_general(left, right, (((0,), (0,)), ((), ())), preferred_element_type=F32)
 
 
+def down_to_keys(weights, values):
+    if weights.shape[1] > values.shape[1]:
+        return times_down(values, weights).astype(BF16).T
+    return times_down(weights, values).astype(BF16)
+
+
 def standard(values):
     center = values - jnp.mean(values, axis=-1, keepdims=True)
     scale = lax.rsqrt(jnp.mean(center * center, axis=-1, keepdims=True) + NORM_EPSILON)
@@ -93,15 +99,16 @@
 
 
 def attention_kernel(
-    memory_len, x_in, memory, w, vec, hs, mirrored,
+    memory_len, x_in, memory, w, vec_in, hs, mirrored,
     left, q, k, v, p, o, h1, cq, ck, cv, pc, co, h2,
-    bias,
+    bias, vec,
 ):
     step = pl.program_id(0)
     masks = head_masks()
 
     @pl.when(step == 0)
     def _():
+        vec[...] = vec_in[...].astype(F32)
         row = lax.broadcasted_iota(jnp.int32, (128, 128), 0)
         column = lax.broadcasted_iota(jnp.int32, (128, 128), 1)
         for head in range(12):
@@ -193,7 +200,7 @@
             spec["t"], spec["m"], whole(square.shape), whole(vectors.shape), whole(head_row.shape), whole(bias.shape),
         ],
         out_specs=tuple(spec[kind] for _, kind in shapes),
-        scratch_shapes=[pltpu.VMEM((6, 256, 128), F32)],
+        scratch_shapes=[pltpu.VMEM((6, 256, 128), F32), pltpu.VMEM(vectors.shape, F32)],
         compiler_params=pltpu.CompilerParams(vmem_limit_bytes=60 << 20),
         cost_estimate=pl.CostEstimate(flops=14_000_000_000, bytes_accessed=60_000_000, transcendentals=5_000_000),
     )(memory_len, inputs, memory, square, vectors, head_row, bias)
@@ -205,9 +212,9 @@
 
 
 def feed_kernel(
-    lengths, h2_in, cot, tall, vec, feed,
+    lengths, h2_in, cot, tall, vec_in, feed_in,
     out, dh2, narrow, wide, dvec, dfeed,
-    u, g, dr, total,
+    u, g, dr, total, vec, feed,
 ):
     step = pl.program_id(0)
     items = TOKENS // 128
@@ -216,6 +223,8 @@
 
     @pl.when(step == 0)
     def _():
+        vec[...] = vec_in[...].astype(F32)
+        feed[...] = feed_in[...].astype(F32)
         dvec[...] = jnp.zeros_like(dvec)
         dfeed[...] = jnp.zeros_like(dfeed)
 
@@ -316,17 +325,22 @@
             pl.BlockSpec((3, width), lambda i: (0, 0)),
             pl.BlockSpec((3, wide), lambda i: (0, 0)),
         ),
-        scratch_shapes=[pltpu.VMEM((TOKENS, wide), F32)] * 3 + [pltpu.VMEM((TOKENS, width), F32)],
+        scratch_shapes=[pltpu.VMEM((TOKENS, wide), F32)] * 3
+        + [
+            pltpu.VMEM((TOKENS, width), F32),
+            pltpu.VMEM(vectors.shape, F32),
+            pltpu.VMEM(feed_vectors.shape, F32),
+        ],
         compiler_params=pltpu.CompilerParams(vmem_limit_bytes=60 << 20),
         cost_estimate=pl.CostEstimate(flops=20_000_000_000, bytes_accessed=40_000_000, transcendentals=7_000_000),
     )(lengths, hidden, cotangent, tall, vectors, feed_vectors)
 
 
 def attention_back_kernel(
-    x_in, dh2, w, vec, hs,
+    x_in, dh2, w, vec_in, hs,
     q, k, v, p, o, h1, cq, ck, cv, pc, co,
     dx, dmem, right, far, dvec, drel,
-    do, dh1, dbias,
+    do, dh1, dbias, vec,
 ):
     step = pl.program_id(0)
     masks = head_masks()
@@ -335,6 +349,7 @@
 
     @pl.when(step == 0)
     def _():
+        vec[...] = vec_in[...].astype(F32)
         dvec[...] = jnp.zeros_like(dvec)
         dbias[...] = jnp.zeros_like(dbias)
 
@@ -353,12 +368,12 @@
         rows = slice(item * 128, item * 128 + 128)
         kept = weights[item, pair]
         grad = stacked(do[rows, lanes], masks)
-        dvalue[keys, lanes] = times_down(kept, grad).astype(BF16)
+        dvalue[keys, lanes] = down_to_keys(kept, grad)
         slope = soften_back(kept, times_back(grad, value[keys, lanes]))
         dquery[rows, lanes] = (
             times(side_by_side(slope), stacked(key[keys, lanes], masks)).astype(BF16) * 0.125
         ).astype(BF16)
-        dkey[keys, lanes] = times_down(slope, stacked(query[rows, lanes], masks)).astype(BF16)
+        dkey[keys, lanes] = down_to_keys(slope, stacked(query[rows, lanes], masks))
         if with_bias:
             dbias[pair] += slope.astype(F32)
 
@@ -445,6 +460,7 @@
             pltpu.VMEM((TOKENS, width), BF16),
             pltpu.VMEM((TOKENS, width), F32),
             pltpu.VMEM((6, 256, 128), F32),
+            pltpu.VMEM(vectors.shape, F32),
         ],
         compiler_params=pltpu.CompilerParams(vmem_limit_bytes=60 << 20),
         cost_estimate=pl.CostEstimate(flops=16_000_000_000, bytes_accessed=60_000_000, transcendentals=0),
@@ -616,18 +632,16 @@
         if stage == 0:
             lanes = pl.ds(pl.multiple_of(mine + column, 128), width)
 
-            @pl.loop(0, 16)
-            def _(block):
-                a, b, d = lax.div(block, 4), lax.rem(lax.div(block, 2), 2), lax.rem(block, 2)
-                r0[j, a, b, d] = (
-                    r0[j, a, b, d].astype(f32) + src[matrix, a, b, d, :, lanes].astype(f32)
+            @pl.loop(0, 4)
+            def _(a):
+                r0[j, a] = (
+                    r0[j, a].astype(f32) + src[matrix, a, :, :, :, lanes].astype(f32)
                 ).astype(jnp.bfloat16)
         elif stage == 1:
-            @pl.loop(0, 8)
-            def _(block):
-                a, b = lax.div(block, 2), lax.rem(block, 2)
-                own = r0[j, a, b, x] if order == 0 else r0[j, a, y, b]
-                r1[j, a, b] = (r1[j, a, b].astype(f32) + own.astype(f32)).astype(jnp.bfloat16)
+            @pl.loop(0, 4)
+            def _(a):
+                own = r0[j, a, :, x] if order == 0 else r0[j, a, y]
+                r1[j, a] = (r1[j, a].astype(f32) + own.astype(f32)).astype(jnp.bfloat16)
         elif stage == 2:
             @pl.loop(0, 4)
             def _(a):
@@ -644,18 +658,18 @@
             lanes = pl.ds(pl.multiple_of(theirs + column, 128), width)
             out[matrix, :, lanes] = r4[j]
 
-    def each(plan, body):
-        @pl.loop(0, plan[0] // 2)
+    def each(plan, body, turns):
+        @pl.loop(0, turns)
         def _(i):
             for order in range(2):
                 body(order, i)
 
-    def start(plan, stage):
+    def start(plan, stage, turns):
         def body(order, i):
             for copy in copies(plan, stage, order, i):
                 copy.start()
 
-        each(plan, body)
+        each(plan, body, turns)
 
     def step(plan, stage, order, i):
         for copy in copies(plan, stage, order, i):
@@ -670,15 +684,21 @@
             for copy in copies(plan, stage, order, i):
                 copy.wait_send()
 
-        each(plan, body)
+        each(plan, body, plan[0] // 2)
 
     for plan in plans:
-        start(plan, 0)
+        start(plan, 0, 2)
     for plan in plans:
         turns = plan[0] // 2
 
         @pl.loop(0, turns + 4)
         def _(turn):
+            @pl.when(turn < turns - 2)
+            def _():
+                for order in range(2):
+                    for copy in copies(plan, 0, order, turn + 2):
+                        copy.start()
+
             for stage in range(5):
                 @pl.when((turn >= stage) & (turn < turns + stage))
                 def _():
@@ -1152,22 +1172,21 @@
         )
     tall_copy = lax.all_gather(tall_master.astype(jnp.bfloat16), AXES, axis=1, tiled=True)
     width = inputs.shape[2]
-    vec, feed = vectors.astype(F32), feed_vectors.astype(F32)
     head_row = jnp.repeat(head_scale.astype(F32), width // head_scale.shape[0])[None]
     bias = jnp.roll(relative.astype(F32)[:, ::-1], 1, axis=1)
     flat_in, flat_memory = inputs.reshape(-1, width), memory.reshape(-1, width)
     left, q, k, v, p, o, h1, cq, ck, cv, pc, co, h2 = attention_forward(
-        flat_in, flat_memory, memory_len, square_copy, vec, head_row, bias
+        flat_in, flat_memory, memory_len, square_copy, vectors, head_row, bias
     )
     output, dh2, narrow, wide, late_slope, feed_slope = feed_both(
-        h2, cotangent.reshape(-1, width), lengths, tall_copy, vec, feed
+        h2, cotangent.reshape(-1, width), lengths, tall_copy, vectors, feed_vectors
     )
 
     tall_slope = jnp.einsum("btf,btd->bfd", wide, narrow, preferred_element_type=F32).astype(BF16)
     tall_slope, dh2 = lax.optimization_barrier((tall_slope, dh2))
     tall_sum = lax.psum_scatter(tall_slope, AXES, scatter_dimension=1, tiled=True).astype(F32)
     input_slope, memory_slope, right, far, early_slope, bias_slope = attention_backward(
-        flat_in, dh2, square_copy, vec, head_row, (q, k, v, p, o, h1, cq, ck, cv, pc, co)
+        flat_in, dh2, square_copy, vectors, head_row, (q, k, v, p, o, h1, cq, ck, cv, pc, co)
     )
     square_slope = square_slopes(left, right, flat_memory, far)
     vector_slope = jnp.concatenate([early_slope[:14], late_slope], axis=0)

time: 489 us -> 486 us (level)
  transfers between devices with their start and end apart: 3 -> 3, of which waited for: 1 -> 1; matrix products, arithmetic and copies ran while one was open for 4% -> 3% of each run, Pallas kernels for 56% -> 56%
where the time goes in v6:
time: 486 us; the launch traced here: 479 us
  Pallas kernels  351 us (72%)
  starting transfers between devices  26.5 us (5%)
  blocking collectives  23.7 us (5%)
  waiting for transfers between devices  17.9 us (4%)
  matrix products  17.2 us (4%)
  between operations  15.9 us (3%)
  local copies, waits for them, and re-layouts  14.4 us (3%)
  other arithmetic  12.5 us (3%)
    pallas_call x1, Pallas kernels, reduce_scatter(): pl.pallas_call(functools.partial(reduce_kernel, tuple(groups), small is n...  77.5 us
    pallas_call x1, Pallas kernels, gather_rows(): pl.pallas_call(functools.partial(gather_kernel, split), out_shape=jax.Sha...  68.8 us
    pallas_call x1, Pallas kernels, attention_backward(): pl.pallas_call(attention_back_kernel, grid=(steps,), out_shape=(token, sl...  61 us
    pallas_call x1, Pallas kernels, feed_both(): pl.pallas_call(feed_kernel, grid=(steps,), out_shape=(jax.ShapeDtypeStruc...  39 us
    pallas_call x1, Pallas kernels, attention_forward(): pl.pallas_call(attention_kernel, grid=(steps,), out_shape=tuple((jax.Shap...  38 us
    pallas_call x1, Pallas kernels, sweeps(): pl.pallas_call(sweep_kernel, out_shape=jax.ShapeDtypeStruct(rows.shape, B...  37.8 us
    all_to_all x1, starting transfers between devices, from_owner_rows(): lax.all_to_all(rows_out.reshape(count, piece, D), AXES, 0, 0, tiled=True)  26.4 us
    pallas_call x1, Pallas kernels, square_slopes(): pl.pallas_call(slope_kernel, grid=(8,), out_shape=jax.ShapeDtypeStruct((8...  24.6 us
  transfers between devices with their start and end apart: 3, of which 1 were waited for; matrix products, arithmetic and copies ran while one was open for 3% of the time, Pallas kernels for 56%

profile of v6, /device:TPU:0, one launch (start us, length us, event | category | flops | bytes accessed | tf_op | source)
XLA Modules:
  0.0 479.4 jit_solution(6946283983740410226)
XLA Ops:
  7.2 1.8 convert_element_type.29
  9.1 0.8 slice.82
  9.9 0.7 slice.81
  10.6 0.7 broadcast_in_dim.6
  12.0 1.1 copy-done.1
  13.1 68.8 %shard_map.212 = bf16[8,4,2,2,48,768]{5,4,3,2,1,0:T(8,128)(2,1)S(1)} custom-call(f32[8,24,768]{2,1,0:T(8,128)S(1)} %copy-done.1), custom_call_target="tpu_custom_call" | custom-call | tf_op jit(solution)/shard_map/pallas_call | solution.py:870
  81.9 3.6 copy-done
  85.4 0.7 pad_maximum_fusion.2.mirrored
  86.1 38.0 %shard_map.213 = (bf16[4,1024,768]{2,1,0:T(8,128)(2,1)}, bf16[1024,768]{1,0:T(8,128)(2,1)}, bf16[1024,768]{1,0:T(8,128)(2,1)}, bf16[1024,768]{1,0:T(8,128)(2,1)}...) custom-call(s32[8]{0:T(128)} %memory_len.1, ...), custom_call_target="tpu_custom_call" | custom-call | flops 14000000000 | bytes 60000000 | tf_op jit(solution)/shard_map/pallas_call | solution.py:194
  124.1 39.0 %shard_map.214 = (bf16[1024,768]{1,0:T(8,128)(2,1)}, f32[1024,768]{1,0:T(8,128)}, bf16[2,1024,768]{2,1,0:T(8,128)(2,1)}, bf16[2,1024,3072]{2,1,0:T(8,128)(2,1)}, f32[3,768]{1,0:T(4,128)}, /*index=5*/f32[3,3072]{1,0:T(4,128)}) custom-call(s32[8]{0:T(128)} %lengths.1, f32[1024,768]{1,0:T(8,128)} %get-tuple-element.40.h2_in, bf16[1024,768]{1,0:T(8,128)(2,1)} %bitcast.33, ...), custom_call_target="tpu_custom_call" | custom-call | flops 20000000000 | bytes 40000000 | tf_op jit(solution)/shard_map/pallas_call | solution.py:308
  163.1 16.3 %convolution_convert_fusion = bf16[2,3072,768]{2,1,0:T(8,128)(2,1)} fusion(bf16[2,1024,3072]{2,1,0:T(8,128)(2,1)} %get-tuple-element.42, bf16[2,1024,768]{2,1,0:T(8,128)(2,1)} %get-tuple-element.43), kind=kOutput, calls=%fused_computation | convolution fusion | flops 9668395008 | bytes 25165824 | tf_op jit(solution)/shard_map/btf,btd->bfd/dot_general | solution.py:1185
  181.5 61.0 %shard_map.215 = (bf16[1024,768]{1,0:T(8,128)(2,1)}, bf16[2048,768]{1,0:T(8,128)(2,1)}, bf16[6,1024,768]{2,1,0:T(8,128)(2,1)}, bf16[2,2048,768]{2,1,0:T(8,128)(2...) custom-call(bf16[1024,768]{1,0:T(8,128)(2,1)} %bitcast.35, f32[1024,768]{1,0:T(8,128)} %get-tuple-element.45.dh2, ...), custom_call_target="tpu_custom_call" | custom-call | flops 16000000000 | bytes 60000000 | tf_op jit(solution)/shard_map/pallas_call | solution.py:440
  242.5 0.8 slice.68
  243.3 0.8 slice_reduce_fusion
  244.1 0.8 slice.66
  245.1 0.8 maximum_bitcast_fusion
  245.8 0.7 concatenate.23
  246.6 24.6 %shard_map.216 = bf16[8,768,768]{2,1,0:T(8,128)(2,1)} custom-call(bf16[4,1024,768]{2,1,0:T(8,128)(2,1)} %get-tuple-element.59.left, bf16[6,1024,768]{2,1,0:T(8,128)(2,1)} %get-tuple-element.60.right, bf16[2048,768]{1,0:T(8,128)(2,1)} %bitcast.32, bf16[2,2048,768]{2,1,0:T(8,128)(2,1)} %get-tuple-element.61.far), custom_call_target="tpu_custom_call" | custom-call | flops 12000000000 | bytes 30000000 | tf_op jit(solution)/shard_map/pallas_call | solution.py:492
  271.2 77.5 %shard_map.217 = (f32[8,24,768]{2,1,0:T(8,128)}, f32[192,128]{1,0:T(8,128)}) custom-call(bf16[8,4,2,2,48,768]{5,4,3,2,1,0:T(8,128)(2,1)} %bitcast.23, f32[192,128]{1,0:T(8,128)} %bitcast.24), custom_call_target="tpu_custom_call" | custom-call | tf_op jit(solution)/shard_map/pallas_call | solution.py:755
  348.7 1.2 slice.83
  350.6 2.0 fusion.2
  352.7 1.9 fusion.3
  354.7 23.7 %all_to_all.10 = bf16[32,12,768]{2,1,0:T(8,128)(2,1)S(1)} all-to-all(bf16[32,12,768]{2,1,0:T(8,128)(2,1)S(1)} %pad_maximum_fusion), channel_id=1, replica_groups=mesh['tall'=4,'square'=4,'row'=2] {'tall','square','row'}, dimensions={0} | all-to-all | bytes 1179648 | tf_op jit(solution)/shard_map/all_to_all | solution.py:1098
  378.5 0.9 convolution_bitcast_fusion
  379.5 4.7 shard_map.218.packed
  384.3 37.8 %shard_map.219 = bf16[384,768]{1,0:T(8,128)(2,1)S(1)} custom-call(f32[1536,256]{1,0:T(8,128)S(1)} %shard_map.218.packed, bf16[384,768]{1,0:T(8,128)(2,1)S(1)} %reshape.113.rows), custom_call_target="tpu_custom_call" | custom-call | flops 40000000000 | bytes 5000000 | tf_op jit(solution)/shard_map/pallas_call | solution.py:1055
  422.2 1.0 reshape.114
  423.2 26.4 %all-to-all-start.1 = ((bf16[32,12,768]{2,1,0:T(8,128)(2,1)}), bf16[32,12,768]{2,1,0:T(8,128)(2,1)S(1)}, u32[]{:S(2)}, u32[]{:S(2)}) async-start(bf16[32,12,768]{2,1,0:T(8,128)(2,1)} %reshape.114), calls=%async_computation.2 | async-start | bytes 1572864 | tf_op jit(solution)/shard_map/all_to_all | solution.py:1111
  450.5 0.7 dynamic-slice_multiply_fusion
  452.5 17.8 %all-to-all-done.1 = bf16[32,12,768]{2,1,0:T(8,128)(2,1)S(1)} async-done(((bf16[32,12,768]{2,1,0:T(8,128)(2,1)}), bf16[32,12,768]{2,1,0:T(8,128)(2,1)S(1)}, u32[]{:S(2)}, u32[]{:S(2)}) %all-to-all-start.1) | async-done | bytes 589856 | tf_op jit(solution)/shard_map/all_to_all | solution.py:1111
  470.5 0.9 multiply_subtract_fusion
  471.5 0.9 multiply_subtract_fusion.1
  (52 shorter events, 5.3 us)
Async XLA Ops:
  7.2 116.9 %all-gather.2.cloned.1.call-start = ((), (), s32[]{:S(2)}) async-start(), calls=%async_computation.3 | async-start | bytes 9732096 | tf_op jit(solution)/shard_map/all_gather | solution.py:1173
  9.1 343.6 %reduce-scatter.2.cloned.1.call-start = ((), (), s32[]{:S(2)}) async-start(), calls=%async_computation.4 | async-start | bytes 9732096 | tf_op jit(solution)/shard_map/reduce_scatter | solution.py:1187
  12.0 1.1 copy-start.1
  81.8 3.6 copy-start
  179.5 0.7 copy-start.9
  179.5 1.9 copy-start.7
  181.5 63.5 %copy-start.8 = (f32[3,768]{1,0:T(4,128)S(1)}, f32[3,768]{1,0:T(4,128)}, u32[]{:S(2)}) copy-start(f32[3,768]{1,0:T(4,128)} %get-tuple-element.64) | copy-start | bytes 27652
  271.2 79.4 %copy-start.4 = (f32[8,24,768]{2,1,0:T(8,128)S(1)}, f32[8,24,768]{2,1,0:T(8,128)}, u32[]{:S(2)}) copy-start(f32[8,24,768]{2,1,0:T(8,128)} %param.20) | copy-start | bytes 1769476
  348.7 4.0 copy-start.5
  422.2 27.5 %copy-start.6 = (f32[192,128]{1,0:T(8,128)S(1)}, f32[192,128]{1,0:T(8,128)}, u32[]{:S(2)}) copy-start(f32[192,128]{1,0:T(8,128)} %get-tuple-element.66) | copy-start | bytes 294916
  423.2 47.0 %all-to-all-start.1 = ((bf16[32,12,768]{2,1,0:T(8,128)(2,1)}), bf16[32,12,768]{2,1,0:T(8,128)(2,1)S(1)}, u32[]{:S(2)}, u32[]{:S(2)}) async-start(bf16[32,12,768]{2,1,0:T(8,128)(2,1)} %reshape.114), calls=%async_computation.2 | async-start | bytes 1572864 | tf_op jit(solution)/shard_map/all_to_all | solution.py:1111
  449.6 20.9 %copy-start.3 = (f32[2,96,768]{2,1,0:T(8,128)S(1)}, f32[2,96,768]{2,1,0:T(8,128)}, u32[]{:S(2)}) copy-start(f32[2,96,768]{2,1,0:T(8,128)} %param.19) | copy-start | bytes 1769476
  470.4 1.1 copy-start.2
Sparse Core Ops, SparseCore 0:
  11.5 98.3 all-gather.1
  179.6 149.3 reduce-scatter.1

commit v7 on v6

--- a/solution.py
+++ b/solution.py
@@ -72,6 +72,14 @@
     return jnp.sum(values, axis=0, keepdims=True)
 
 
+def spread_heads(scales):
+    heads, width = scales.shape[1], scales.shape[1] * LANES // 2
+    row = lax.broadcasted_iota(jnp.int32, (heads, width), 0)
+    column = lax.broadcasted_iota(jnp.int32, (heads, width), 1)
+    own = (column >= row * (LANES // 2)) & (column < (row + 1) * (LANES // 2))
+    return times(scales, jnp.where(own, 1.0, 0.0).astype(BF16))
+
+
 def head_masks():
     lane = lax.broadcasted_iota(jnp.int32, (1, LANES), 1)
     even = jnp.where(lane < LANES // 2, 1.0, 0.0)
@@ -99,9 +107,9 @@
 
 
 def attention_kernel(
-    memory_len, x_in, memory, w, vec_in, hs, mirrored,
+    memory_len, x_in, memory, w, vec_in, scales, relative,
     left, q, k, v, p, o, h1, cq, ck, cv, pc, co, h2,
-    bias, vec,
+    bias, vec, hs,
 ):
     step = pl.program_id(0)
     masks = head_masks()
@@ -111,6 +119,9 @@
         vec[...] = vec_in[...].astype(F32)
         row = lax.broadcasted_iota(jnp.int32, (128, 128), 0)
         column = lax.broadcasted_iota(jnp.int32, (128, 128), 1)
+        turned = jnp.where((row + column == 128) | (row + column == 0), 1.0, 0.0).astype(BF16)
+        mirrored = times(relative[...], turned)
+        hs[...] = spread_heads(scales[...])
         for head in range(12):
             line = jnp.broadcast_to(mirrored[head : head + 1], (128, 128))
             line = pltpu.roll(line, 0, 1, stride=1, stride_axis=0)
@@ -200,7 +211,11 @@
             spec["t"], spec["m"], whole(square.shape), whole(vectors.shape), whole(head_row.shape), whole(bias.shape),
         ],
         out_specs=tuple(spec[kind] for _, kind in shapes),
-        scratch_shapes=[pltpu.VMEM((6, 256, 128), F32), pltpu.VMEM(vectors.shape, F32)],
+        scratch_shapes=[
+            pltpu.VMEM((6, 256, 128), F32),
+            pltpu.VMEM(vectors.shape, F32),
+            pltpu.VMEM((1, width), F32),
+        ],
         compiler_params=pltpu.CompilerParams(vmem_limit_bytes=60 << 20),
         cost_estimate=pl.CostEstimate(flops=14_000_000_000, bytes_accessed=60_000_000, transcendentals=5_000_000),
     )(memory_len, inputs, memory, square, vectors, head_row, bias)
@@ -337,10 +352,10 @@
 
 
 def attention_back_kernel(
-    x_in, dh2, w, vec_in, hs,
+    x_in, dh2, w, vec_in, scales,
     q, k, v, p, o, h1, cq, ck, cv, pc, co,
     dx, dmem, right, far, dvec, drel,
-    do, dh1, dbias, vec,
+    do, dh1, dbias, vec, hs,
 ):
     step = pl.program_id(0)
     masks = head_masks()
@@ -350,6 +365,7 @@
     @pl.when(step == 0)
     def _():
         vec[...] = vec_in[...].astype(F32)
+        hs[...] = spread_heads(scales[...])
         dvec[...] = jnp.zeros_like(dvec)
         dbias[...] = jnp.zeros_like(dbias)
 
@@ -461,6 +477,7 @@
             pltpu.VMEM((TOKENS, width), F32),
             pltpu.VMEM((6, 256, 128), F32),
             pltpu.VMEM(vectors.shape, F32),
+            pltpu.VMEM((1, width), F32),
         ],
         compiler_params=pltpu.CompilerParams(vmem_limit_bytes=60 << 20),
         cost_estimate=pl.CostEstimate(flops=16_000_000_000, bytes_accessed=60_000_000, transcendentals=0),
@@ -528,14 +545,21 @@
     pl.semaphore_wait(barrier, len(partners))
 
 
+def small_tiles(arrays):
+    places, at = [], 0
+    for array in arrays:
+        for tile in range(array.shape[1] // 128):
+            places.append((array, at, tile))
+            at += -(-array.shape[0] // 8) * 8
+    return places
+
+
 def reduce_kernel(groups, has_small, *refs):
     n = len(groups)
     ins, refs = refs[:n], refs[n:]
-    if has_small:
-        small, refs = refs[0], refs[1:]
+    small_in, refs = refs[:has_small], refs[has_small:]
     outs, refs = refs[:n], refs[n:]
-    if has_small:
-        small_out, refs = refs[0], refs[1:]
+    small_outs, refs = refs[:has_small], refs[has_small:]
     z, y, x, core = place()
     other = 1 - core
     sibling = device(z, y, x, other)
@@ -546,7 +570,7 @@
     theirs = other * 384
 
     if has_small:
-        held, total, refs = refs[0], refs[1], refs[2:]
+        small, held, total, refs = refs[0], refs[1], refs[2], refs[3:]
         small_send, small_recv, refs = refs[0], refs[1], refs[2:]
 
         def small_copies(stage):
@@ -567,6 +591,9 @@
                 for k in range(3)
             ]
 
+        small[...] = jnp.zeros_like(small)
+        for source, at, tile in small_tiles(small_in):
+            small[at : at + source.shape[0]] = source[:, tile * 128 : tile * 128 + 128]
         for copy in small_copies(0):
             copy.start()
 
@@ -581,7 +608,9 @@
                 for copy in small_copies(stage + 1):
                     copy.start()
             else:
-                small_out[...] = ((held[3] + held[4]) + held[5]) + held[6]
+                total[3] = ((held[3] + held[4]) + held[5]) + held[6]
+                for target, at, tile in small_tiles(small_outs):
+                    target[:, tile * 128 : tile * 128 + 128] = total[3, at : at + target.shape[0]]
     else:
         def small_step(stage):
             pass
@@ -723,10 +752,13 @@
 def reduce_scatter(arrays, small, collective_id, split=1):
     groups, views, outs, scratch = [], [], [], []
     bf16, f32 = jnp.bfloat16, jnp.float32
-    if small is not None:
+    if small:
+        last = small_tiles(small)[-1]
+        lines = last[1] + -(-last[0].shape[0] // 8) * 8
         scratch += [
-            pltpu.VMEM((7,) + small.shape, f32),
-            pltpu.VMEM((3,) + small.shape, f32),
+            pltpu.VMEM((lines, 128), f32),
+            pltpu.VMEM((7, lines, 128), f32),
+            pltpu.VMEM((4, lines, 128), f32),
             pltpu.SemaphoreType.DMA((6,)),
             pltpu.SemaphoreType.DMA((6,)),
         ]
@@ -748,12 +780,12 @@
             pltpu.SemaphoreType.DMA((7, pieces)),
             pltpu.SemaphoreType.DMA((7, pieces)),
         ]
-    if small is not None:
-        views.append(small)
-        outs.append(jax.ShapeDtypeStruct(small.shape, f32))
+    for array in small:
+        views.append(array)
+        outs.append(jax.ShapeDtypeStruct(array.shape, f32))
     vmem = pl.BlockSpec(memory_space=pltpu.VMEM)
     return pl.pallas_call(
-        functools.partial(reduce_kernel, tuple(groups), small is not None),
+        functools.partial(reduce_kernel, tuple(groups), len(small)),
         out_shape=tuple(outs),
         in_specs=[vmem] * len(views),
         out_specs=tuple([vmem] * len(outs)),
@@ -1172,11 +1204,10 @@
         )
     tall_copy = lax.all_gather(tall_master.astype(jnp.bfloat16), AXES, axis=1, tiled=True)
     width = inputs.shape[2]
-    head_row = jnp.repeat(head_scale.astype(F32), width // head_scale.shape[0])[None]
-    bias = jnp.roll(relative.astype(F32)[:, ::-1], 1, axis=1)
+    head_row = head_scale[None]
     flat_in, flat_memory = inputs.reshape(-1, width), memory.reshape(-1, width)
     left, q, k, v, p, o, h1, cq, ck, cv, pc, co, h2 = attention_forward(
-        flat_in, flat_memory, memory_len, square_copy, vectors, head_row, bias
+        flat_in, flat_memory, memory_len, square_copy, vectors, head_row, relative
     )
     output, dh2, narrow, wide, late_slope, feed_slope = feed_both(
         h2, cotangent.reshape(-1, width), lengths, tall_copy, vectors, feed_vectors
@@ -1189,42 +1220,33 @@
         flat_in, dh2, square_copy, vectors, head_row, (q, k, v, p, o, h1, cq, ck, cv, pc, co)
     )
     square_slope = square_slopes(left, right, flat_memory, far)
-    vector_slope = jnp.concatenate([early_slope[:14], late_slope], axis=0)
-    scale_slope = jnp.sum(early_slope[17].reshape(head_scale.shape[0], -1), axis=1)
-    bias_slope = jnp.roll(bias_slope, 1, axis=1)
     small = [
-        jnp.sum(lengths).astype(jnp.float32).reshape(1),
-        scale_slope.reshape(-1),
-        bias_slope.reshape(-1),
-        vector_slope.reshape(-1),
-        feed_slope.reshape(-1),
+        jnp.full((8, 128), jnp.sum(lengths).astype(F32)),
+        early_slope,
+        late_slope,
+        feed_slope,
+        bias_slope,
     ]
-    sizes = [piece.shape[0] for piece in small]
-    starts = [sum(sizes[:i]) for i in range(len(sizes) + 1)]
     if kernels:
-        lines = -(-starts[-1] // 1024) * 8
-        small.append(jnp.zeros((lines * 128 - starts[-1],), jnp.float32))
-        square_sum, summed = reduce_scatter(
-            [square_slope], jnp.concatenate(small).reshape(lines, 128), 1
-        )
-        summed = summed.reshape(-1)
+        square_sum, *small = reduce_scatter([square_slope], small, 1)
     else:
         square_sum = lax.psum_scatter(
             square_slope, AXES, scatter_dimension=1, tiled=True
         ).astype(jnp.float32)
-        summed = lax.psum(jnp.concatenate(small), AXES)
-    total, scale_sum, bias_sum, vector_sum, feed_sum = (
-        summed[starts[i] : starts[i + 1]] for i in range(len(sizes))
-    )
+        small = lax.psum(small, AXES)
+    total, early_sum, late_sum, feed_sum, bias_sum = small
+    total = total[0, :1]
+    vector_sum = jnp.concatenate([early_sum[:14], late_sum], axis=0)
+    scale_sum = jnp.sum(early_sum[17].reshape(head_scale.shape[0], -1), axis=1)
+    bias_sum = jnp.roll(bias_sum, 1, axis=1)
     factor = inputs.shape[0] * count / total[0]
-    bias_sum = bias_sum.reshape(bias_slope.shape)
-    width = vector_slope.shape[1] // count
+    width = vector_sum.shape[1] // count
     vector_sum = lax.dynamic_slice_in_dim(
-        vector_sum.reshape(vector_slope.shape), index * width, width, axis=1
+        vector_sum, index * width, width, axis=1
     )
     width = feed_slope.shape[1] // count
     feed_sum = lax.dynamic_slice_in_dim(
-        feed_sum.reshape(feed_slope.shape), index * width, width, axis=1
+        feed_sum, index * width, width, axis=1
     )
     square_state = MOMENTUM_DECAY * square_momentum + factor * square_sum
     tall_state = MOMENTUM_DECAY * tall_momentum + factor * tall_sum

time: 486 us -> 491 us (1.010)
  Pallas kernels: 351 us -> 364 us
  local copies, waits for them, and re-layouts: 14.4 us -> 8.87 us
    pallas_call x1, Pallas kernels: 77.5 us -> 89.5 us  [reduce_scatter(): pl.pallas_call(functools.partial(reduce_kernel, tuple(groups), len(small)...]
  transfers between devices with their start and end apart: 3 -> 3, of which waited for: 1 -> 1; matrix products, arithmetic and copies ran while one was open for 3% -> 2% of each run, Pallas kernels for 56% -> 58%
where the time goes in v7:
time: 491 us; the launch traced here: 485 us
  Pallas kernels  364 us (74%)
  starting transfers between devices  26.5 us (5%)
  blocking collectives  23.7 us (5%)
  waiting for transfers between devices  17.2 us (4%)
  matrix products  17.2 us (4%)
  between operations  16.1 us (3%)
  other arithmetic  11.6 us (2%)
  local copies, waits for them, and re-layouts  8.87 us (2%)
    pallas_call x1, Pallas kernels, reduce_scatter(): pl.pallas_call(functools.partial(reduce_kernel, tuple(groups), len(small)...  89.5 us
    pallas_call x1, Pallas kernels, gather_rows(): pl.pallas_call(functools.partial(gather_kernel, split), out_shape=jax.Sha...  69 us
    pallas_call x1, Pallas kernels, attention_backward(): pl.pallas_call(attention_back_kernel, grid=(steps,), out_shape=(token, sl...  61.4 us
    pallas_call x1, Pallas kernels, feed_both(): pl.pallas_call(feed_kernel, grid=(steps,), out_shape=(jax.ShapeDtypeStruc...  39 us
    pallas_call x1, Pallas kernels, attention_forward(): pl.pallas_call(attention_kernel, grid=(steps,), out_shape=tuple((jax.Shap...  38 us
    pallas_call x1, Pallas kernels, sweeps(): pl.pallas_call(sweep_kernel, out_shape=jax.ShapeDtypeStruct(rows.shape, B...  37.8 us
    all_to_all x1, starting transfers between devices, from_owner_rows(): lax.all_to_all(rows_out.reshape(count, piece, D), AXES, 0, 0, tiled=True)  26.4 us
    pallas_call x1, Pallas kernels, square_slopes(): pl.pallas_call(slope_kernel, grid=(8,), out_shape=jax.ShapeDtypeStruct((8...  24.3 us
  transfers between devices with their start and end apart: 3, of which 1 were waited for; matrix products, arithmetic and copies ran while one was open for 2% of the time, Pallas kernels for 58%

profile of v7, /device:TPU:0, one launch (start us, length us, event | category | flops | bytes accessed | tf_op | source)
XLA Modules:
  0.0 484.9 jit_solution(4005721446437023257)
XLA Ops:
  7.2 1.8 convert_element_type.21
  9.1 1.1 copy-done.1
  10.2 69.0 %shard_map.212 = bf16[8,4,2,2,48,768]{5,4,3,2,1,0:T(8,128)(2,1)S(1)} custom-call(f32[8,24,768]{2,1,0:T(8,128)S(1)} %copy-done.1), custom_call_target="tpu_custom_call" | custom-call | tf_op jit(solution)/shard_map/pallas_call | solution.py:902
  79.2 3.6 copy-done
  82.8 38.0 %shard_map.213 = (bf16[4,1024,768]{2,1,0:T(8,128)(2,1)}, bf16[1024,768]{1,0:T(8,128)(2,1)}, bf16[1024,768]{1,0:T(8,128)(2,1)}, bf16[1024,768]{1,0:T(8,128)(2,1)}...) custom-call(s32[8]{0:T(128)} %memory_len.1, ...), custom_call_target="tpu_custom_call" | custom-call | flops 14000000000 | bytes 60000000 | tf_op jit(solution)/shard_map/pallas_call | solution.py:205
  120.9 39.0 %shard_map.214 = (bf16[1024,768]{1,0:T(8,128)(2,1)}, f32[1024,768]{1,0:T(8,128)}, bf16[2,1024,768]{2,1,0:T(8,128)(2,1)}, bf16[2,1024,3072]{2,1,0:T(8,128)(2,1)}, f32[3,768]{1,0:T(4,128)}, /*index=5*/f32[3,3072]{1,0:T(4,128)}) custom-call(s32[8]{0:T(128)} %lengths.1, f32[1024,768]{1,0:T(8,128)} %get-tuple-element.44.h2_in, bf16[1024,768]{1,0:T(8,128)(2,1)} %bitcast.21, ...), custom_call_target="tpu_custom_call" | custom-call | flops 20000000000 | bytes 40000000 | tf_op jit(solution)/shard_map/pallas_call | solution.py:323
  159.9 16.3 %convolution_convert_fusion = bf16[2,3072,768]{2,1,0:T(8,128)(2,1)} fusion(bf16[2,1024,3072]{2,1,0:T(8,128)(2,1)} %get-tuple-element.46, bf16[2,1024,768]{2,1,0:T(8,128)(2,1)} %get-tuple-element.47), kind=kOutput, calls=%fused_computation | convolution fusion | flops 9668395008 | bytes 25165824 | tf_op jit(solution)/shard_map/btf,btd->bfd/dot_general | solution.py:1216
  176.2 0.6 copy-done.9
  176.9 0.6 reduce_sum.18
  178.1 61.4 %shard_map.215 = (bf16[1024,768]{1,0:T(8,128)(2,1)}, bf16[2048,768]{1,0:T(8,128)(2,1)}, bf16[6,1024,768]{2,1,0:T(8,128)(2,1)}, bf16[2,2048,768]{2,1,0:T(8,128)(2...) custom-call(bf16[1024,768]{1,0:T(8,128)(2,1)} %bitcast.23, f32[1024,768]{1,0:T(8,128)} %get-tuple-element.49.dh2, ...), custom_call_target="tpu_custom_call" | custom-call | flops 16000000000 | bytes 60000000 | tf_op jit(solution)/shard_map/pallas_call | solution.py:456
  239.5 24.3 %shard_map.216 = bf16[8,768,768]{2,1,0:T(8,128)(2,1)} custom-call(bf16[4,1024,768]{2,1,0:T(8,128)(2,1)} %get-tuple-element.63.left, bf16[6,1024,768]{2,1,0:T(8,128)(2,1)} %get-tuple-element.64.right, bf16[2048,768]{1,0:T(8,128)(2,1)} %bitcast.20, bf16[2,2048,768]{2,1,0:T(8,128)(2,1)} %get-tuple-element.65.far), custom_call_target="tpu_custom_call" | custom-call | flops 12000000000 | bytes 30000000 | tf_op jit(solution)/shard_map/pallas_call | solution.py:509
  263.8 0.6 broadcast_in_dim.7.refs_1_
  264.4 89.5 %shard_map.217 = (f32[8,24,768]{2,1,0:T(8,128)}, f32[8,128]{1,0:T(8,128)}, f32[18,768]{1,0:T(8,128)}, f32[3,768]{1,0:T(4,128)}, f32[3,3072]{1,0:T(4,128)}, /*index=5*/f32[12,128]{1,0:T(8,128)}) custom-call(bf16[8,4,2,2,48,768]{5,4,3,2,1,0:T(8,128)(2,1)} %bitcast.17, f32[8,128]{1,0:T(8,128)} %broadcast_in_dim.7.refs_1_, f32[18,768]{1,0:T(8,128)} %get-tuple-element.66.refs_2_, ...), custom_call_target="tpu_custom_call" | custom-call | tf_op jit(solution)/shard_map/pallas_call | solution.py:787
  354.0 1.3 slice.40
  355.9 2.0 fusion.3
  358.0 1.9 fusion.4
  360.1 23.7 %all_to_all.10 = bf16[32,12,768]{2,1,0:T(8,128)(2,1)S(1)} all-to-all(bf16[32,12,768]{2,1,0:T(8,128)(2,1)S(1)} %pad_maximum_fusion), channel_id=1, replica_groups=mesh['tall'=4,'square'=4,'row'=2] {'tall','square','row'}, dimensions={0} | all-to-all | bytes 1179648 | tf_op jit(solution)/shard_map/all_to_all | solution.py:1130
  383.7 0.9 convolution_bitcast_fusion
  384.7 4.7 shard_map.218.packed
  389.4 0.1 reshape.80.rows
  389.6 37.8 %shard_map.219 = bf16[384,768]{1,0:T(8,128)(2,1)S(1)} custom-call(f32[1536,256]{1,0:T(8,128)S(1)} %shard_map.218.packed, bf16[384,768]{1,0:T(8,128)(2,1)S(1)} %reshape.80.rows), custom_call_target="tpu_custom_call" | custom-call | flops 40000000000 | bytes 5000000 | tf_op jit(solution)/shard_map/pallas_call | solution.py:1087
  427.5 1.0 reshape.81
  428.5 26.4 %all-to-all-start.1 = ((bf16[32,12,768]{2,1,0:T(8,128)(2,1)}), bf16[32,12,768]{2,1,0:T(8,128)(2,1)S(1)}, u32[]{:S(2)}, u32[]{:S(2)}) async-start(bf16[32,12,768]{2,1,0:T(8,128)(2,1)} %reshape.81), calls=%async_computation.2 | async-start | bytes 1572864 | tf_op jit(solution)/shard_map/all_to_all | solution.py:1143
  455.1 0.1 reduce_sum.19
  455.2 1.3 dynamic-slice_multiply_fusion
  456.5 0.7 maximum_multiply_fusion
  457.2 0.7 fusion.2
  457.9 0.5 broadcast_multiply_fusion
  458.4 17.1 %all-to-all-done.1 = bf16[32,12,768]{2,1,0:T(8,128)(2,1)S(1)} async-done(((bf16[32,12,768]{2,1,0:T(8,128)(2,1)}), bf16[32,12,768]{2,1,0:T(8,128)(2,1)S(1)}, u32[]{:S(2)}, u32[]{:S(2)}) %all-to-all-start.1) | async-done | bytes 589856 | tf_op jit(solution)/shard_map/all_to_all | solution.py:1143
  475.5 0.2 convert_multiply_fusion
  475.8 0.9 multiply_subtract_fusion
  476.8 0.9 multiply_subtract_fusion.1
  (37 shorter events, 0.9 us)
Async XLA Ops:
  7.2 113.7 %all-gather.2.cloned.1.call-start = ((), (), s32[]{:S(2)}) async-start(), calls=%async_computation.3 | async-start | bytes 9732096 | tf_op jit(solution)/shard_map/all_gather | solution.py:1205
  9.1 348.9 %reduce-scatter.2.cloned.1.call-start = ((), (), s32[]{:S(2)}) async-start(), calls=%async_computation.4 | async-start | bytes 9732096 | tf_op jit(solution)/shard_map/reduce_scatter | solution.py:1218
  9.1 1.1 copy-start.1
  79.2 3.6 copy-start
  176.2 0.7 copy-start.9
  264.4 91.5 %copy-start.4 = (f32[8,24,768]{2,1,0:T(8,128)S(1)}, f32[8,24,768]{2,1,0:T(8,128)}, u32[]{:S(2)}) copy-start(f32[8,24,768]{2,1,0:T(8,128)} %param.20) | copy-start | bytes 1769476
  354.0 4.0 copy-start.5
  427.4 27.5 %copy-start.7 = (f32[12,128]{1,0:T(8,128)S(1)}, f32[12,128]{1,0:T(8,128)}, u32[]{:S(2)}) copy-start(f32[12,128]{1,0:T(8,128)} %get-tuple-element.76) | copy-start | bytes 18436
  427.4 27.6 %copy-start.6 = (f32[18,768]{1,0:T(8,128)S(1)}, f32[18,768]{1,0:T(8,128)}, u32[]{:S(2)}) copy-start(f32[18,768]{1,0:T(8,128)} %get-tuple-element.73) | copy-start | bytes 165892
  427.4 29.8 %copy-start.8 = (f32[3,768]{1,0:T(4,128)S(1)}, f32[3,768]{1,0:T(4,128)}, u32[]{:S(2)}) copy-start(f32[3,768]{1,0:T(4,128)} %get-tuple-element.74) | copy-start | bytes 27652
  428.5 47.0 %all-to-all-start.1 = ((bf16[32,12,768]{2,1,0:T(8,128)(2,1)}), bf16[32,12,768]{2,1,0:T(8,128)(2,1)S(1)}, u32[]{:S(2)}, u32[]{:S(2)}) async-start(bf16[32,12,768]{2,1,0:T(8,128)(2,1)} %reshape.81), calls=%async_computation.2 | async-start | bytes 1572864 | tf_op jit(solution)/shard_map/all_to_all | solution.py:1143
  454.9 20.9 %copy-start.3 = (f32[2,96,768]{2,1,0:T(8,128)S(1)}, f32[2,96,768]{2,1,0:T(8,128)}, u32[]{:S(2)}) copy-start(f32[2,96,768]{2,1,0:T(8,128)} %param.19) | copy-start | bytes 1769476
  475.7 1.1 copy-start.2
Sparse Core Ops, SparseCore 0:
  11.5 96.1 all-gather.1
  176.4 151.6 reduce-scatter.1

commit v8 on v7

--- a/solution.py
+++ b/solution.py
@@ -550,7 +550,7 @@
     for array in arrays:
         for tile in range(array.shape[1] // 128):
             places.append((array, at, tile))
-            at += -(-array.shape[0] // 8) * 8
+            at += array.shape[0]
     return places
 
 
@@ -573,23 +573,26 @@
         small, held, total, refs = refs[0], refs[1], refs[2], refs[3:]
         small_send, small_recv, refs = refs[0], refs[1], refs[2:]
 
+        side = small.shape[0] // 2
+        own_rows = pl.ds(pl.multiple_of(core * side, 8), side)
+
         def small_copies(stage):
-            source = small if stage == 0 else total.at[stage - 1]
+            def make(source, target, slot, partner):
+                return pltpu.make_async_remote_copy(
+                    source, target, small_send.at[slot], small_recv.at[slot],
+                    device_id=partner, device_id_type=MESH,
+                )
+
+            if stage == 0:
+                return [make(small, held.at[0], 0, sibling)]
             if stage < 3:
-                partner = (sibling, across["x"], across["y"])[stage]
-                return [
-                    pltpu.make_async_remote_copy(
-                        source, held.at[stage], small_send.at[stage], small_recv.at[stage],
-                        device_id=partner, device_id_type=MESH,
-                    )
-                ]
-            return [
-                pltpu.make_async_remote_copy(
-                    source, held.at[3 + z], small_send.at[3 + k], small_recv.at[3 + k],
-                    device_id=along[k], device_id_type=MESH,
-                )
-                for k in range(3)
-            ]
+                source = total.at[stage - 1, own_rows]
+                partner = across["x"] if stage == 1 else across["y"]
+                return [make(source, held.at[stage, own_rows], stage, partner)]
+            if stage == 3:
+                source = total.at[2, own_rows]
+                return [make(source, held.at[3 + z, own_rows], 3 + k, along[k]) for k in range(3)]
+            return [make(total.at[3, own_rows], held.at[7, own_rows], 6, sibling)]
 
         small[...] = jnp.zeros_like(small)
         for source, at, tile in small_tiles(small_in):
@@ -598,19 +601,32 @@
             copy.start()
 
         def small_step(stage):
-            for copy in small_copies(stage):
-                copy.wait_recv()
-            if stage < 3:
-                own = small if stage == 0 else total.at[stage - 1]
-                total[stage] = own[...] + held[stage]
+            if stage < 4:
+                for copy in small_copies(stage):
+                    copy.wait_recv()
+            if stage == 0:
+                total[0] = small[...] + held[0]
+            elif stage < 3:
+                total[stage, own_rows] = total[stage - 1, own_rows] + held[stage, own_rows]
                 if stage == 2:
-                    held[3 + z] = total[2]
+                    held[3 + z, own_rows] = total[2, own_rows]
+            elif stage == 3:
+                total[3, own_rows] = (
+                    (held[3, own_rows] + held[4, own_rows]) + held[5, own_rows]
+                ) + held[6, own_rows]
+            else:
+                rest = pl.ds(pl.multiple_of(other * side, 8), side)
+                pltpu.make_async_remote_copy(
+                    total.at[3, rest], held.at[7, rest], small_send.at[6], small_recv.at[6],
+                    device_id=sibling, device_id_type=MESH,
+                ).wait_recv()
+                held[7, own_rows] = total[3, own_rows]
+                for target, at, tile in small_tiles(small_outs):
+                    target[:, tile * 128 : tile * 128 + 128] = held[7, at : at + target.shape[0]]
+            if stage < 4:
                 for copy in small_copies(stage + 1):
                     copy.start()
-            else:
-                total[3] = ((held[3] + held[4]) + held[5]) + held[6]
-                for target, at, tile in small_tiles(small_outs):
-                    target[:, tile * 128 : tile * 128 + 128] = total[3, at : at + target.shape[0]]
+
     else:
         def small_step(stage):
             pass
@@ -735,7 +751,7 @@
                         step(plan, stage, order, turn - stage)
 
             if plan is plans[0]:
-                for stage in range(4):
+                for stage in range(5):
                     @pl.when(turn == stage)
                     def _():
                         small_step(stage)
@@ -744,7 +760,7 @@
         for plan in plans:
             finish(plan, stage)
     if has_small:
-        for stage in range(4):
+        for stage in range(5):
             for copy in small_copies(stage):
                 copy.wait_send()
 
@@ -754,13 +770,13 @@
     bf16, f32 = jnp.bfloat16, jnp.float32
     if small:
         last = small_tiles(small)[-1]
-        lines = last[1] + -(-last[0].shape[0] // 8) * 8
+        lines = -(-(last[1] + last[0].shape[0]) // 16) * 16
         scratch += [
             pltpu.VMEM((lines, 128), f32),
-            pltpu.VMEM((7, lines, 128), f32),
+            pltpu.VMEM((8, lines, 128), f32),
             pltpu.VMEM((4, lines, 128), f32),
-            pltpu.SemaphoreType.DMA((6,)),
-            pltpu.SemaphoreType.DMA((6,)),
+            pltpu.SemaphoreType.DMA((7,)),
+            pltpu.SemaphoreType.DMA((7,)),
         ]
     for array in arrays:
         matrices, height, width_all = array.shape
@@ -1221,7 +1237,7 @@
     )
     square_slope = square_slopes(left, right, flat_memory, far)
     small = [
-        jnp.full((8, 128), jnp.sum(lengths).astype(F32)),
+        jnp.full((1, 128), jnp.sum(lengths).astype(F32)),
         early_slope,
         late_slope,
         feed_slope,

time: 491 us -> 477 us (0.971)
  Pallas kernels: 364 us -> 351 us
    pallas_call x1, Pallas kernels: 89.5 us -> 76.6 us  [reduce_scatter(): pl.pallas_call(functools.partial(reduce_kernel, tuple(groups), len(small)...]
  transfers between devices with their start and end apart: 3 -> 3, of which waited for: 1 -> 1; matrix products, arithmetic and copies ran while one was open for 2% -> 1% of each run, Pallas kernels for 58% -> 57%
where the time goes in v8:
time: 477 us; the launch traced here: 471 us
  Pallas kernels  351 us (74%)
  starting transfers between devices  26.5 us (6%)
  blocking collectives  23.8 us (5%)
  waiting for transfers between devices  17.2 us (4%)
  matrix products  17.2 us (4%)
  between operations  16.1 us (3%)
  other arithmetic  11.6 us (2%)
  local copies, waits for them, and re-layouts  7.53 us (2%)
    pallas_call x1, Pallas kernels, reduce_scatter(): pl.pallas_call(functools.partial(reduce_kernel, tuple(groups), len(small)...  76.6 us
    pallas_call x1, Pallas kernels, gather_rows(): pl.pallas_call(functools.partial(gather_kernel, split), out_shape=jax.Sha...  69 us
    pallas_call x1, Pallas kernels, attention_backward(): pl.pallas_call(attention_back_kernel, grid=(steps,), out_shape=(token, sl...  61.4 us
    pallas_call x1, Pallas kernels, feed_both(): pl.pallas_call(feed_kernel, grid=(steps,), out_shape=(jax.ShapeDtypeStruc...  39 us
    pallas_call x1, Pallas kernels, attention_forward(): pl.pallas_call(attention_kernel, grid=(steps,), out_shape=tuple((jax.Shap...  38 us
    pallas_call x1, Pallas kernels, sweeps(): pl.pallas_call(sweep_kernel, out_shape=jax.ShapeDtypeStruct(rows.shape, B...  37.8 us
    all_to_all x1, starting transfers between devices, from_owner_rows(): lax.all_to_all(rows_out.reshape(count, piece, D), AXES, 0, 0, tiled=True)  26.4 us
    pallas_call x1, Pallas kernels, square_slopes(): pl.pallas_call(slope_kernel, grid=(8,), out_shape=jax.ShapeDtypeStruct((8...  24.3 us
  transfers between devices with their start and end apart: 3, of which 1 were waited for; matrix products, arithmetic and copies ran while one was open for 1% of the time, Pallas kernels for 57%

profile of v8, /device:TPU:0, one launch (start us, length us, event | category | flops | bytes accessed | tf_op | source)
XLA Modules:
  0.0 470.7 jit_solution(3820418588723581488)
XLA Ops:
  7.2 1.8 convert_element_type.21
  9.1 1.1 copy-done.1
  10.2 69.0 %shard_map.212 = bf16[8,4,2,2,48,768]{5,4,3,2,1,0:T(8,128)(2,1)S(1)} custom-call(f32[8,24,768]{2,1,0:T(8,128)S(1)} %copy-done.1), custom_call_target="tpu_custom_call" | custom-call | tf_op jit(solution)/shard_map/pallas_call | solution.py:918
  79.2 3.6 copy-done
  82.8 38.0 %shard_map.213 = (bf16[4,1024,768]{2,1,0:T(8,128)(2,1)}, bf16[1024,768]{1,0:T(8,128)(2,1)}, bf16[1024,768]{1,0:T(8,128)(2,1)}, bf16[1024,768]{1,0:T(8,128)(2,1)}...) custom-call(s32[8]{0:T(128)} %memory_len.1, ...), custom_call_target="tpu_custom_call" | custom-call | flops 14000000000 | bytes 60000000 | tf_op jit(solution)/shard_map/pallas_call | solution.py:205
  120.9 39.0 %shard_map.214 = (bf16[1024,768]{1,0:T(8,128)(2,1)}, f32[1024,768]{1,0:T(8,128)}, bf16[2,1024,768]{2,1,0:T(8,128)(2,1)}, bf16[2,1024,3072]{2,1,0:T(8,128)(2,1)}, f32[3,768]{1,0:T(4,128)}, /*index=5*/f32[3,3072]{1,0:T(4,128)}) custom-call(s32[8]{0:T(128)} %lengths.1, f32[1024,768]{1,0:T(8,128)} %get-tuple-element.44.h2_in, bf16[1024,768]{1,0:T(8,128)(2,1)} %bitcast.22, ...), custom_call_target="tpu_custom_call" | custom-call | flops 20000000000 | bytes 40000000 | tf_op jit(solution)/shard_map/pallas_call | solution.py:323
  159.9 16.3 %convolution_convert_fusion = bf16[2,3072,768]{2,1,0:T(8,128)(2,1)} fusion(bf16[2,1024,3072]{2,1,0:T(8,128)(2,1)} %get-tuple-element.46, bf16[2,1024,768]{2,1,0:T(8,128)(2,1)} %get-tuple-element.47), kind=kOutput, calls=%fused_computation | convolution fusion | flops 9668395008 | bytes 25165824 | tf_op jit(solution)/shard_map/btf,btd->bfd/dot_general | solution.py:1232
  176.2 0.6 copy-done.9
  176.9 0.6 reduce_sum.18
  178.1 61.4 %shard_map.215 = (bf16[1024,768]{1,0:T(8,128)(2,1)}, bf16[2048,768]{1,0:T(8,128)(2,1)}, bf16[6,1024,768]{2,1,0:T(8,128)(2,1)}, bf16[2,2048,768]{2,1,0:T(8,128)(2...) custom-call(bf16[1024,768]{1,0:T(8,128)(2,1)} %bitcast.24, f32[1024,768]{1,0:T(8,128)} %get-tuple-element.49.dh2, ...), custom_call_target="tpu_custom_call" | custom-call | flops 16000000000 | bytes 60000000 | tf_op jit(solution)/shard_map/pallas_call | solution.py:456
  239.5 24.3 %shard_map.216 = bf16[8,768,768]{2,1,0:T(8,128)(2,1)} custom-call(bf16[4,1024,768]{2,1,0:T(8,128)(2,1)} %get-tuple-element.63.left, bf16[6,1024,768]{2,1,0:T(8,128)(2,1)} %get-tuple-element.64.right, bf16[2048,768]{1,0:T(8,128)(2,1)} %bitcast.21, bf16[2,2048,768]{2,1,0:T(8,128)(2,1)} %get-tuple-element.65.far), custom_call_target="tpu_custom_call" | custom-call | flops 12000000000 | bytes 30000000 | tf_op jit(solution)/shard_map/pallas_call | solution.py:509
  263.8 0.5 broadcast_in_dim.7.refs_1_
  264.3 76.6 %shard_map.217 = (f32[8,24,768]{2,1,0:T(8,128)}, f32[1,128]{1,0:T(1,128)}, f32[18,768]{1,0:T(8,128)}, f32[3,768]{1,0:T(4,128)}, f32[3,3072]{1,0:T(4,128)}, /*index=5*/f32[12,128]{1,0:T(8,128)}) custom-call(bf16[8,4,2,2,48,768]{5,4,3,2,1,0:T(8,128)(2,1)} %bitcast.18, f32[1,128]{1,0:T(1,128)} %broadcast_in_dim.7.refs_1_, f32[18,768]{1,0:T(8,128)} %get-tuple-element.66.refs_2_, ...), custom_call_target="tpu_custom_call" | custom-call | tf_op jit(solution)/shard_map/pallas_call | solution.py:803
  341.6 2.0 fusion.3
  343.7 1.9 fusion.4
  345.6 0.1 pad_maximum_fusion
  345.7 23.8 %all_to_all.10 = bf16[32,12,768]{2,1,0:T(8,128)(2,1)S(1)} all-to-all(bf16[32,12,768]{2,1,0:T(8,128)(2,1)S(1)} %pad_maximum_fusion), channel_id=1, replica_groups=mesh['tall'=4,'square'=4,'row'=2] {'tall','square','row'}, dimensions={0} | all-to-all | bytes 1179648 | tf_op jit(solution)/shard_map/all_to_all | solution.py:1146
  369.5 0.9 convolution_bitcast_fusion
  370.5 4.7 shard_map.218.packed
  375.2 0.1 reshape.80.rows
  375.4 37.8 %shard_map.219 = bf16[384,768]{1,0:T(8,128)(2,1)S(1)} custom-call(f32[1536,256]{1,0:T(8,128)S(1)} %shard_map.218.packed, bf16[384,768]{1,0:T(8,128)(2,1)S(1)} %reshape.80.rows), custom_call_target="tpu_custom_call" | custom-call | flops 40000000000 | bytes 5000000 | tf_op jit(solution)/shard_map/pallas_call | solution.py:1103
  413.2 1.0 reshape.81
  414.3 26.4 %all-to-all-start.1 = ((bf16[32,12,768]{2,1,0:T(8,128)(2,1)}), bf16[32,12,768]{2,1,0:T(8,128)(2,1)S(1)}, u32[]{:S(2)}, u32[]{:S(2)}) async-start(bf16[32,12,768]{2,1,0:T(8,128)(2,1)} %reshape.81), calls=%async_computation.2 | async-start | bytes 1572864 | tf_op jit(solution)/shard_map/all_to_all | solution.py:1159
  440.9 0.1 reduce_sum.19
  441.0 1.3 dynamic-slice_multiply_fusion
  442.3 0.7 maximum_multiply_fusion
  443.0 0.7 fusion.2
  443.7 0.5 broadcast_multiply_fusion
  444.2 17.1 %all-to-all-done.1 = bf16[32,12,768]{2,1,0:T(8,128)(2,1)S(1)} async-done(((bf16[32,12,768]{2,1,0:T(8,128)(2,1)}), bf16[32,12,768]{2,1,0:T(8,128)(2,1)S(1)}, u32[]{:S(2)}, u32[]{:S(2)}) %all-to-all-start.1) | async-done | bytes 589856 | tf_op jit(solution)/shard_map/all_to_all | solution.py:1159
  461.3 0.2 convert_multiply_fusion
  461.6 0.9 multiply_subtract_fusion
  462.6 0.9 multiply_subtract_fusion.1
  (36 shorter events, 0.8 us)
Async XLA Ops:
  7.2 113.7 %all-gather.2.cloned.1.call-start = ((), (), s32[]{:S(2)}) async-start(), calls=%async_computation.3 | async-start | bytes 9732096 | tf_op jit(solution)/shard_map/all_gather | solution.py:1221
  9.1 334.6 %reduce-scatter.2.cloned.1.call-start = ((), (), s32[]{:S(2)}) async-start(), calls=%async_computation.4 | async-start | bytes 9732096 | tf_op jit(solution)/shard_map/reduce_scatter | solution.py:1234
  9.1 1.1 copy-start.1
  79.2 3.6 copy-start
  176.2 0.7 copy-start.9
  264.3 77.3 %copy-start.4 = (f32[8,24,768]{2,1,0:T(8,128)S(1)}, f32[8,24,768]{2,1,0:T(8,128)}, u32[]{:S(2)}) copy-start(f32[8,24,768]{2,1,0:T(8,128)} %param.20) | copy-start | bytes 1769476
  340.9 2.7 copy-start.5
  413.2 27.5 %copy-start.7 = (f32[12,128]{1,0:T(8,128)S(1)}, f32[12,128]{1,0:T(8,128)}, u32[]{:S(2)}) copy-start(f32[12,128]{1,0:T(8,128)} %get-tuple-element.76) | copy-start | bytes 18436
  413.2 27.6 %copy-start.6 = (f32[18,768]{1,0:T(8,128)S(1)}, f32[18,768]{1,0:T(8,128)}, u32[]{:S(2)}) copy-start(f32[18,768]{1,0:T(8,128)} %get-tuple-element.73) | copy-start | bytes 165892
  413.2 29.8 %copy-start.8 = (f32[3,768]{1,0:T(4,128)S(1)}, f32[3,768]{1,0:T(4,128)}, u32[]{:S(2)}) copy-start(f32[3,768]{1,0:T(4,128)} %get-tuple-element.74) | copy-start | bytes 27652
  414.3 47.0 %all-to-all-start.1 = ((bf16[32,12,768]{2,1,0:T(8,128)(2,1)}), bf16[32,12,768]{2,1,0:T(8,128)(2,1)S(1)}, u32[]{:S(2)}, u32[]{:S(2)}) async-start(bf16[32,12,768]{2,1,0:T(8,128)(2,1)} %reshape.81), calls=%async_computation.2 | async-start | bytes 1572864 | tf_op jit(solution)/shard_map/all_to_all | solution.py:1159
  440.7 20.9 %copy-start.3 = (f32[2,96,768]{2,1,0:T(8,128)S(1)}, f32[2,96,768]{2,1,0:T(8,128)}, u32[]{:S(2)}) copy-start(f32[2,96,768]{2,1,0:T(8,128)} %param.19) | copy-start | bytes 1769476
  461.5 1.1 copy-start.2
Sparse Core Ops, SparseCore 0:
  11.5 96.1 all-gather.1
  176.4 148.0 reduce-scatter.1
